TPU v7x, 256 devices: a whole 4x4x8 slice. The times are simulated.
256 devices in a mesh: shot: 32 (over x_hi, z, core), depth: 8 (over x_lo, y).
Axes of the slice: x: 4 (x_hi: 2, x_lo: 2; x = x_hi * 2 + x_lo), y: 4, z: 8, core: 2. Of those that a mesh axis runs over, the one named last changes fastest.
Arguments:
- u_prev: float32 [32, 64, 128, 128], P('shot', None, 'depth'), may hold values from -8 to 8.5
- u_cur: float32 [32, 64, 128, 128], P('shot', None, 'depth'), may hold values from -8 to 8.5
- a_prev: float32 [32, 64, 128, 128], P('shot', None, 'depth'), may hold values from -8 to 8.5
- a_cur: float32 [32, 64, 128, 128], P('shot', None, 'depth'), may hold values from -8 to 8.5
- model: float32 [64, 128, 128], P('shot', 'depth'), may hold values from 0.03 to 0.09
- aniso_h: float32 [64, 128, 128], P('shot', 'depth'), may hold values from 0.7 to 1.5
- aniso_c: float32 [64, 128, 128], P('shot', 'depth'), may hold values from -0.5 to 0.5
- smooth_coef: float32 [64, 128, 128], P('shot', 'depth'), may hold values from 0.02 to 0.16
- bin_onehot: int32 [16, 16, 4], P(None, 'depth'), may hold values from 0 to 1, as said below
- shot_group: int32 [32], P('shot'), may hold values from 0 to 15
- src_cell: int32 [32], P('shot'), may hold values from 0 to 1048575
- rec_cell: int32 [32, 128], P('shot'), may hold values from 0 to 1048575
- src_wave: float32 [32, 3], P('shot'), may hold values from -6 to 6
- rec_data: float32 [32, 2, 128], P('shot'), may hold values from -6 to 6
Outputs:
- model_next: float32 [64, 128, 128], P('shot', 'depth')
- grad_dir: float32 [64, 128, 128], P('shot', 'depth')
- wave_next: float32 [32, 64, 128, 128], P('shot', None, 'depth')
Inputs may be any that keep to these rules, and one draw needn't show every extreme that they name: `bin_onehot`: each entry along the last dimension is one-hot: exactly one 1 per row.
All inputs are finite; a program needn't handle non-finite values.
Results may differ from a plain program's by a relative error of at most 0.000092.
Values sent between devices are 32-bit elements; how exact they have to be, the bound alone decides.
No kernel may reach another device: no remote copies, remote signals or barrier semaphores. Data moves between devices by JAX's collectives and lax.ppermute only.
A program may use at most 64 MiB of HBM per device.

v0:
```python
import jax
import jax.numpy as jnp
from jax import lax
from jax.sharding import PartitionSpec as P

second_coef = (-205.0 / 72.0, 8.0 / 5.0, -1.0 / 5.0, 8.0 / 315.0, -1.0 / 560.0)
first_coef = (0.8, -0.2, 4.0 / 105.0, -1.0 / 280.0)


def extended(block, sides, width):
    for axis, dim in sides:
        count = lax.axis_size(axis)
        forward = [(i, i + 1) for i in range(count - 1)]
        backward = [(target, source) for source, target in forward]
        low = lax.ppermute(
            lax.slice_in_dim(block, block.shape[dim] - width, None, axis=dim), axis, forward
        )
        high = lax.ppermute(lax.slice_in_dim(block, 0, width, axis=dim), axis, backward)
        block = jnp.concatenate([low, block, high], axis=dim)
    return block


def pad_axis(field, axis, width):
    widths = [(0, 0)] * field.ndim
    widths[axis] = (width, width)
    return jnp.pad(field, widths)


def shifted(padded, axis, offset, count):
    return lax.slice_in_dim(padded, 4 + offset, 4 + offset + count, axis=axis)


def second_along(padded, axis, count):
    result = second_coef[0] * shifted(padded, axis, 0, count)
    for offset in range(1, 5):
        result = result + second_coef[offset] * (
            shifted(padded, axis, offset, count) + shifted(padded, axis, -offset, count)
        )
    return result


def first_along(padded, axis, count):
    result = first_coef[0] * (shifted(padded, axis, 1, count) - shifted(padded, axis, -1, count))
    for offset in range(2, 5):
        result = result + first_coef[offset - 1] * (
            shifted(padded, axis, offset, count) - shifted(padded, axis, -offset, count)
        )
    return result


def apply_operator(padded_z, aniso_h, aniso_c):
    ndim = padded_z.ndim
    axis_x, axis_z, axis_y = (ndim - 3, ndim - 2, ndim - 1)
    count_z = padded_z.shape[axis_z] - 8
    count_x = padded_z.shape[axis_x]
    count_y = padded_z.shape[axis_y]
    centre = lax.slice_in_dim(padded_z, 4, 4 + count_z, axis=axis_z)
    depth_two = second_along(padded_z, axis_z, count_z)
    depth_one = first_along(padded_z, axis_z, count_z)
    lateral = second_along(pad_axis(centre, axis_x, 4), axis_x, count_x) + second_along(
        pad_axis(centre, axis_y, 4), axis_y, count_y
    )
    crossing = first_along(pad_axis(depth_one, axis_x, 4), axis_x, count_x)
    return aniso_h * lateral + depth_two + aniso_c * crossing


def relax_once(padded, centre, coef):
    neighbours = padded[2:, 1:-1, 1:-1] + padded[:-2, 1:-1, 1:-1]
    neighbours = neighbours + padded[1:-1, 2:, 1:-1] + padded[1:-1, :-2, 1:-1]
    neighbours = neighbours + padded[1:-1, 1:-1, 2:] + padded[1:-1, 1:-1, :-2]
    return centre + coef * (neighbours - 6.0 * centre)


def body(
    u_prev,
    u_cur,
    a_prev,
    a_cur,
    model,
    aniso_h,
    aniso_c,
    smooth_coef,
    bin_onehot,
    shot_group,
    src_cell,
    rec_cell,
    src_wave,
    rec_data,
):
    shot_count, cells_x, cells_z, cells_y = u_cur.shape
    depth_cells = cells_z * lax.axis_size("depth")
    z_start = lax.axis_index("depth") * cells_z
    model_slab, aniso_hs, aniso_cs, coef_slab = (
        lax.all_gather(model, "shot", axis=0, tiled=True),
        lax.all_gather(aniso_h, "shot", axis=0, tiled=True),
        lax.all_gather(aniso_c, "shot", axis=0, tiled=True),
        lax.all_gather(smooth_coef, "shot", axis=0, tiled=True),
    )
    x_pos = lax.broadcasted_iota(jnp.int32, (cells_x, cells_z, cells_y), 0)
    z_pos = lax.broadcasted_iota(jnp.int32, (cells_x, cells_z, cells_y), 1) + z_start
    y_pos = lax.broadcasted_iota(jnp.int32, (cells_x, cells_z, cells_y), 2)
    source_x = src_cell // (depth_cells * cells_y)
    source_z = src_cell // cells_y % depth_cells
    source_y = src_cell % cells_y
    receiver_x = rec_cell // (depth_cells * cells_y)
    receiver_z = rec_cell // cells_y % depth_cells
    receiver_y = rec_cell % cells_y
    receivers = rec_cell.shape[1]

    def source_term(step_index):
        hits = (
            (x_pos == source_x[:, None, None, None])
            & (z_pos == source_z[:, None, None, None])
            & (y_pos == source_y[:, None, None, None])
        )
        return jnp.where(hits, src_wave[:, step_index][:, None, None, None], 0.0)

    wave_pair = jnp.stack([u_cur, a_cur])
    old_pair = jnp.stack([u_prev, a_prev])
    gradient = jnp.zeros_like(u_cur)
    for step_index in range(rec_data.shape[1]):
        padded = extended(wave_pair, (("depth", 3),), 4)
        applied = apply_operator(padded, aniso_hs, aniso_cs)
        gradient = gradient + wave_pair[1] * applied[0]
        records = rec_data[:, step_index]
        along_x = (receiver_x[..., None] == jnp.arange(cells_x, dtype=jnp.int32)).astype(
            jnp.float32
        ) * records[..., None]
        along_z = (receiver_z[..., None] == z_start + jnp.arange(cells_z, dtype=jnp.int32)).astype(
            jnp.float32
        )
        along_y = (receiver_y[..., None] == jnp.arange(cells_y, dtype=jnp.int32)).astype(
            jnp.float32
        )
        plane = (along_x[..., :, None] * along_z[..., None, :]).reshape(
            shot_count, receivers, cells_x * cells_z
        )
        placed = jnp.einsum("srk,sry->sky", plane, along_y, precision=lax.Precision.HIGHEST)
        forcing = jnp.stack(
            [source_term(step_index), placed.reshape(shot_count, cells_x, cells_z, cells_y)]
        )
        next_pair = 2.0 * wave_pair - old_pair + model_slab * applied + forcing
        old_pair, wave_pair = (wave_pair, next_pair)
    nbins = bin_onehot.shape[2]
    groups = bin_onehot.shape[0]
    powers = jnp.exp2(-jnp.arange(nbins, dtype=jnp.float32))
    block_weight = jnp.sum(bin_onehot.astype(jnp.float32) * powers, axis=2)
    chosen = (shot_group[:, None] == jnp.arange(groups, dtype=jnp.int32)).astype(jnp.float32)
    shot_weight = jnp.dot(chosen, block_weight, precision=lax.Precision.HIGHEST)
    depth_weight = jnp.repeat(shot_weight, cells_z // bin_onehot.shape[1], axis=1)
    local_sum = jnp.sum(depth_weight[:, None, :, None] * gradient, axis=0)
    total_cells = cells_x * depth_cells * cells_y
    smoothed = lax.psum_scatter(local_sum, "shot", scatter_dimension=0, tiled=True)
    for sweep_index in range(2):
        rim_field = extended(smoothed, (("shot", 0), ("depth", 1)), 1)
        smoothed = relax_once(pad_axis(rim_field, 2, 1), smoothed, smooth_coef)
    square_sum = lax.psum(jnp.sum(smoothed * smoothed), ("shot", "depth"))
    norm_scale = jnp.sqrt(square_sum / total_cells + 1e-06)
    grad_dir = smoothed / norm_scale
    model_next = model * (1.0 - 0.25 * jnp.tanh(grad_dir))
    model_full = lax.all_gather(model_next, "shot", axis=0, tiled=True)
    final_padded = extended(wave_pair[0], (("depth", 2),), 4)
    final_applied = apply_operator(final_padded, aniso_hs, aniso_cs)
    wave_next = (
        2.0 * wave_pair[0]
        - old_pair[0]
        + model_full * final_applied
        + source_term(rec_data.shape[1])
    )
    return (model_next, grad_dir, wave_next)


def solution(mesh):
    return jax.shard_map(
        body,
        mesh=mesh,
        in_specs=(
            P("shot", None, "depth", None),
            P("shot", None, "depth", None),
            P("shot", None, "depth", None),
            P("shot", None, "depth", None),
            P("shot", "depth", None),
            P("shot", "depth", None),
            P("shot", "depth", None),
            P("shot", "depth", None),
            P(None, "depth", None),
            P("shot"),
            P("shot"),
            P("shot", None),
            P("shot", None),
            P("shot", None, None),
        ),
        out_specs=(
            P("shot", "depth", None),
            P("shot", "depth", None),
            P("shot", None, "depth", None),
        ),
        check_vma=False,
    )
```

profile of v0, /device:TPU:1, one launch (start us, length us, event | category | flops | bytes accessed | tf_op | source)
XLA Modules:
  0.0 478.0 jit_solution(2410898033158480735)
XLA Ops:
  7.3 1.3 fusion.157
  8.6 1.3 collective-permute-start
  9.9 4.7 collective-permute-start.1
  15.3 1.0 pad_maximum_fusion
  17.1 47.3 %all_gather.12 = f32[64,16,128]{2,1,0:T(8,128)S(1)} all-gather(f32[2,16,128]{2,1,0:T(8,128)S(1)} %copy-done.13), channel_id=1, replica_groups=mesh['shot'=32,'depth'=8] {'shot'}, dimensions={0}, use_global_device_ids=true | all-gather | bytes 540672 | tf_op jit(solution)/shard_map/all_gather | solution.py:95
  64.4 38.1 %all_gather.13 = f32[64,16,128]{2,1,0:T(8,128)S(1)} all-gather(f32[2,16,128]{2,1,0:T(8,128)S(1)} %copy-done.14), channel_id=1, replica_groups=mesh['shot'=32,'depth'=8] {'shot'}, dimensions={0}, use_global_device_ids=true | all-gather | bytes 540672 | tf_op jit(solution)/shard_map/all_gather | solution.py:96
  102.6 2.2 fusion.155
  105.3 39.5 %all_gather.14 = f32[64,16,128]{2,1,0:T(8,128)S(1)} all-gather(f32[2,16,128]{2,1,0:T(8,128)S(1)} %copy-done.11), channel_id=1, replica_groups=mesh['shot'=32,'depth'=8] {'shot'}, dimensions={0}, use_global_device_ids=true | all-gather | bytes 540672 | tf_op jit(solution)/shard_map/all_gather | solution.py:94
  146.6 4.6 fusion.87
  152.1 1.3 collective-permute-start.2
  153.4 4.7 collective-permute-start.3
  159.1 2.8 collective-permute-done.2
  161.9 1.0 collective-permute-done.3
  162.9 2.7 multiply_add_fusion
  165.7 5.4 %fusion.37 = f32[2,1,64,16,128]{4,3,2,1,0:T(8,128)S(1)} fusion(f32[2,1,64,16,128]{4,3,2,1,0:T(8,128)S(1)} %get-tuple-element.7, f32[2,1,64,16,128]{4,3,2,1,0:T(8,128)S(1)} %multiply_add_fusion, f32[2,1,64,4,128]{4,3,2,1,0:T(4,128)S(1)} %collective-permute-done.2, f32[2,1,64,4,128]{4,3,2,1,0:T(4,128)} %collective-permute-done.3, ...), kind=kLoop, calls=%fused_computation.123 | loop fusion | flops 15990784 | bytes 4718592 | tf_op jit(solution)/shard_map/add | solution.py:64
  173.0 1.2 convolution_bitcast_fusion
  174.3 108.8 %reduce-scatter.2.cloned.1.call-done = f32[2,16,128]{2,1,0:T(8,128)} async-done(((f32[64,16,128]{2,1,0:T(8,128)}), f32[2,16,128]{2,1,0:T(8,128)}) %reduce-scatter.2.cloned.1.call-update) | async-done | bytes 16400 | tf_op jit(solution)/shard_map/reduce_scatter | solution.py:153
  283.8 8.1 %collective-permute-start.5 = (f32[1,16,128]{2,1,0:T(8,128)S(1)}, f32[1,16,128]{2,1,0:T(8,128)S(1)}, u32[]{:S(2)}, u32[]{:S(2)}) collective-permute-start(f32[1,16,128]{2,1,0:T(8,128)S(1)} %get-tuple-element.24), channel_id=1, source_target_pairs={{0,8},{8,16},{16,24},{24,32},{32,40},{40,48},{48,56},{56,64},{64,7... | collective-permute-start | bytes 24584 | tf_op jit(solution)/shard_map/ppermute | solution.py:15
  291.9 1.5 fusion.129
  293.5 1.9 collective-permute-start.4
  295.4 3.0 collective-permute-done.4
  298.4 1.3 collective-permute-start.6
  299.7 4.0 collective-permute-start.7
  303.8 1.3 collective-permute-start.12
  305.1 4.0 collective-permute-start.13
  309.3 1.9 collective-permute-start.8
  311.3 3.6 collective-permute-start.9
  315.7 1.3 collective-permute-start.10
  317.0 4.0 collective-permute-start.11
  322.5 95.2 %psum.7 = f32[]{:T(128)} all-reduce(f32[]{:T(128)} %get-tuple-element.5), channel_id=1, replica_groups=mesh['shot'=32,'depth'=8] {'shot','depth'}, use_global_device_ids=true, to_apply=%region_3.4 | all-reduce | flops 1 | bytes 8 | tf_op jit(solution)/shard_map/psum | solution.py:157
  419.0 41.2 %all_gather.15 = f32[64,16,128]{2,1,0:T(8,128)S(1)} all-gather(f32[2,16,128]{2,1,0:T(8,128)S(1)} %get-tuple-element.3), channel_id=1, replica_groups=mesh['shot'=32,'depth'=8] {'shot'}, dimensions={0}, use_global_device_ids=true | all-gather | bytes 540672 | tf_op jit(solution)/shard_map/all_gather | solution.py:161
  460.2 10.9 %fusion.100 = f32[1,64,16,128]{3,2,1,0:T(8,128)} fusion(f32[1,64,16,128]{3,2,1,0:T(8,128)} %copy-done.2, f32[1,64,16,128]{3,2,1,0:T(8,128)S(1)} %multiply_add_fusion.2, f32[64,16,128]{2,1,0:T(8,128)S(1)} %all_gather.13, f32[64,16,128]{2,1,0:T(8,128)S(1)} %all_gather.12, f32[64,16,128]{2,1,0:T(8,128)S(1)} %all_gather.15, ...), kind=kLoop, calls=%fused_computation.213 | loop fusion | flops 9306112 | bytes 3932188 | tf_op jit(solution)/shard_map/add | solution.py:165
  (82 shorter events, 10.1 us)
Async XLA Ops:
  7.2 8.1 %copy-start.1 = (f32[1,64,16,128]{3,2,1,0:T(8,128)S(1)}, f32[1,64,16,128]{3,2,1,0:T(8,128)}, u32[]{:S(2)}) copy-start(f32[1,64,16,128]{3,2,1,0:T(8,128)} %param.15) | copy-start | bytes 1572868
  7.2 8.1 %copy-start = (f32[1,64,16,128]{3,2,1,0:T(8,128)S(1)}, f32[1,64,16,128]{3,2,1,0:T(8,128)}, u32[]{:S(2)}) copy-start(f32[1,64,16,128]{3,2,1,0:T(8,128)} %param.17) | copy-start | bytes 1572868
  7.2 275.9 %reduce-scatter.2.cloned.1.call-start = ((), (), s32[]{:S(2)}) async-start(), calls=%async_computation.1 | async-start | bytes 540672 | tf_op jit(solution)/shard_map/reduce_scatter | solution.py:153
  7.2 9.2 %copy-start.15 = (f32[1,3]{1,0:T(1,128)S(1)}, f32[1,3]{1,0:T(1,128)}, u32[]{:S(2)}) copy-start(f32[1,3]{1,0:T(1,128)} %param.26) | copy-start | bytes 40
  7.2 9.8 %copy-start.18 = (s32[1,128]{1,0:T(1,128)S(1)}, s32[1,128]{1,0:T(1,128)}, u32[]{:S(2)}) copy-start(s32[1,128]{1,0:T(1,128)} %param.25) | copy-start | bytes 1540
  7.3 9.8 %copy-start.17 = (f32[1,2,128]{2,1,0:T(2,128)S(1)}, f32[1,2,128]{2,1,0:T(2,128)}, u32[]{:S(2)}) copy-start(f32[1,2,128]{2,1,0:T(2,128)} %param.27) | copy-start | bytes 3076
  7.3 9.8 %copy-start.13 = (f32[2,16,128]{2,1,0:T(8,128)S(1)}, f32[2,16,128]{2,1,0:T(8,128)}, u32[]{:S(2)}) copy-start(f32[2,16,128]{2,1,0:T(8,128)} %param.19) | copy-start | bytes 49156
  8.6 55.8 %copy-start.14 = (f32[2,16,128]{2,1,0:T(8,128)S(1)}, f32[2,16,128]{2,1,0:T(8,128)}, u32[]{:S(2)}) copy-start(f32[2,16,128]{2,1,0:T(8,128)} %param.20) | copy-start | bytes 49156
  8.6 136.2 %collective-permute-start = (f32[2,1,64,4,128]{4,3,2,1,0:T(4,128)S(1)}, f32[2,1,64,4,128]{4,3,2,1,0:T(4,128)S(1)}, u32[]{:S(2)}, u32[]{:S(2)}) collective-permute-start(f32[2,1,64,4,128]{4,3,2,1,0:T(4,128)S(1)} %get-tuple-element.13), channel_id=1, source_target_pairs={{1,0},{2,1},{3,2},{4,3},{5,4},{6,5},{7,6},{9,8},{10,9},{11,10},{12... | collective-permute-start | bytes 786440 | tf_op jit(solution)/shard_map/ppermute | solution.py:18
  9.9 134.9 %collective-permute-start.1 = (f32[2,1,64,4,128]{4,3,2,1,0:T(4,128)S(1)}, f32[2,1,64,4,128]{4,3,2,1,0:T(4,128)S(1)}, u32[]{:S(2)}, u32[]{:S(2)}) collective-permute-start(f32[2,1,64,4,128]{4,3,2,1,0:T(4,128)S(1)} %get-tuple-element.14), channel_id=1, source_target_pairs={{0,1},{1,2},{2,3},{3,4},{4,5},{5,6},{6,7},{8,9},{9,10},{10,11},{11... | collective-permute-start | bytes 786440 | tf_op jit(solution)/shard_map/ppermute | solution.py:15
  16.4 89.0 %copy-start.11 = (f32[2,16,128]{2,1,0:T(8,128)S(1)}, f32[2,16,128]{2,1,0:T(8,128)}, u32[]{:S(2)}) copy-start(f32[2,16,128]{2,1,0:T(8,128)} %param.18) | copy-start | bytes 49156
  145.1 1.2 copy-start.4
  145.1 1.3 copy-start.7
  145.1 1.5 copy-start.8
  146.6 12.1 %copy-start.16 = (s32[16,2,4]{0,2,1:T(4,128)S(1)}, s32[16,2,4]{0,2,1:T(4,128)}, u32[]{:S(2)}) copy-start(s32[16,2,4]{0,2,1:T(4,128)} %param.22) | copy-start | bytes 1540
  152.1 9.8 %collective-permute-start.2 = (f32[2,1,64,4,128]{4,3,2,1,0:T(4,128)}, f32[2,1,64,4,128]{4,3,2,1,0:T(4,128)S(1)}, u32[]{:S(2)}, u32[]{:S(2)}) collective-permute-start(f32[2,1,64,4,128]{4,3,2,1,0:T(4,128)} %get-tuple-element.10), channel_id=1, source_target_pairs={{1,0},{2,1},{3,2},{4,3},{5,4},{6,5},{7,6},{9,8},{10,9},{11,10},{12... | collective-permute-start | bytes 786440 | tf_op jit(solution)/shard_map/ppermute | solution.py:18
  153.4 9.5 %collective-permute-start.3 = (f32[2,1,64,4,128]{4,3,2,1,0:T(4,128)}, f32[2,1,64,4,128]{4,3,2,1,0:T(4,128)}, u32[]{:S(2)}, u32[]{:S(2)}) collective-permute-start(f32[2,1,64,4,128]{4,3,2,1,0:T(4,128)} %get-tuple-element.9), channel_id=1, source_target_pairs={{0,1},{1,2},{2,3},{3,4},{4,5},{5,6},{6,7},{8,9},{9,10},{10,11},{11... | collective-permute-start | bytes 786440 | tf_op jit(solution)/shard_map/ppermute | solution.py:15
  165.6 6.4 %copy-start.6 = (f32[2,1,64,16,128]{4,3,2,1,0:T(8,128)S(1)}, f32[2,1,64,16,128]{4,3,2,1,0:T(8,128)}, u32[]{:S(2)}) copy-start(f32[2,1,64,16,128]{4,3,2,1,0:T(8,128)} %get-tuple-element.8) | copy-start | bytes 3145732
  283.8 11.6 %collective-permute-start.5 = (f32[1,16,128]{2,1,0:T(8,128)S(1)}, f32[1,16,128]{2,1,0:T(8,128)S(1)}, u32[]{:S(2)}, u32[]{:S(2)}) collective-permute-start(f32[1,16,128]{2,1,0:T(8,128)S(1)} %get-tuple-element.24), channel_id=1, source_target_pairs={{0,8},{8,16},{16,24},{24,32},{32,40},{40,48},{48,56},{56,64},{64,7... | collective-permute-start | bytes 24584 | tf_op jit(solution)/shard_map/ppermute | solution.py:15
  291.9 3.5 copy-start.9
  291.9 17.3 %copy-start.10 = (f32[2,16,128]{2,1,0:T(8,128)S(1)}, f32[2,16,128]{2,1,0:T(8,128)}, u32[]{:S(2)}) copy-start(f32[2,16,128]{2,1,0:T(8,128)} %param.21) | copy-start | bytes 49156
  293.5 27.5 %copy-start.2 = (f32[1,64,16,128]{3,2,1,0:T(8,128)}, f32[1,64,16,128]{3,2,1,0:T(8,128)S(1)}, u32[]{:S(2)}) copy-start(f32[1,64,16,128]{3,2,1,0:T(8,128)S(1)} %fusion.129) | copy-start | bytes 1572868
  293.5 5.0 %collective-permute-start.4 = (f32[1,16,128]{2,1,0:T(8,128)S(1)}, f32[1,16,128]{2,1,0:T(8,128)S(1)}, u32[]{:S(2)}, u32[]{:S(2)}) collective-permute-start(f32[1,16,128]{2,1,0:T(8,128)S(1)} %get-tuple-element.23), channel_id=1, source_target_pairs={{8,0},{16,8},{24,16},{32,24},{40,32},{48,40},{56,48},{64,56},{72,6... | collective-permute-start | bytes 24584 | tf_op jit(solution)/shard_map/ppermute | solution.py:18
  298.4 10.6 %collective-permute-start.6 = (f32[4,1,128]{2,1,0:T(1,128)S(1)}, f32[4,1,128]{2,1,0:T(1,128)S(1)}, u32[]{:S(2)}, u32[]{:S(2)}) collective-permute-start(f32[4,1,128]{2,1,0:T(1,128)S(1)} %get-tuple-element.20), channel_id=1, source_target_pairs={{1,0},{2,1},{3,2},{4,3},{5,4},{6,5},{7,6},{9,8},{10,9},{11,10},{12... | collective-permute-start | bytes 6152 | tf_op jit(solution)/shard_map/ppermute | solution.py:18
  299.7 9.4 %collective-permute-start.7 = (f32[4,1,128]{2,1,0:T(1,128)S(1)}, f32[4,1,128]{2,1,0:T(1,128)S(1)}, u32[]{:S(2)}, u32[]{:S(2)}) collective-permute-start(f32[4,1,128]{2,1,0:T(1,128)S(1)} %get-tuple-element.19), channel_id=1, source_target_pairs={{0,1},{1,2},{2,3},{3,4},{4,5},{5,6},{6,7},{8,9},{9,10},{10,11},{11... | collective-permute-start | bytes 6152 | tf_op jit(solution)/shard_map/ppermute | solution.py:15
  303.8 17.2 %collective-permute-start.12 = (f32[1,64,4,128]{3,2,1,0:T(4,128)S(1)}, f32[1,64,4,128]{3,2,1,0:T(4,128)S(1)}, u32[]{:S(2)}, u32[]{:S(2)}) collective-permute-start(f32[1,64,4,128]{3,2,1,0:T(4,128)S(1)} %get-tuple-element.16), channel_id=1, source_target_pairs={{1,0},{2,1},{3,2},{4,3},{5,4},{6,5},{7,6},{9,8},{10,9},{11,10},{12... | collective-permute-start | bytes 393224 | tf_op jit(solution)/shard_map/ppermute | solution.py:18
  305.1 15.9 %collective-permute-start.13 = (f32[1,64,4,128]{3,2,1,0:T(4,128)S(1)}, f32[1,64,4,128]{3,2,1,0:T(4,128)S(1)}, u32[]{:S(2)}, u32[]{:S(2)}) collective-permute-start(f32[1,64,4,128]{3,2,1,0:T(4,128)S(1)} %get-tuple-element.15), channel_id=1, source_target_pairs={{0,1},{1,2},{2,3},{3,4},{4,5},{5,6},{6,7},{8,9},{9,10},{10,11},{11... | collective-permute-start | bytes 393224 | tf_op jit(solution)/shard_map/ppermute | solution.py:15
  309.3 5.6 %collective-permute-start.8 = (f32[1,16,128]{2,1,0:T(8,128)S(1)}, f32[1,16,128]{2,1,0:T(8,128)S(1)}, u32[]{:S(2)}, u32[]{:S(2)}) collective-permute-start(f32[1,16,128]{2,1,0:T(8,128)S(1)} %get-tuple-element.22), channel_id=1, source_target_pairs={{8,0},{16,8},{24,16},{32,24},{40,32},{48,40},{56,48},{64,56},{72,6... | collective-permute-start | bytes 24584 | tf_op jit(solution)/shard_map/ppermute | solution.py:18
  311.3 4.4 collective-permute-start.9
  315.7 6.0 %collective-permute-start.10 = (f32[4,1,128]{2,1,0:T(1,128)S(1)}, f32[4,1,128]{2,1,0:T(1,128)S(1)}, u32[]{:S(2)}, u32[]{:S(2)}) collective-permute-start(f32[4,1,128]{2,1,0:T(1,128)S(1)} %get-tuple-element.18), channel_id=1, source_target_pairs={{1,0},{2,1},{3,2},{4,3},{5,4},{6,5},{7,6},{9,8},{10,9},{11,10},{12... | collective-permute-start | bytes 6152 | tf_op jit(solution)/shard_map/ppermute | solution.py:18
  317.0 4.7 collective-permute-start.11
  419.0 52.1 %copy-start.12 = (f32[2,16,128]{2,1,0:T(8,128)}, f32[2,16,128]{2,1,0:T(8,128)S(1)}, u32[]{:S(2)}) copy-start(f32[2,16,128]{2,1,0:T(8,128)S(1)} %get-tuple-element.3) | copy-start | bytes 49156
  (2 other events, 2.2 us)
Sparse Core Ops, SparseCore 0:
  173.1 109.8 reduce-scatter.1
where the time goes:
time: 479 us; the launch traced here: 478 us
  blocking collectives  261 us (54%)
  waiting for transfers between devices  116 us (24%)
  starting transfers between devices  43.4 us (9%)
  other arithmetic  34.4 us (7%)
  between operations  16.6 us (3%)
    reduce_scatter x1, waiting for transfers between devices, body(): lax.psum_scatter(local_sum, 'shot', scatter_dimension=0, tiled=True)  109 us
    psum x1, blocking collectives, body(): square_sum = lax.psum(jnp.sum(smoothed * smoothed), ('shot', 'depth'))  95.2 us
    all_gather x1, blocking collectives, body(): lax.all_gather(aniso_h, 'shot', axis=0, tiled=True)  47.3 us
    all_gather x1, blocking collectives, body(): model_full = lax.all_gather(model_next, 'shot', axis=0, tiled=True)  41.2 us
    all_gather x1, blocking collectives, body(): lax.all_gather(model, 'shot', axis=0, tiled=True)  39.5 us
    all_gather x1, blocking collectives, body(): lax.all_gather(aniso_c, 'shot', axis=0, tiled=True)  38.1 us
    ppermute x7, starting transfers between devices, extended(): lax.ppermute(lax.slice_in_dim(block, block.shape[dim] - width, None, axis...  33.1 us
    add x1, other arithmetic, body(): 2.0 * wave_pair[0] - old_pair[0] + model_full * final_applied  10.9 us
  transfers between devices with their start and end apart: 15, of which 5 were waited for; matrix products, arithmetic and copies ran while one was open for 2% of the time, Pallas kernels for 0%

commit v1 on v0

v1 whole, which is shorter than its diff:
```python
import jax
import jax.numpy as jnp
from jax import lax
from jax.sharding import PartitionSpec as P

second_coef = (-205.0 / 72.0, 8.0 / 5.0, -1.0 / 5.0, 8.0 / 315.0, -1.0 / 560.0)
first_coef = (0.8, -0.2, 4.0 / 105.0, -1.0 / 280.0)


def pad_axis(field, axis, width):
    widths = [(0, 0)] * field.ndim
    widths[axis] = (width, width)
    return jnp.pad(field, widths)


def shifted(padded, axis, offset, count):
    return lax.slice_in_dim(padded, 4 + offset, 4 + offset + count, axis=axis)


def second_along(padded, axis, count):
    result = second_coef[0] * shifted(padded, axis, 0, count)
    for offset in range(1, 5):
        result = result + second_coef[offset] * (
            shifted(padded, axis, offset, count) + shifted(padded, axis, -offset, count)
        )
    return result


def first_along(padded, axis, count):
    result = first_coef[0] * (shifted(padded, axis, 1, count) - shifted(padded, axis, -1, count))
    for offset in range(2, 5):
        result = result + first_coef[offset - 1] * (
            shifted(padded, axis, offset, count) - shifted(padded, axis, -offset, count)
        )
    return result


def apply_operator(padded_z, aniso_h, aniso_c):
    ndim = padded_z.ndim
    axis_x, axis_z, axis_y = (ndim - 3, ndim - 2, ndim - 1)
    count_z = padded_z.shape[axis_z] - 8
    count_x = padded_z.shape[axis_x]
    count_y = padded_z.shape[axis_y]
    centre = lax.slice_in_dim(padded_z, 4, 4 + count_z, axis=axis_z)
    depth_two = second_along(padded_z, axis_z, count_z)
    depth_one = first_along(padded_z, axis_z, count_z)
    lateral = second_along(pad_axis(centre, axis_x, 4), axis_x, count_x) + second_along(
        pad_axis(centre, axis_y, 4), axis_y, count_y
    )
    crossing = first_along(pad_axis(depth_one, axis_x, 4), axis_x, count_x)
    return aniso_h * lateral + depth_two + aniso_c * crossing


def relax_once(padded, centre, coef):
    neighbours = padded[2:, 1:-1, 1:-1] + padded[:-2, 1:-1, 1:-1]
    neighbours = neighbours + padded[1:-1, 2:, 1:-1] + padded[1:-1, :-2, 1:-1]
    neighbours = neighbours + padded[1:-1, 1:-1, 2:] + padded[1:-1, 1:-1, :-2]
    return centre + coef * (neighbours - 6.0 * centre)


SHOT = ("xh", "z", "core")
DEPTH = ("xl", "y")
PEERS = ("xh", "z")
SWAP = [(0, 1), (1, 0)]


def both_cores(mine):
    other = lax.ppermute(mine, "core", SWAP)
    first = lax.axis_index("core") == 0
    return jnp.stack([jnp.where(first, mine, other), jnp.where(first, other, mine)], axis=1)


def gather_rows(block):
    peers = lax.axis_size(PEERS)
    spread = jnp.broadcast_to(block[None], (peers, *block.shape))
    mine = lax.all_to_all(spread, PEERS, 0, 0, tiled=True)
    return both_cores(mine)


def halo(block, dim, width):
    count = lax.axis_size(DEPTH)
    forward = [(i, i + 1) for i in range(count - 1)]
    backward = [(target, source) for source, target in forward]
    low = lax.ppermute(
        lax.slice_in_dim(block, block.shape[dim] - width, None, axis=dim), DEPTH, forward
    )
    high = lax.ppermute(lax.slice_in_dim(block, 0, width, axis=dim), DEPTH, backward)
    return low, high


def extended_z(block, dim, width):
    low, high = halo(block, dim, width)
    return jnp.concatenate([low, block, high], axis=dim)


def body(
    u_prev,
    u_cur,
    a_prev,
    a_cur,
    model,
    aniso_h,
    aniso_c,
    smooth_coef,
    bin_onehot,
    shot_group,
    src_cell,
    rec_cell,
    src_wave,
    rec_data,
):
    shot_count, cells_x, cells_z, cells_y = u_cur.shape
    depth_cells = cells_z * lax.axis_size(DEPTH)
    z_start = lax.axis_index(DEPTH) * cells_z
    rows = model.shape[0]
    own = jnp.stack([model, aniso_h, aniso_c, smooth_coef])
    slabs = gather_rows(own)
    slabs = jnp.moveaxis(slabs, 2, 0).reshape(4, cells_x, cells_z, cells_y)
    model_slab, aniso_hs, aniso_cs, coef_slab = slabs[0], slabs[1], slabs[2], slabs[3]
    x_pos = lax.broadcasted_iota(jnp.int32, (cells_x, cells_z, cells_y), 0)
    z_pos = lax.broadcasted_iota(jnp.int32, (cells_x, cells_z, cells_y), 1) + z_start
    y_pos = lax.broadcasted_iota(jnp.int32, (cells_x, cells_z, cells_y), 2)
    flat_pos = (x_pos * depth_cells + z_pos) * cells_y + y_pos
    receiver_x = rec_cell // (depth_cells * cells_y)
    receiver_z = rec_cell // cells_y % depth_cells
    receiver_y = rec_cell % cells_y
    receivers = rec_cell.shape[1]

    def source_term(step_index):
        hits = flat_pos[None] == src_cell[:, None, None, None]
        return jnp.where(hits, src_wave[:, step_index][:, None, None, None], 0.0)

    def receiver_term(step_index):
        records = rec_data[:, step_index]
        along_x = (receiver_x[..., None] == jnp.arange(cells_x, dtype=jnp.int32)).astype(
            jnp.float32
        ) * records[..., None]
        along_z = (receiver_z[..., None] == z_start + jnp.arange(cells_z, dtype=jnp.int32)).astype(
            jnp.float32
        )
        along_y = (receiver_y[..., None] == jnp.arange(cells_y, dtype=jnp.int32)).astype(
            jnp.float32
        )
        plane = (along_x[..., :, None] * along_z[..., None, :]).reshape(
            shot_count, receivers, cells_x * cells_z
        )
        placed = jnp.einsum("srk,sry->sky", plane, along_y, precision=lax.Precision.HIGHEST)
        return placed.reshape(shot_count, cells_x, cells_z, cells_y)

    wave, adjoint = u_cur, a_cur
    wave_old, adjoint_old = u_prev, a_prev
    gradient = jnp.zeros_like(u_cur)
    for step_index in range(rec_data.shape[1]):
        pair = extended_z(jnp.stack([wave, adjoint]), 3, 4) if step_index == 0 else None
        wave_ext = pair[0] if step_index == 0 else extended_z(wave, 2, 4)
        adjoint_ext = pair[1] if step_index == 0 else extended_z(adjoint, 2, 4)
        applied = apply_operator(wave_ext, aniso_hs, aniso_cs)
        adjoint_applied = apply_operator(adjoint_ext, aniso_hs, aniso_cs)
        gradient = gradient + adjoint * applied
        wave_new = 2.0 * wave - wave_old + model_slab * applied + source_term(step_index)
        adjoint_new = (
            2.0 * adjoint - adjoint_old + model_slab * adjoint_applied + receiver_term(step_index)
        )
        wave_old, wave = wave, wave_new
        adjoint_old, adjoint = adjoint, adjoint_new
    nbins = bin_onehot.shape[2]
    groups = bin_onehot.shape[0]
    powers = jnp.exp2(-jnp.arange(nbins, dtype=jnp.float32))
    block_weight = jnp.sum(bin_onehot.astype(jnp.float32) * powers, axis=2)
    chosen = (shot_group[:, None] == jnp.arange(groups, dtype=jnp.int32)).astype(jnp.float32)
    shot_weight = jnp.dot(chosen, block_weight, precision=lax.Precision.HIGHEST)
    depth_weight = jnp.repeat(shot_weight, cells_z // bin_onehot.shape[1], axis=1)
    local_sum = jnp.sum(depth_weight[:, None, :, None] * gradient, axis=0)
    total_cells = cells_x * depth_cells * cells_y

    peers = lax.axis_size(PEERS)
    core = lax.axis_index("core")
    parts = local_sum.reshape(peers, 2, rows, cells_z, cells_y)
    keep = jnp.where(core == 0, parts[:, 0], parts[:, 1])
    send = jnp.where(core == 0, parts[:, 1], parts[:, 0])
    chip_sum = keep + lax.ppermute(send, "core", SWAP)
    summed = jnp.sum(lax.all_to_all(chip_sum, PEERS, 0, 0, tiled=True), axis=0)
    summed = gather_rows(summed).reshape(cells_x, cells_z, cells_y)

    coef_ext = extended_z(coef_slab, 1, 1)
    low, high = halo(summed, 1, 2)
    wide = jnp.concatenate([low, summed, high], axis=1)
    index = lax.axis_index(DEPTH)
    inside = jnp.ones((cells_z + 2,), jnp.float32)
    inside = inside.at[0].set(jnp.where(index == 0, 0.0, 1.0))
    inside = inside.at[cells_z + 1].set(jnp.where(index == lax.axis_size(DEPTH) - 1, 0.0, 1.0))
    around = jnp.pad(wide, ((1, 1), (0, 0), (1, 1)))
    once = relax_once(around, wide[:, 1:-1], coef_ext) * inside[None, :, None]
    around = jnp.pad(once, ((1, 1), (0, 0), (1, 1)))
    smoothed = relax_once(around, once[:, 1:-1], coef_slab)
    slab_square = jnp.sum(smoothed * smoothed)
    squares = jnp.broadcast_to(slab_square, (lax.axis_size(DEPTH), 1, 128))
    square_sum = jnp.sum(lax.all_to_all(squares, DEPTH, 0, 0, tiled=True)[:, 0, 0])
    norm_scale = jnp.sqrt(square_sum / total_cells + 1e-06)
    direction = smoothed / norm_scale
    model_full = model_slab * (1.0 - 0.25 * jnp.tanh(direction))
    final_applied = apply_operator(extended_z(wave, 2, 4), aniso_hs, aniso_cs)
    wave_next = 2.0 * wave - wave_old + model_full * final_applied + source_term(rec_data.shape[1])
    start = lax.axis_index(SHOT) * rows
    model_next = lax.dynamic_slice_in_dim(model_full, start, rows, axis=0)
    grad_dir = lax.dynamic_slice_in_dim(direction, start, rows, axis=0)
    return (model_next, grad_dir, wave_next)


def solution(mesh):
    mesh = jax.sharding.Mesh(
        mesh.devices.reshape(2, 8, 2, 2, 4), ("xh", "z", "core", "xl", "y")
    )
    return jax.shard_map(
        body,
        mesh=mesh,
        in_specs=(
            P(SHOT, None, DEPTH, None),
            P(SHOT, None, DEPTH, None),
            P(SHOT, None, DEPTH, None),
            P(SHOT, None, DEPTH, None),
            P(SHOT, DEPTH, None),
            P(SHOT, DEPTH, None),
            P(SHOT, DEPTH, None),
            P(SHOT, DEPTH, None),
            P(None, DEPTH, None),
            P(SHOT),
            P(SHOT),
            P(SHOT, None),
            P(SHOT, None),
            P(SHOT, None, None),
        ),
        out_specs=(
            P(SHOT, DEPTH, None),
            P(SHOT, DEPTH, None),
            P(SHOT, None, DEPTH, None),
        ),
        check_vma=False,
    )
```

time: 479 us -> 146 us (0.30)
  blocking collectives: 261 us -> 29 us
  waiting for transfers between devices: 116 us -> 28.7 us
  other arithmetic: 34.4 us -> 19.9 us
  between operations: 16.6 us -> 3.06 us
  starting transfers between devices: 43.4 us -> 55.2 us
    all_gather x4 -> x0, blocking collectives: 166 us -> none  [the longest x1 47.3 us: body(): lax.all_gather(aniso_h, 'shot', axis=0, tiled=True)]
    reduce_scatter x1 -> x0, waiting for transfers between devices: 109 us -> none  [body(): lax.psum_scatter(local_sum, 'shot', scatter_dimension=0, tiled=True)]
    psum x1 -> x0, blocking collectives: 95.2 us -> none  [body(): square_sum = lax.psum(jnp.sum(smoothed * smoothed), ('shot', 'depth'))]
    all_to_all x0 -> x2, blocking collectives: none -> 29 us  [the longest x1 14.6 us: gather_rows(): mine = lax.all_to_all(spread, PEERS, 0, 0, tiled=True)]
    all_to_all x0 -> x2, waiting for transfers between devices: none -> 25 us  [the longest x1 20.7 us: gather_rows(): mine = lax.all_to_all(spread, PEERS, 0, 0, tiled=True)]
    all_to_all x0 -> x2, starting transfers between devices: none -> 20.8 us  [the longest x1 11.7 us: gather_rows(): mine = lax.all_to_all(spread, PEERS, 0, 0, tiled=True)]
    add x5, other arithmetic: 21 us -> 10.2 us  [the longest x2 5.56 us: body(): 2.0 * wave - wave_old + model_slab * applied + source_term(step_index)]
    ppermute x14 -> x13, starting transfers between devices: 43.3 us -> 34.4 us  [the longest x5 20.7 us: halo(): lax.ppermute(lax.slice_in_dim(block, block.shape[dim] - width, None, axis...]
  transfers between devices with their start and end apart: 15 -> 15, of which waited for: 5 -> 6; matrix products, arithmetic and copies ran while one was open for 2% -> 6% of each run, Pallas kernels for 0% -> 0%
where the time goes in v1:
time: 146 us; the launch traced here: 144 us
  starting transfers between devices  55.2 us (38%)
  blocking collectives  29 us (20%)
  waiting for transfers between devices  28.7 us (20%)
  other arithmetic  19.9 us (14%)
  local copies, waits for them, and re-layouts  6.17 us (4%)
  between operations  3.06 us (2%)
  matrix products  1.86 us (1%)
    all_to_all x1, waiting for transfers between devices, gather_rows(): mine = lax.all_to_all(spread, PEERS, 0, 0, tiled=True)  20.7 us
    ppermute x5, starting transfers between devices, halo(): lax.ppermute(lax.slice_in_dim(block, block.shape[dim] - width, None, axis...  20.7 us
    all_to_all x1, blocking collectives, gather_rows(): mine = lax.all_to_all(spread, PEERS, 0, 0, tiled=True)  14.6 us
    all_to_all x1, blocking collectives, body(): summed = jnp.sum(lax.all_to_all(chip_sum, PEERS, 0, 0, tiled=True), axis=0)  14.3 us
    all_to_all x1, starting transfers between devices, gather_rows(): mine = lax.all_to_all(spread, PEERS, 0, 0, tiled=True)  11.7 us
    all_to_all x1, starting transfers between devices, body(): lax.all_to_all(squares, DEPTH, 0, 0, tiled=True)[:, 0, 0]  9.14 us
    ppermute x5, starting transfers between devices, halo(): lax.ppermute(lax.slice_in_dim(block, 0, width, axis=dim), DEPTH, backward)  6.46 us
    ppermute x2, starting transfers between devices, both_cores(): other = lax.ppermute(mine, 'core', SWAP)  5.59 us
  transfers between devices with their start and end apart: 15, of which 6 were waited for; matrix products, arithmetic and copies ran while one was open for 6% of the time, Pallas kernels for 0%

profile of v1, /device:TPU:1, one launch (start us, length us, event | category | flops | bytes accessed | tf_op | source)
XLA Modules:
  0.0 143.9 jit_solution(9827854119065841997)
XLA Ops:
  1.4 1.1 broadcast_in_dim.71
  2.5 11.7 %all-to-all-start = ((f32[16,4,2,16,128]{4,3,2,1,0:T(8,128)}), f32[16,4,2,16,128]{4,3,2,1,0:T(8,128)S(1)}, u32[]{:S(2)}, u32[]{:S(2)}) async-start(f32[16,4,2,16,128]{4,3,2,1,0:T(8,128)} %broadcast_in_dim.71), calls=%async_computation | async-start | bytes 2097152 | tf_op jit(solution)/shard_map/all_to_all | solution.py:76
  14.4 3.2 %collective-permute-start.1 = (f32[2,1,64,4,128]{4,3,2,1,0:T(4,128)S(1)}, f32[2,1,64,4,128]{4,3,2,1,0:T(4,128)S(1)}, u32[]{:S(2)}, u32[]{:S(2)}) collective-permute-start(f32[2,1,64,4,128]{4,3,2,1,0:T(4,128)S(1)} %get-tuple-element.44), channel_id=1, source_target_pairs={{0,1},{1,2},{2,3},{3,4},{4,5},{5,6},{6,7},{8,9},{9,10},{10,11},{11... | collective-permute-start | bytes 786440 | tf_op jit(solution)/shard_map/ppermute | solution.py:84
  17.6 1.3 collective-permute-start.2
  20.6 20.7 %all-to-all-done = f32[16,4,2,16,128]{4,3,2,1,0:T(8,128)S(1)} async-done(((f32[16,4,2,16,128]{4,3,2,1,0:T(8,128)}), f32[16,4,2,16,128]{4,3,2,1,0:T(8,128)S(1)}, u32[]{:S(2)}, u32[]{:S(2)}) %all-to-all-start) | async-done | bytes 1048608 | tf_op jit(solution)/shard_map/all_to_all | solution.py:76
  41.3 2.5 %collective-permute-start = (f32[16,4,2,16,128]{4,3,2,1,0:T(8,128)S(1)}, f32[16,4,2,16,128]{4,3,2,1,0:T(8,128)}, u32[]{:S(2)}, u32[]{:S(2)}) collective-permute-start(f32[16,4,2,16,128]{4,3,2,1,0:T(8,128)S(1)} %all-to-all-done), channel_id=1, source_target_pairs={{0,8},{8,0},{1,9},{9,1},{2,10},{10,2},{3,11},{11,3},{4,12},{12,4},... | collective-permute-start | bytes 3145736 | tf_op jit(solution)/shard_map/ppermute | solution.py:68
  46.3 1.5 %select_bitcast_fusion.1 = (f32[16,1,4,2,16,128]{5,4,3,2,0,1:T(8,128)S(1)}, f32[16,1,4,2,16,128]{5,4,3,2,0,1:T(8,128)S(1)}) fusion(f32[16,4,2,16,128]{4,3,2,1,0:T(8,128)S(1)} %all-to-all-done, f32[16,4,2,16,128]{4,3,2,1,0:T(8,128)} %collective-permute-done, pred[]{:T(512)S(6)} %eq.135), kind=kLoop, calls=%fused_computation.61 | loop fusion | flops 524288 | bytes 4194305 | tf_op jit(solution)/shard_map/stack | solution.py:70
  48.0 1.0 fusion.217
  49.1 0.9 copy-done.4
  50.0 2.6 %select_add_fusion.1 = (f32[1,64,16,128]{3,2,1,0:T(8,128)S(1)}, f32[1,64,16,128]{3,2,1,0:T(8,128)S(1)}) fusion(f32[1,64,16,128]{3,2,1,0:T(8,128)S(1)} %bitcast.110, f32[1,64,16,128]{3,2,1,0:T(8,128)S(1)} %copy-done.4, f32[1,64,16,128]{3,2,1,0:T(8,128)S(1)} %copy-done, f32[]{:T(128)} %bitcast.29, s32[]{:T(128)} %bitcast.97, s32[16]{0:T(128)S(1)} %iota_add_fusion, ...), kind=kLoop, calls=%fused_computation.346 | loop fusion | flops 8257536 | bytes 8913224 | tf_op jit(solution)/shard_map/add | solution.py:160
  52.7 1.3 collective-permute-start.3
  54.0 4.0 %collective-permute-start.4 = (f32[1,64,4,128]{3,2,1,0:T(4,128)S(1)}, f32[1,64,4,128]{3,2,1,0:T(4,128)S(1)}, u32[]{:S(2)}, u32[]{:S(2)}) collective-permute-start(f32[1,64,4,128]{3,2,1,0:T(4,128)S(1)} %get-tuple-element.58), channel_id=1, source_target_pairs={{0,1},{1,2},{2,3},{3,4},{4,5},{5,6},{6,7},{8,9},{9,10},{10,11},{11... | collective-permute-start | bytes 393224 | tf_op jit(solution)/shard_map/ppermute | solution.py:84
  59.3 0.9 collective-permute-done.4
  60.9 2.9 %select_add_fusion = (f32[1,64,16,128]{3,2,1,0:T(8,128)S(1)}, f32[1,64,16,128]{3,2,1,0:T(8,128)S(1)}) fusion(f32[1,64,16,128]{3,2,1,0:T(8,128)S(1)} %bitcast.111, f32[1,64,16,128]{3,2,1,0:T(8,128)S(1)} %copy-done, f32[1,64,16,128]{3,2,1,0:T(8,128)S(1)} %get-tuple-element.34, f32[]{:T(128)} %bitcast.43, s32[]{:T(128)} %bitcast.99, s32[16]{0:T(128)S(1)} %iota_add_fusion, ...), kind=kLoop, calls=%fused_computation.343 | loop fusion | flops 9306112 | bytes 4456776 | tf_op jit(solution)/shard_map/add | solution.py:160
  63.8 1.7 %fusion.3 = f32[1,64,16,128]{3,2,1,0:T(8,128)S(1)} fusion(f32[1,64,16,128]{3,2,1,0:T(8,128)S(1)} %get-tuple-element.31, f32[1,64,16,128]{3,2,1,0:T(8,128)S(1)} %bitcast.112, f32[1,64,16,128]{3,2,1,0:T(8,128)S(1)} %bitcast.104, f32[1,64,16,128]{3,2,1,0:T(8,128)S(1)} %get-tuple-element.47, f32[1,64,16,128]{3,2,1,0:T(8,128)S(1)} %bitcast.108, ...), kind=kOutput, calls=%fused_computation.58 | convolution fusion | flops 209600512 | bytes 9478720 | tf_op jit(solution)/shard_map/srk,sry->sky/dot_general | solution.py:147
  65.6 1.6 %collective-permute-start.5 = (f32[16,2,16,128]{3,2,1,0:T(8,128)S(1)}, f32[16,2,16,128]{3,2,1,0:T(8,128)S(1)}, u32[]{:S(2)}, u32[]{:S(2)}) collective-permute-start(f32[16,2,16,128]{3,2,1,0:T(8,128)S(1)} %select_bitcast_fusion.4), channel_id=1, source_target_pairs={{0,8},{8,0},{1,9},{9,1},{2,10},{10,2},{3,11},{11,3},{4,12},{12,4},... | collective-permute-start | bytes 786440 | tf_op jit(solution)/shard_map/ppermute | solution.py:181
  67.2 1.2 collective-permute-done.5
  68.4 14.3 %all_to_all.20 = f32[16,2,16,128]{3,2,1,0:T(8,128)S(1)} all-to-all(f32[16,2,16,128]{3,2,1,0:T(8,128)S(1)} %fusion.201), channel_id=1, replica_groups=mesh['xh'=2,'z'=8,'core'=2,'xl'=2,'y'=4] {'xh','z'}, dimensions={0} | all-to-all | bytes 524288 | tf_op jit(solution)/shard_map/all_to_all | solution.py:182
  82.8 14.6 %all_to_all.21 = f32[16,2,16,128]{3,2,1,0:T(8,128)S(1)} all-to-all(f32[16,2,16,128]{3,2,1,0:T(8,128)S(1)} %broadcast_in_dim.77), channel_id=1, replica_groups=mesh['xh'=2,'z'=8,'core'=2,'xl'=2,'y'=4] {'xh','z'}, dimensions={0} | all-to-all | bytes 524288 | tf_op jit(solution)/shard_map/all_to_all | solution.py:76
  97.5 3.1 %collective-permute-start.6 = (f32[16,2,16,128]{3,2,1,0:T(8,128)S(1)}, f32[16,2,16,128]{3,2,1,0:T(8,128)}, u32[]{:S(2)}, u32[]{:S(2)}) collective-permute-start(f32[16,2,16,128]{3,2,1,0:T(8,128)S(1)} %all_to_all.21), channel_id=1, source_target_pairs={{0,8},{8,0},{1,9},{9,1},{2,10},{10,2},{3,11},{11,3},{4,12},{12,4},... | collective-permute-start | bytes 786440 | tf_op jit(solution)/shard_map/ppermute | solution.py:68
  100.7 1.3 collective-permute-start.10
  102.0 4.7 %collective-permute-start.9 = (f32[64,1,128]{2,1,0:T(1,128)S(1)}, f32[64,1,128]{2,1,0:T(1,128)S(1)}, u32[]{:S(2)}, u32[]{:S(2)}) collective-permute-start(f32[64,1,128]{2,1,0:T(1,128)S(1)} %get-tuple-element.50), channel_id=1, source_target_pairs={{0,1},{1,2},{2,3},{3,4},{4,5},{5,6},{6,7},{8,9},{9,10},{10,11},{11... | collective-permute-start | bytes 98312 | tf_op jit(solution)/shard_map/ppermute | solution.py:84
  106.7 1.0 select_bitcast_fusion.3
  107.8 3.4 %collective-permute-start.7 = (f32[64,2,128]{2,1,0:T(2,128)S(1)}, f32[64,2,128]{2,1,0:T(2,128)S(1)}, u32[]{:S(2)}, u32[]{:S(2)}) collective-permute-start(f32[64,2,128]{2,1,0:T(2,128)S(1)} %get-tuple-element.52), channel_id=1, source_target_pairs={{0,1},{1,2},{2,3},{3,4},{4,5},{5,6},{6,7},{8,9},{9,10},{10,11},{11... | collective-permute-start | bytes 196616 | tf_op jit(solution)/shard_map/ppermute | solution.py:84
  111.2 1.3 collective-permute-start.8
  112.5 1.3 collective-permute-start.11
  113.8 5.4 %collective-permute-start.12 = (f32[1,64,4,128]{3,2,1,0:T(4,128)S(1)}, f32[1,64,4,128]{3,2,1,0:T(4,128)S(1)}, u32[]{:S(2)}, u32[]{:S(2)}) collective-permute-start(f32[1,64,4,128]{3,2,1,0:T(4,128)S(1)} %get-tuple-element.56), channel_id=1, source_target_pairs={{0,1},{1,2},{2,3},{3,4},{4,5},{5,6},{6,7},{8,9},{9,10},{10,11},{11... | collective-permute-start | bytes 393224 | tf_op jit(solution)/shard_map/ppermute | solution.py:84
  120.2 1.9 %multiply_reduce_fusion = (f32[]{:T(128)}, f32[64,16,128]{2,1,0:T(8,128)}) fusion(f32[64,18,128]{2,1,0:T(8,128)S(1)} %fusion.12, f32[1,16,2,2,16,128]{5,4,3,2,1,0:T(8,128)S(1)} %copy.52), kind=kLoop, calls=%fused_computation.344 | loop fusion | flops 1441791 | bytes 3407876 | tf_op jit(solution)/shard_map/reduce_sum | solution.py:196
  122.1 1.2 broadcast_in_dim.78
  123.3 9.1 %all-to-all-start.3 = ((f32[8,1,128]{2,1,0:T(1,128)}), f32[8,1,128]{2,1,0:T(1,128)S(1)}, u32[]{:S(2)}, u32[]{:S(2)}) async-start(f32[8,1,128]{2,1,0:T(1,128)} %broadcast_in_dim.78), calls=%async_computation.3 | async-start | bytes 8192 | tf_op jit(solution)/shard_map/all_to_all | solution.py:198
  133.1 4.3 %all-to-all-done.3 = f32[8,1,128]{2,1,0:T(1,128)S(1)} async-done(((f32[8,1,128]{2,1,0:T(1,128)}), f32[8,1,128]{2,1,0:T(1,128)S(1)}, u32[]{:S(2)}, u32[]{:S(2)}) %all-to-all-start.3) | async-done | bytes 4128 | tf_op jit(solution)/shard_map/all_to_all | solution.py:198
  138.7 4.6 %fusion.111 = (f32[1,64,16,128]{3,2,1,0:T(8,128)}, f32[64,16,128]{2,1,0:T(8,128)S(1)}, f32[64,16,128]{2,1,0:T(8,128)S(1)}) fusion(f32[1,64,16,128]{3,2,1,0:T(8,128)S(1)} %bitcast.105, f32[1,64,16,128]{3,2,1,0:T(8,128)S(1)} %get-tuple-element.30, f32[1,64,16,128]{3,2,1,0:T(8,128)S(1)} %bitcast.109, f32[1,64,16,128]{3,2,1,0:T(8,128)S(1)} %multiply_add_fusion, ...), kind=kLoop, calls=%fused_computation.248 | loop fusion | flops 9830400 | bytes 5505356 | tf_op jit(solution)/shard_map/add | solution.py:203
  (70 shorter events, 9.1 us)
Async XLA Ops:
  1.4 12.8 %copy-start = (f32[1,64,16,128]{3,2,1,0:T(8,128)S(1)}, f32[1,64,16,128]{3,2,1,0:T(8,128)}, u32[]{:S(2)}) copy-start(f32[1,64,16,128]{3,2,1,0:T(8,128)} %param.19) | copy-start | bytes 1572868
  1.4 12.9 %copy-start.1 = (f32[1,64,16,128]{3,2,1,0:T(8,128)S(1)}, f32[1,64,16,128]{3,2,1,0:T(8,128)}, u32[]{:S(2)}) copy-start(f32[1,64,16,128]{3,2,1,0:T(8,128)} %param.21) | copy-start | bytes 1572868
  2.5 17.1 %copy-start.6 = (s32[16,2,4]{0,2,1:T(4,128)S(1)}, s32[16,2,4]{0,2,1:T(4,128)}, u32[]{:S(2)}) copy-start(s32[16,2,4]{0,2,1:T(4,128)} %param.26) | copy-start | bytes 1540
  2.5 17.3 %copy-start.5 = (f32[1,3]{1,0:T(1,128)S(1)}, f32[1,3]{1,0:T(1,128)}, u32[]{:S(2)}) copy-start(f32[1,3]{1,0:T(1,128)} %param.30) | copy-start | bytes 40
  2.5 17.9 %copy-start.9 = (f32[1,2,128]{2,1,0:T(2,128)S(1)}, f32[1,2,128]{2,1,0:T(2,128)}, u32[]{:S(2)}) copy-start(f32[1,2,128]{2,1,0:T(2,128)} %param.31) | copy-start | bytes 3076
  2.5 17.9 %copy-start.7 = (s32[1,128]{1,0:T(1,128)S(1)}, s32[1,128]{1,0:T(1,128)}, u32[]{:S(2)}) copy-start(s32[1,128]{1,0:T(1,128)} %param.29) | copy-start | bytes 1540
  2.5 38.8 %all-to-all-start = ((f32[16,4,2,16,128]{4,3,2,1,0:T(8,128)}), f32[16,4,2,16,128]{4,3,2,1,0:T(8,128)S(1)}, u32[]{:S(2)}, u32[]{:S(2)}) async-start(f32[16,4,2,16,128]{4,3,2,1,0:T(8,128)} %broadcast_in_dim.71), calls=%async_computation | async-start | bytes 2097152 | tf_op jit(solution)/shard_map/all_to_all | solution.py:76
  14.4 30.3 %collective-permute-start.1 = (f32[2,1,64,4,128]{4,3,2,1,0:T(4,128)S(1)}, f32[2,1,64,4,128]{4,3,2,1,0:T(4,128)S(1)}, u32[]{:S(2)}, u32[]{:S(2)}) collective-permute-start(f32[2,1,64,4,128]{4,3,2,1,0:T(4,128)S(1)} %get-tuple-element.44), channel_id=1, source_target_pairs={{0,1},{1,2},{2,3},{3,4},{4,5},{5,6},{6,7},{8,9},{9,10},{10,11},{11... | collective-permute-start | bytes 786440 | tf_op jit(solution)/shard_map/ppermute | solution.py:84
  17.6 27.1 %collective-permute-start.2 = (f32[2,1,64,4,128]{4,3,2,1,0:T(4,128)S(1)}, f32[2,1,64,4,128]{4,3,2,1,0:T(4,128)S(1)}, u32[]{:S(2)}, u32[]{:S(2)}) collective-permute-start(f32[2,1,64,4,128]{4,3,2,1,0:T(4,128)S(1)} %get-tuple-element.45), channel_id=1, source_target_pairs={{1,0},{2,1},{3,2},{4,3},{5,4},{6,5},{7,6},{9,8},{10,9},{11,10},{12... | collective-permute-start | bytes 786440 | tf_op jit(solution)/shard_map/ppermute | solution.py:87
  41.3 5.0 %collective-permute-start = (f32[16,4,2,16,128]{4,3,2,1,0:T(8,128)S(1)}, f32[16,4,2,16,128]{4,3,2,1,0:T(8,128)}, u32[]{:S(2)}, u32[]{:S(2)}) collective-permute-start(f32[16,4,2,16,128]{4,3,2,1,0:T(8,128)S(1)} %all-to-all-done), channel_id=1, source_target_pairs={{0,8},{8,0},{1,9},{9,1},{2,10},{10,2},{3,11},{11,3},{4,12},{12,4},... | collective-permute-start | bytes 3145736 | tf_op jit(solution)/shard_map/ppermute | solution.py:68
  49.0 1.0 copy-start.4
  52.7 6.6 %collective-permute-start.3 = (f32[1,64,4,128]{3,2,1,0:T(4,128)S(1)}, f32[1,64,4,128]{3,2,1,0:T(4,128)S(1)}, u32[]{:S(2)}, u32[]{:S(2)}) collective-permute-start(f32[1,64,4,128]{3,2,1,0:T(4,128)S(1)} %get-tuple-element.59), channel_id=1, source_target_pairs={{1,0},{2,1},{3,2},{4,3},{5,4},{6,5},{7,6},{9,8},{10,9},{11,10},{12... | collective-permute-start | bytes 393224 | tf_op jit(solution)/shard_map/ppermute | solution.py:87
  54.0 6.2 %collective-permute-start.4 = (f32[1,64,4,128]{3,2,1,0:T(4,128)S(1)}, f32[1,64,4,128]{3,2,1,0:T(4,128)S(1)}, u32[]{:S(2)}, u32[]{:S(2)}) collective-permute-start(f32[1,64,4,128]{3,2,1,0:T(4,128)S(1)} %get-tuple-element.58), channel_id=1, source_target_pairs={{0,1},{1,2},{2,3},{3,4},{4,5},{5,6},{6,7},{8,9},{9,10},{10,11},{11... | collective-permute-start | bytes 393224 | tf_op jit(solution)/shard_map/ppermute | solution.py:84
  60.8 3.0 %copy-start.2 = (f32[1,64,16,128]{3,2,1,0:T(8,128)S(1)}, f32[1,64,16,128]{3,2,1,0:T(8,128)}, u32[]{:S(2)}) copy-start(f32[1,64,16,128]{3,2,1,0:T(8,128)} %param.21) | copy-start | bytes 1572868
  60.8 3.0 %copy-start.8 = (f32[1,64,16,128]{3,2,1,0:T(8,128)S(1)}, f32[1,64,16,128]{3,2,1,0:T(8,128)}, u32[]{:S(2)}) copy-start(f32[1,64,16,128]{3,2,1,0:T(8,128)} %param.20) | copy-start | bytes 1572868
  65.6 35.0 %copy-start.3 = (f32[1,16,2,2,16,128]{5,4,3,0,1,2:T(8,128)S(1)}, f32[1,16,2,2,16,128]{5,4,3,0,1,2:T(8,128)}, u32[]{:S(2)}) copy-start(f32[1,16,2,2,16,128]{5,4,3,0,1,2:T(8,128)} %get-tuple-element.36) | copy-start | bytes 1572868
  65.6 2.8 %collective-permute-start.5 = (f32[16,2,16,128]{3,2,1,0:T(8,128)S(1)}, f32[16,2,16,128]{3,2,1,0:T(8,128)S(1)}, u32[]{:S(2)}, u32[]{:S(2)}) collective-permute-start(f32[16,2,16,128]{3,2,1,0:T(8,128)S(1)} %select_bitcast_fusion.4), channel_id=1, source_target_pairs={{0,8},{8,0},{1,9},{9,1},{2,10},{10,2},{3,11},{11,3},{4,12},{12,4},... | collective-permute-start | bytes 786440 | tf_op jit(solution)/shard_map/ppermute | solution.py:181
  97.5 9.2 %collective-permute-start.6 = (f32[16,2,16,128]{3,2,1,0:T(8,128)S(1)}, f32[16,2,16,128]{3,2,1,0:T(8,128)}, u32[]{:S(2)}, u32[]{:S(2)}) collective-permute-start(f32[16,2,16,128]{3,2,1,0:T(8,128)S(1)} %all_to_all.21), channel_id=1, source_target_pairs={{0,8},{8,0},{1,9},{9,1},{2,10},{10,2},{3,11},{11,3},{4,12},{12,4},... | collective-permute-start | bytes 786440 | tf_op jit(solution)/shard_map/ppermute | solution.py:68
  100.7 18.7 %collective-permute-start.10 = (f32[64,1,128]{2,1,0:T(1,128)S(1)}, f32[64,1,128]{2,1,0:T(1,128)S(1)}, u32[]{:S(2)}, u32[]{:S(2)}) collective-permute-start(f32[64,1,128]{2,1,0:T(1,128)S(1)} %get-tuple-element.51), channel_id=1, source_target_pairs={{1,0},{2,1},{3,2},{4,3},{5,4},{6,5},{7,6},{9,8},{10,9},{11,10},{12... | collective-permute-start | bytes 98312 | tf_op jit(solution)/shard_map/ppermute | solution.py:87
  102.0 17.4 %collective-permute-start.9 = (f32[64,1,128]{2,1,0:T(1,128)S(1)}, f32[64,1,128]{2,1,0:T(1,128)S(1)}, u32[]{:S(2)}, u32[]{:S(2)}) collective-permute-start(f32[64,1,128]{2,1,0:T(1,128)S(1)} %get-tuple-element.50), channel_id=1, source_target_pairs={{0,1},{1,2},{2,3},{3,4},{4,5},{5,6},{6,7},{8,9},{9,10},{10,11},{11... | collective-permute-start | bytes 98312 | tf_op jit(solution)/shard_map/ppermute | solution.py:84
  107.8 6.0 %collective-permute-start.7 = (f32[64,2,128]{2,1,0:T(2,128)S(1)}, f32[64,2,128]{2,1,0:T(2,128)S(1)}, u32[]{:S(2)}, u32[]{:S(2)}) collective-permute-start(f32[64,2,128]{2,1,0:T(2,128)S(1)} %get-tuple-element.52), channel_id=1, source_target_pairs={{0,1},{1,2},{2,3},{3,4},{4,5},{5,6},{6,7},{8,9},{9,10},{10,11},{11... | collective-permute-start | bytes 196616 | tf_op jit(solution)/shard_map/ppermute | solution.py:84
  111.2 8.1 %collective-permute-start.8 = (f32[64,2,128]{2,1,0:T(2,128)S(1)}, f32[64,2,128]{2,1,0:T(2,128)S(1)}, u32[]{:S(2)}, u32[]{:S(2)}) collective-permute-start(f32[64,2,128]{2,1,0:T(2,128)S(1)} %get-tuple-element.53), channel_id=1, source_target_pairs={{1,0},{2,1},{3,2},{4,3},{5,4},{6,5},{7,6},{9,8},{10,9},{11,10},{12... | collective-permute-start | bytes 196616 | tf_op jit(solution)/shard_map/ppermute | solution.py:87
  112.5 19.9 %collective-permute-start.11 = (f32[1,64,4,128]{3,2,1,0:T(4,128)S(1)}, f32[1,64,4,128]{3,2,1,0:T(4,128)S(1)}, u32[]{:S(2)}, u32[]{:S(2)}) collective-permute-start(f32[1,64,4,128]{3,2,1,0:T(4,128)S(1)} %get-tuple-element.57), channel_id=1, source_target_pairs={{1,0},{2,1},{3,2},{4,3},{5,4},{6,5},{7,6},{9,8},{10,9},{11,10},{12... | collective-permute-start | bytes 393224 | tf_op jit(solution)/shard_map/ppermute | solution.py:87
  113.8 18.6 %collective-permute-start.12 = (f32[1,64,4,128]{3,2,1,0:T(4,128)S(1)}, f32[1,64,4,128]{3,2,1,0:T(4,128)S(1)}, u32[]{:S(2)}, u32[]{:S(2)}) collective-permute-start(f32[1,64,4,128]{3,2,1,0:T(4,128)S(1)} %get-tuple-element.56), channel_id=1, source_target_pairs={{0,1},{1,2},{2,3},{3,4},{4,5},{5,6},{6,7},{8,9},{9,10},{10,11},{11... | collective-permute-start | bytes 393224 | tf_op jit(solution)/shard_map/ppermute | solution.py:84
  123.3 14.1 %all-to-all-start.3 = ((f32[8,1,128]{2,1,0:T(1,128)}), f32[8,1,128]{2,1,0:T(1,128)S(1)}, u32[]{:S(2)}, u32[]{:S(2)}) async-start(f32[8,1,128]{2,1,0:T(1,128)} %broadcast_in_dim.78), calls=%async_computation.3 | async-start | bytes 8192 | tf_op jit(solution)/shard_map/all_to_all | solution.py:198

commit v2 on v1

v2 whole, which is shorter than its diff:
```python
import jax
import jax.numpy as jnp
from jax import lax
from jax.experimental import pallas as pl
from jax.experimental.pallas import tpu as pltpu
from jax.sharding import PartitionSpec as P


second_coef = (-205.0 / 72.0, 8.0 / 5.0, -1.0 / 5.0, 8.0 / 315.0, -1.0 / 560.0)
first_coef = (0.8, -0.2, 4.0 / 105.0, -1.0 / 280.0)

SHOT = ("xh", "z", "core")
DEPTH = ("xl", "y")
PEERS = ("xh", "z")
SWAP = [(0, 1), (1, 0)]
REACH = 4
VMEM_LIMIT = 16 * 2**20
MID = 8
CHUNK = 4
VMEM = pl.BlockSpec(memory_space=pltpu.VMEM)
SMEM = pl.BlockSpec(memory_space=pltpu.SMEM)


def f32(*shape):
    return jax.ShapeDtypeStruct(shape, jnp.float32)


def call(kernel, args, smem, outs, scratch=(), flops=0):
    bytes_accessed = 4 * sum(a.size for a in args)
    return pl.pallas_call(
        kernel,
        out_shape=outs,
        in_specs=[SMEM if i < smem else VMEM for i in range(len(args))],
        out_specs=jax.tree.map(lambda _: VMEM, outs),
        scratch_shapes=list(scratch),
        cost_estimate=pl.CostEstimate(
            flops=flops, bytes_accessed=bytes_accessed, transcendentals=0
        ),
        compiler_params=pltpu.CompilerParams(vmem_limit_bytes=VMEM_LIMIT),
    )(*args)


def fill_padded(pad, read, low, high):
    cells_x, cells_z = pad.shape[0] - 2 * REACH, pad.shape[1] - 2 * MID
    zeros = jnp.zeros((REACH, *pad.shape[1:]), jnp.float32)
    pad[pl.ds(0, REACH)] = zeros
    pad[pl.ds(REACH + cells_x, REACH)] = zeros

    @pl.loop(0, cells_x // CHUNK)
    def _(step):
        x = step * CHUNK
        to = pl.ds(REACH + x, CHUNK)
        pad[to, pl.ds(MID, cells_z), :] = read(x)
        pad[to, pl.ds(MID - REACH, REACH), :] = low(x)
        pad[to, pl.ds(MID + cells_z, REACH), :] = high(x)


def depth_pass(pad, first_z, second_z):
    cells_x, cells_z = second_z.shape[0], second_z.shape[1]
    zeros = jnp.zeros((REACH, *first_z.shape[1:]), jnp.float32)
    first_z[pl.ds(0, REACH)] = zeros
    first_z[pl.ds(REACH + cells_x, REACH)] = zeros

    @pl.loop(0, cells_x // CHUNK)
    def _(step):
        x = step * CHUNK
        at = lambda k: pad[pl.ds(REACH + x, CHUNK), pl.ds(MID + k, cells_z), :]
        two = second_coef[0] * at(0)
        one = None
        for k in range(1, 5):
            above, below = at(k), at(-k)
            two = two + second_coef[k] * (above + below)
            term = first_coef[k - 1] * (above - below)
            one = term if one is None else one + term
        second_z[pl.ds(x, CHUNK)] = two
        first_z[pl.ds(REACH + x, CHUNK)] = one


def lateral_masks(cells_y):
    lane = lax.broadcasted_iota(jnp.int32, (1, 8, cells_y), 2)
    up = [jnp.where(lane < cells_y - k, second_coef[k], 0.0) for k in range(1, 5)]
    down = [jnp.where(lane >= k, second_coef[k], 0.0) for k in range(1, 5)]
    return up, down


def lateral(pad, x, masks, cells_z):
    up, down = masks
    at = lambda k: pad[pl.ds(REACH + x + k, CHUNK), pl.ds(MID, cells_z), :]
    v = at(0)
    cells_y = v.shape[2]
    total = (2.0 * second_coef[0]) * v
    for k in range(1, 5):
        total = total + second_coef[k] * (at(k) + at(-k))
    flat = v.reshape(CHUNK * cells_z // 8, 8, cells_y)
    along_y = None
    for k in range(1, 5):
        term = up[k - 1] * pltpu.roll(flat, cells_y - k, 2) + down[k - 1] * pltpu.roll(flat, k, 2)
        along_y = term if along_y is None else along_y + term
    return total + along_y.reshape(v.shape)


def crossing(first_z, x):
    at = lambda k: first_z[pl.ds(REACH + x + k, CHUNK)]
    total = None
    for k in range(1, 5):
        term = first_coef[k - 1] * (at(k) - at(-k))
        total = term if total is None else total + term
    return total


def add_at(ref, cell, amount, z_start, depth_cells):
    cells_z, cells_y = ref.shape[1], ref.shape[2]
    row = cell // cells_y
    x, z = row // depth_cells, row % depth_cells - z_start

    @pl.when((z >= 0) & (z < cells_z))
    def _():
        lane = lax.broadcasted_iota(jnp.int32, (1, 1, cells_y), 2)
        at = (pl.ds(x, 1), pl.ds(z, 1), slice(None))
        ref[at] = ref[at] + jnp.where(lane == cell % cells_y, amount, 0.0)


def spread_kernel(model, aniso_h, aniso_c, smooth, out):
    for j, ref in enumerate((model, aniso_h, aniso_c, smooth)):
        block = ref[...]
        for peer in range(out.shape[0]):
            out[peer, j] = block


def land_kernel(low, high, low_out, high_out):
    low_out[...] = low[...]
    high_out[...] = high[...]


def open_kernel(
    place, src_cell, src_wave, rec_cell, rec_data, onehot, shot_group,
    u_prev, u_cur, a_prev, a_cur, low, high,
    base_u, lat_u, dep_u, cross_u, base_a, lat_a, dep_a, cross_a, weight,
    pad, first_z,
):
    cells_x, cells_z, cells_y = lat_u.shape
    masks = lateral_masks(cells_y)
    sides = ((u_prev, u_cur, base_u, lat_u, dep_u, cross_u),
             (a_prev, a_cur, base_a, lat_a, dep_a, cross_a))
    for j, (old, now, base, lat, dep, cross) in enumerate(sides):
        fill_padded(
            pad,
            lambda x, now=now: now[0, pl.ds(x, CHUNK)],
            lambda x, j=j: low[j, pl.ds(x, CHUNK)],
            lambda x, j=j: high[j, pl.ds(x, CHUNK)],
        )
        depth_pass(pad, first_z, dep)

        @pl.loop(0, cells_x // CHUNK)
        def _(step, old=old, now=now, base=base, lat=lat, cross=cross):
            x = step * CHUNK
            rows = pl.ds(x, CHUNK)
            lat[rows] = lateral(pad, x, masks, cells_z)
            cross[rows] = crossing(first_z, x)
            base[rows] = 2.0 * now[0, rows] - old[0, rows]

    z_start, depth_cells = place[0], place[1]
    add_at(base_u, src_cell[0], src_wave[0, 0], z_start, depth_cells)

    @pl.loop(0, rec_cell.shape[1])
    def _(r):
        add_at(base_a, rec_cell[0, r], rec_data[0, 0, r], z_start, depth_cells)

    blocks = onehot.shape[1]
    position = lax.broadcasted_iota(jnp.int32, weight.shape, 1)
    value = jnp.zeros(weight.shape, jnp.float32)
    for block in range(blocks):
        scale = sum(
            onehot[shot_group[0], block, b].astype(jnp.float32) * 2.0 ** (-b)
            for b in range(onehot.shape[2])
        )
        value = jnp.where(position // (cells_z // blocks) == block, scale, value)
    weight[...] = value


def first_kernel(
    place, mine, other, a_cur,
    base_u, lat_u, dep_u, cross_u, base_a, lat_a, dep_a, cross_a,
    u_one, a_one, grad, model, aniso_h, aniso_c, smooth, low, high,
):
    cells_x, cells_z, _ = u_one.shape
    own = place[2] == 0

    @pl.loop(0, mine.shape[0])
    def _(q):
        for p in range(2):
            rows = pl.ds(q * 4 + p * 2, 2)
            pick = lambda j: jnp.where(own == (p == 0), mine[q, j], other[q, j])
            m, h, c, s = pick(0), pick(1), pick(2), pick(3)
            model[rows], aniso_h[rows], aniso_c[rows], smooth[rows] = m, h, c, s
            k_u = h * lat_u[rows] + dep_u[rows] + c * cross_u[rows]
            k_a = h * lat_a[rows] + dep_a[rows] + c * cross_a[rows]
            grad[rows] = a_cur[0, rows] * k_u
            new = base_u[rows] + m * k_u
            u_one[rows] = new
            a_one[rows] = base_a[rows] + m * k_a
            low[rows] = new[:, :REACH]
            high[rows] = new[:, cells_z - REACH :]
            edge = (pl.ds(cells_x + q, 1), pl.ds(2 * p, 2), slice(None))
            low[edge] = s[:, 0][None]
            high[edge] = s[:, cells_z - 1][None]


def second_kernel(
    place, src_cell, src_wave,
    u_one, u_cur, a_one, grad, weight, model, aniso_h, aniso_c, low, high,
    u_two, keep, send, pad, first_z, dep,
):
    cells_x, cells_z, cells_y = u_two.shape
    masks = lateral_masks(cells_y)
    fill_padded(
        pad,
        lambda x: u_one[pl.ds(x, CHUNK)],
        lambda x: low[pl.ds(x, CHUNK)],
        lambda x: high[pl.ds(x, CHUNK)],
    )
    depth_pass(pad, first_z, dep)
    own = place[2] == 0

    @pl.loop(0, cells_x // CHUNK)
    def _(step):
        x = step * CHUNK
        rows = pl.ds(x, CHUNK)
        k_u = (
            aniso_h[rows] * lateral(pad, x, masks, cells_z)
            + dep[rows]
            + aniso_c[rows] * crossing(first_z, x)
        )
        u_two[rows] = 2.0 * u_one[rows] - u_cur[0, rows] + model[rows] * k_u
        total = weight[...] * (grad[rows] + a_one[rows] * k_u)
        keep[step] = jnp.where(own, total[:2], total[2:])
        send[step] = jnp.where(own, total[2:], total[:2])

    add_at(u_two, src_cell[0], src_wave[0, 1], place[0], place[1])


def sum_kernel(parts, out):
    total = parts[0]
    for peer in range(1, parts.shape[0]):
        total = total + parts[peer]
    for peer in range(parts.shape[0]):
        out[peer] = total


def join_kernel(place, mine, other, u_two, summed, low, high):
    cells_x, cells_z, _ = summed.shape
    own = place[2] == 0

    @pl.loop(0, mine.shape[0])
    def _(q):
        for p in range(2):
            rows = pl.ds(q * 4 + p * 2, 2)
            g = jnp.where(own == (p == 0), mine[q], other[q])
            summed[rows] = g
            low[rows] = u_two[rows, :REACH]
            high[rows] = u_two[rows, cells_z - REACH :]
            for r in range(2):
                edge = (pl.ds(cells_x + 2 * q + p, 1), pl.ds(2 * r, 2), slice(None))
                low[edge] = g[r, :2][None]
                high[edge] = g[r, cells_z - 2 :][None]


SM = 16


def relax_kernel(summed, smooth, low_g, high_g, low_s, high_s, out, square, wide, once, coef):
    cells_x, cells_z, cells_y = summed.shape
    tall = wide.shape[1]
    zero_row = jnp.zeros((1, tall, cells_y), jnp.float32)
    for ref in (wide, once):
        ref[pl.ds(0, 1)] = zero_row
        ref[pl.ds(cells_x + 1, 1)] = zero_row

    @pl.loop(0, cells_x // CHUNK)
    def _(q):
        for ref, shift in ((wide, 1), (coef, 0)):
            zero = jnp.zeros((CHUNK, 8, cells_y), jnp.float32)
            for tile in (0, 8, SM + cells_z, SM + cells_z + 8):
                ref[pl.ds(q * CHUNK + shift, CHUNK), pl.ds(tile, 8), :] = zero
        for j in range(CHUNK):
            x = q * CHUNK + j
            halo = (pl.ds(cells_x + 2 * q + j // 2, 1), pl.ds(2 * (j % 2), 2), slice(None))
            wide[pl.ds(x + 1, 1), pl.ds(SM, cells_z), :] = summed[pl.ds(x, 1)]
            wide[pl.ds(x + 1, 1), pl.ds(SM - 2, 2), :] = low_g[halo]
            wide[pl.ds(x + 1, 1), pl.ds(SM + cells_z, 2), :] = high_g[halo]
            edge = (pl.ds(cells_x + q, 1), pl.ds(j, 1), slice(None))
            coef[pl.ds(x, 1), pl.ds(SM, cells_z), :] = smooth[pl.ds(x, 1)]
            coef[pl.ds(x, 1), pl.ds(SM - 1, 1), :] = low_s[edge]
            coef[pl.ds(x, 1), pl.ds(SM + cells_z, 1), :] = high_s[edge]

    lane = lax.broadcasted_iota(jnp.int32, (1, 8, cells_y), 2)

    def relaxed(ref, x, start, count, factor):
        at = lambda dx, dz: ref[pl.ds(x + 1 + dx, CHUNK), pl.ds(start + dz, count), :]
        v = at(0, 0)
        near = at(1, 0) + at(-1, 0) + at(0, 1) + at(0, -1)
        flat = v.reshape(CHUNK * count // 8, 8, cells_y)
        right = jnp.where(lane < cells_y - 1, pltpu.roll(flat, cells_y - 1, 2), 0.0)
        left = jnp.where(lane >= 1, pltpu.roll(flat, 1, 2), 0.0)
        near = near + (right + left).reshape(v.shape)
        return v + factor * (near - 6.0 * v)

    @pl.loop(0, cells_x // CHUNK)
    def _(q):
        x = q * CHUNK
        once[pl.ds(x + 1, CHUNK), pl.ds(8, cells_z + 16), :] = relaxed(
            wide, x, 8, cells_z + 16, coef[pl.ds(x, CHUNK), pl.ds(8, cells_z + 16), :]
        )

    def sweep(q, total):
        x = q * CHUNK
        value = relaxed(once, x, SM, cells_z, smooth[pl.ds(x, CHUNK)])
        out[pl.ds(x, CHUNK)] = value
        squares = (value * value).reshape(CHUNK * cells_z // 8, 8, cells_y)
        return total + jnp.sum(squares, axis=0)

    total = lax.fori_loop(0, cells_x // CHUNK, sweep, jnp.zeros((8, cells_y), jnp.float32))
    row = jnp.sum(total, axis=0, keepdims=True)
    square[...] = jnp.broadcast_to(row[None], square.shape)


def third_kernel(
    place, src_cell, src_wave, u_two, u_one, model, aniso_h, aniso_c, low, high,
    base, change, pad, first_z, dep,
):
    cells_x, cells_z, cells_y = base.shape
    masks = lateral_masks(cells_y)
    fill_padded(
        pad,
        lambda x: u_two[pl.ds(x, CHUNK)],
        lambda x: low[pl.ds(x, CHUNK)],
        lambda x: high[pl.ds(x, CHUNK)],
    )
    depth_pass(pad, first_z, dep)

    @pl.loop(0, cells_x // CHUNK)
    def _(step):
        x = step * CHUNK
        rows = pl.ds(x, CHUNK)
        k_u = (
            aniso_h[rows] * lateral(pad, x, masks, cells_z)
            + dep[rows]
            + aniso_c[rows] * crossing(first_z, x)
        )
        base[rows] = 2.0 * u_two[rows] - u_one[rows]
        change[rows] = model[rows] * k_u

    add_at(base, src_cell[0], src_wave[0, 2], place[0], place[1])


def close_kernel(place, squares, smoothed, model, base, change, model_next, grad_dir, wave_next):
    cells_x, cells_z, cells_y = smoothed.shape
    rows = grad_dir.shape[0]
    total = jnp.sum(jnp.sum(squares[...], axis=0), axis=1, keepdims=True)
    cells = (cells_x * place[1] * cells_y).astype(jnp.float32)
    scale = lax.rsqrt(total / cells + 1e-06)
    scale = jnp.broadcast_to(scale, (8, cells_y))[None]

    def factor(value):
        flat = value.reshape(value.shape[0] * cells_z // 8, 8, cells_y) * scale
        return flat.reshape(value.shape)

    @pl.loop(0, cells_x // CHUNK)
    def _(step):
        at = pl.ds(step * CHUNK, CHUNK)
        shrink = 1.0 - 0.25 * jnp.tanh(factor(smoothed[at]))
        wave_next[0, at] = base[at] + change[at] * shrink

    at = pl.ds(place[3], rows)
    direction = factor(smoothed[at])
    grad_dir[...] = direction
    model_next[...] = model[at] * (1.0 - 0.25 * jnp.tanh(direction))


def shift(low_edge, high_edge):
    count = lax.axis_size(DEPTH)
    forward = [(i, i + 1) for i in range(count - 1)]
    backward = [(target, source) for source, target in forward]
    return lax.ppermute(high_edge, DEPTH, forward), lax.ppermute(low_edge, DEPTH, backward)


def body(
    u_prev,
    u_cur,
    a_prev,
    a_cur,
    model,
    aniso_h,
    aniso_c,
    smooth_coef,
    bin_onehot,
    shot_group,
    src_cell,
    rec_cell,
    src_wave,
    rec_data,
):
    _, cells_x, cells_z, cells_y = u_cur.shape
    rows = model.shape[0]
    peers = lax.axis_size(PEERS)
    slab = f32(cells_x, cells_z, cells_y)
    depth_cells = cells_z * lax.axis_size(DEPTH)
    place = jnp.stack(
        [
            lax.axis_index(DEPTH) * cells_z,
            jnp.int32(depth_cells),
            lax.axis_index("core"),
            lax.axis_index(SHOT) * rows,
        ]
    )
    pad = pltpu.VMEM((cells_x + 2 * REACH, cells_z + 2 * MID, cells_y), jnp.float32)
    first_z = pltpu.VMEM((cells_x + 2 * REACH, cells_z, cells_y), jnp.float32)
    dep = pltpu.VMEM((cells_x, cells_z, cells_y), jnp.float32)
    work = 80 * cells_x * cells_z * cells_y

    spread = call(
        spread_kernel,
        (model, aniso_h, aniso_c, smooth_coef),
        0,
        f32(peers, 4, rows, cells_z, cells_y),
    )
    mine = lax.all_to_all(spread, PEERS, 0, 0, tiled=True)

    edges = lambda start: jnp.concatenate(
        [lax.slice_in_dim(v, start, start + REACH, axis=2) for v in (u_cur, a_cur)]
    )
    low, high = shift(edges(0), edges(cells_z - REACH))
    low, high = call(land_kernel, (low, high), 0, (f32(*low.shape), f32(*high.shape)))
    *parts, weight = call(
        open_kernel,
        (place, src_cell, src_wave, rec_cell, rec_data, bin_onehot, shot_group)
        + (u_prev, u_cur, a_prev, a_cur, low, high),
        7,
        (slab,) * 8 + (f32(1, cells_z, cells_y),),
        (pad, first_z),
        2 * work,
    )
    other = lax.ppermute(mine, "core", SWAP)
    payload = f32(cells_x + peers, REACH, cells_y)
    u_one, a_one, grad, model_slab, h_slab, c_slab, smooth_slab, low_edge, high_edge = call(
        first_kernel,
        (place, mine, other, a_cur, *parts),
        1,
        (slab,) * 7 + (payload, payload),
        (),
        20 * slab.size,
    )
    low_one, high_one = shift(low_edge, high_edge)
    split = f32(peers, rows, cells_z, cells_y)
    u_two, keep, send = call(
        second_kernel,
        (place, src_cell, src_wave)
        + (u_one, u_cur, a_one, grad, weight, model_slab, h_slab, c_slab, low_one, high_one),
        3,
        (slab, split, split),
        (pad, first_z, dep),
        work,
    )
    chip_sum = keep + lax.ppermute(send, "core", SWAP)
    shares = lax.all_to_all(chip_sum, PEERS, 0, 0, tiled=True)
    total = call(sum_kernel, (shares,), 0, split)
    mine = lax.all_to_all(total, PEERS, 0, 0, tiled=True)
    other = lax.ppermute(mine, "core", SWAP)
    payload = f32(cells_x + 2 * peers, REACH, cells_y)
    summed, low_edge, high_edge = call(
        join_kernel, (place, mine, other, u_two), 1, (slab, payload, payload)
    )
    low_two, high_two = shift(low_edge, high_edge)
    tall = cells_z + 2 * SM
    smoothed, square = call(
        relax_kernel,
        (summed, smooth_slab, low_two, high_two, low_one, high_one),
        0,
        (slab, f32(lax.axis_size(DEPTH), 1, cells_y)),
        (
            pltpu.VMEM((cells_x + 2, tall, cells_y), jnp.float32),
            pltpu.VMEM((cells_x + 2, tall, cells_y), jnp.float32),
            pltpu.VMEM((cells_x, tall, cells_y), jnp.float32),
        ),
        40 * slab.size,
    )
    squares = lax.all_to_all(square, DEPTH, 0, 0, tiled=True)
    base, change = call(
        third_kernel,
        (place, src_cell, src_wave)
        + (u_two, u_one, model_slab, h_slab, c_slab, low_two, high_two),
        3,
        (slab, slab),
        (pad, first_z, dep),
        work,
    )
    share = f32(rows, cells_z, cells_y)
    return call(
        close_kernel,
        (place, squares, smoothed, model_slab, base, change),
        1,
        (share, share, f32(1, cells_x, cells_z, cells_y)),
        (),
        20 * slab.size,
    )


def solution(mesh):
    mesh = jax.sharding.Mesh(
        mesh.devices.reshape(2, 8, 2, 2, 4), ("xh", "z", "core", "xl", "y")
    )
    return jax.shard_map(
        body,
        mesh=mesh,
        in_specs=(
            P(SHOT, None, DEPTH, None),
            P(SHOT, None, DEPTH, None),
            P(SHOT, None, DEPTH, None),
            P(SHOT, None, DEPTH, None),
            P(SHOT, DEPTH, None),
            P(SHOT, DEPTH, None),
            P(SHOT, DEPTH, None),
            P(SHOT, DEPTH, None),
            P(None, DEPTH, None),
            P(SHOT),
            P(SHOT),
            P(SHOT, None),
            P(SHOT, None),
            P(SHOT, None, None),
        ),
        out_specs=(
            P(SHOT, DEPTH, None),
            P(SHOT, DEPTH, None),
            P(SHOT, None, DEPTH, None),
        ),
        check_vma=False,
    )
```

time: 146 us -> 160 us (1.096)
  blocking collectives: 29 us -> 67.2 us
  Pallas kernels: 0 us -> 28.2 us
  starting transfers between devices: 55.2 us -> 29 us
  other arithmetic: 19.9 us -> 1.63 us
  waiting for transfers between devices: 28.7 us -> 20.7 us
  local copies, waits for them, and re-layouts: 6.17 us -> 9.27 us
  matrix products: 1.86 us -> 0 us
    all_to_all x2 -> x3, blocking collectives: 29 us -> 67.2 us  [the longest x1 38 us: body(): mine = lax.all_to_all(spread, PEERS, 0, 0, tiled=True)]
    pallas_call x0 -> x10, Pallas kernels: none -> 28.2 us  [call(): pl.pallas_call(kernel, out_shape=outs, in_specs=[SMEM if i < smem else VM...]
    all_to_all x2 -> x1, waiting for transfers between devices: 25 us -> 0.01 us  [body(): squares = lax.all_to_all(square, DEPTH, 0, 0, tiled=True)]
    ppermute x12 -> x8, waiting for transfers between devices: 2.55 us -> 19.6 us  [the longest x3 12.5 us: shift(): lax.ppermute(low_edge, DEPTH, backward)]
    all_to_all x2 -> x1, starting transfers between devices: 20.8 us -> 6.13 us  [body(): squares = lax.all_to_all(square, DEPTH, 0, 0, tiled=True)]
    ppermute x12 -> x8, starting transfers between devices: 32.8 us -> 20.2 us  [the longest x3 10.4 us: shift(): lax.ppermute(high_edge, DEPTH, forward)]
    add x7 -> x0, other arithmetic: 12 us -> none  [the longest x2 5.56 us: body(): 2.0 * wave - wave_old + model_slab * applied + source_term(step_index)]
    unnamed x20 -> x45, local copies, waits for them, and re-layouts: 0.95 us -> 9.17 us
  transfers between devices with their start and end apart: 15 -> 10, of which waited for: 6 -> 8; matrix products, arithmetic and copies ran while one was open for 6% -> 1% of each run, Pallas kernels for 0% -> 10%
where the time goes in v2:
time: 160 us; the launch traced here: 158 us
  blocking collectives  67.2 us (42%)
  starting transfers between devices  29 us (18%)
  Pallas kernels  28.2 us (18%)
  waiting for transfers between devices  20.7 us (13%)
  local copies, waits for them, and re-layouts  9.27 us (6%)
  between operations  2.22 us (1%)
  other arithmetic  1.63 us (1%)
    all_to_all x1, blocking collectives, body(): mine = lax.all_to_all(spread, PEERS, 0, 0, tiled=True)  38 us
    pallas_call x10, Pallas kernels, call(): pl.pallas_call(kernel, out_shape=outs, in_specs=[SMEM if i < smem else VM...  28.2 us
    all_to_all x1, blocking collectives, body(): mine = lax.all_to_all(total, PEERS, 0, 0, tiled=True)  14.6 us
    all_to_all x1, blocking collectives, body(): shares = lax.all_to_all(chip_sum, PEERS, 0, 0, tiled=True)  14.6 us
    ppermute x3, waiting for transfers between devices, shift(): lax.ppermute(low_edge, DEPTH, backward)  12.5 us
    ppermute x3, starting transfers between devices, shift(): lax.ppermute(high_edge, DEPTH, forward)  10.4 us
    unnamed x45, local copies, waits for them, and re-layouts  9.17 us
    all_to_all x1, starting transfers between devices, body(): squares = lax.all_to_all(square, DEPTH, 0, 0, tiled=True)  6.13 us
  transfers between devices with their start and end apart: 10, of which 8 were waited for; matrix products, arithmetic and copies ran while one was open for 1% of the time, Pallas kernels for 10%

profile of v2, /device:TPU:1, one launch (start us, length us, event | category | flops | bytes accessed | tf_op | source)
XLA Modules:
  0.0 158.3 jit_solution(18388059735458982941)
XLA Ops:
  3.6 38.0 %all_to_all.20.mine = f32[16,4,2,16,128]{4,3,2,1,0:T(8,128)S(1)} all-to-all(f32[16,4,2,16,128]{4,3,2,1,0:T(8,128)S(1)} %shard_map.157), channel_id=1, replica_groups=mesh['xh'=2,'z'=8,'core'=2,'xl'=2,'y'=4] {'xh','z'}, dimensions={0} | all-to-all | bytes 2097152 | tf_op jit(solution)/shard_map/all_to_all | solution.py:427
  41.6 2.8 %collective-permute-start = (f32[16,4,2,16,128]{4,3,2,1,0:T(8,128)S(1)}, f32[16,4,2,16,128]{4,3,2,1,0:T(8,128)}, u32[]{:S(2)}, u32[]{:S(2)}) collective-permute-start(f32[16,4,2,16,128]{4,3,2,1,0:T(8,128)S(1)} %all_to_all.20.mine), channel_id=1, source_target_pairs={{0,8},{8,0},{1,9},{9,1},{2,10},{10,2},{3,11},{11,3},{4,12},{12,4},... | collective-permute-start | bytes 3145736 | tf_op jit(solution)/shard_map/ppermute | solution.py:443
  45.4 3.2 %collective-permute-start.1 = (f32[2,64,4,128]{3,2,1,0:T(4,128)}, f32[2,64,4,128]{3,2,1,0:T(4,128)S(1)}, u32[]{:S(2)}, u32[]{:S(2)}) collective-permute-start(f32[2,64,4,128]{3,2,1,0:T(4,128)} %pad_maximum_fusion), channel_id=1, source_target_pairs={{0,1},{1,2},{2,3},{3,4},{4,5},{5,6},{6,7},{8,9},{9,10},{10,11},{11... | collective-permute-start | bytes 786440 | tf_op jit(solution)/shard_map/ppermute | solution.py:384
  49.4 1.3 collective-permute-start.2
  52.1 2.4 %collective-permute-done.1.low = f32[2,64,4,128]{3,2,1,0:T(4,128)S(1)} collective-permute-done((f32[2,64,4,128]{3,2,1,0:T(4,128)}, f32[2,64,4,128]{3,2,1,0:T(4,128)S(1)}, u32[]{:S(2)}, u32[]{:S(2)}) %collective-permute-start.1) | collective-permute-done | bytes 262176 | tf_op jit(solution)/shard_map/ppermute | solution.py:384
  54.5 4.6 %collective-permute-done.2.high = f32[2,64,4,128]{3,2,1,0:T(4,128)} collective-permute-done((f32[2,64,4,128]{3,2,1,0:T(4,128)}, f32[2,64,4,128]{3,2,1,0:T(4,128)}, u32[]{:S(2)}, u32[]{:S(2)}) %collective-permute-start.2) | collective-permute-done | bytes 262176 | tf_op jit(solution)/shard_map/ppermute | solution.py:384
  59.1 1.0 shard_map.158
  60.8 11.4 %shard_map.159 = (f32[64,16,128]{2,1,0:T(8,128)S(1)}, f32[64,16,128]{2,1,0:T(8,128)S(1)}, f32[64,16,128]{2,1,0:T(8,128)S(1)}, f32[64,16,128]{2,1,0:T(8,128)S(1)}...) custom-call(s32[4]{0:T(128)S(1)} %pad_add_fusion.place, ...), custom_call_target="tpu_custom_call" | custom-call | flops 20971520 | bytes 2623524 | tf_op jit(solution)/shard_map/pallas_call | solution.py:30
  72.3 1.8 %shard_map.160 = (f32[64,16,128]{2,1,0:T(8,128)S(1)}, f32[64,16,128]{2,1,0:T(8,128)S(1)}, f32[64,16,128]{2,1,0:T(8,128)S(1)}, f32[64,16,128]{2,1,0:T(8,128)S(1)}...) custom-call(s32[4]{0:T(128)S(1)} %pad_add_fusion.place, ...), custom_call_target="tpu_custom_call" | custom-call | flops 2621440 | bytes 6815760 | tf_op jit(solution)/shard_map/pallas_call | solution.py:30
  74.1 3.2 %collective-permute-start.3 = (f32[80,4,128]{2,1,0:T(4,128)S(1)}, f32[80,4,128]{2,1,0:T(4,128)S(1)}, u32[]{:S(2)}, u32[]{:S(2)}) collective-permute-start(f32[80,4,128]{2,1,0:T(4,128)S(1)} %get-tuple-element.50), channel_id=1, source_target_pairs={{0,1},{1,2},{2,3},{3,4},{4,5},{5,6},{6,7},{8,9},{9,10},{10,11},{11... | collective-permute-start | bytes 491528 | tf_op jit(solution)/shard_map/ppermute | solution.py:384
  77.3 1.3 collective-permute-start.4
  78.6 0.9 collective-permute-done.3.low.low_s
  79.5 3.8 %collective-permute-done.4.high.high_s = f32[80,4,128]{2,1,0:T(4,128)S(1)} collective-permute-done((f32[80,4,128]{2,1,0:T(4,128)S(1)}, f32[80,4,128]{2,1,0:T(4,128)S(1)}, u32[]{:S(2)}, u32[]{:S(2)}) %collective-permute-start.4) | collective-permute-done | bytes 163872 | tf_op jit(solution)/shard_map/ppermute | solution.py:384
  83.4 3.8 %shard_map.161 = (f32[64,16,128]{2,1,0:T(8,128)S(1)}, f32[16,2,16,128]{3,2,1,0:T(8,128)S(1)}, f32[16,2,16,128]{3,2,1,0:T(8,128)S(1)}) custom-call(s32[4]{0:T(128)S(1)} %pad_add_fusion.place, s32[1]{0:T(128)S(6)} %copy.19.src_cell, f32[1,3]{1,0:T(1,128)S(1)} %copy-done.18, f32[64,16,128]{2,1,0:T(8,128)S(1)} %get-tuple-element.43.u_one, ...), custom_call_target="tpu_custom_call" | custom-call | flops 10485760 | bytes 4005920 | tf_op jit(solution)/shard_map/pallas_call | solution.py:30
  87.1 2.7 %collective-permute-start.5 = (f32[16,2,16,128]{3,2,1,0:T(8,128)S(1)}, f32[16,2,16,128]{3,2,1,0:T(8,128)S(1)}, u32[]{:S(2)}, u32[]{:S(2)}) collective-permute-start(f32[16,2,16,128]{3,2,1,0:T(8,128)S(1)} %get-tuple-element.53), channel_id=1, source_target_pairs={{0,8},{8,0},{1,9},{9,1},{2,10},{10,2},{3,11},{11,3},{4,12},{12,4},... | collective-permute-start | bytes 786440 | tf_op jit(solution)/shard_map/ppermute | solution.py:464
  89.8 1.2 collective-permute-done.5
  91.0 14.6 %all_to_all.21.parts = f32[16,2,16,128]{3,2,1,0:T(8,128)S(1)} all-to-all(f32[16,2,16,128]{3,2,1,0:T(8,128)S(1)} %add.15), channel_id=1, replica_groups=mesh['xh'=2,'z'=8,'core'=2,'xl'=2,'y'=4] {'xh','z'}, dimensions={0} | all-to-all | bytes 524288 | tf_op jit(solution)/shard_map/all_to_all | solution.py:465
  105.6 14.6 %all_to_all.22.mine = f32[16,2,16,128]{3,2,1,0:T(8,128)S(1)} all-to-all(f32[16,2,16,128]{3,2,1,0:T(8,128)S(1)} %shard_map.162), channel_id=1, replica_groups=mesh['xh'=2,'z'=8,'core'=2,'xl'=2,'y'=4] {'xh','z'}, dimensions={0} | all-to-all | bytes 524288 | tf_op jit(solution)/shard_map/all_to_all | solution.py:467
  120.3 3.1 %collective-permute-start.6 = (f32[16,2,16,128]{3,2,1,0:T(8,128)S(1)}, f32[16,2,16,128]{3,2,1,0:T(8,128)S(1)}, u32[]{:S(2)}, u32[]{:S(2)}) collective-permute-start(f32[16,2,16,128]{3,2,1,0:T(8,128)S(1)} %all_to_all.22.mine), channel_id=1, source_target_pairs={{0,8},{8,0},{1,9},{9,1},{2,10},{10,2},{3,11},{11,3},{4,12},{12,4},... | collective-permute-start | bytes 786440 | tf_op jit(solution)/shard_map/ppermute | solution.py:468
  123.3 1.2 collective-permute-done.6.other
  125.2 4.0 %collective-permute-start.7 = (f32[96,4,128]{2,1,0:T(4,128)S(1)}, f32[96,4,128]{2,1,0:T(4,128)S(1)}, u32[]{:S(2)}, u32[]{:S(2)}) collective-permute-start(f32[96,4,128]{2,1,0:T(4,128)S(1)} %get-tuple-element.57), channel_id=1, source_target_pairs={{0,1},{1,2},{2,3},{3,4},{4,5},{5,6},{6,7},{8,9},{9,10},{10,11},{11... | collective-permute-start | bytes 589832 | tf_op jit(solution)/shard_map/ppermute | solution.py:384
  129.2 1.3 collective-permute-start.8
  130.5 2.6 %collective-permute-done.7.low_g.low = f32[96,4,128]{2,1,0:T(4,128)S(1)} collective-permute-done((f32[96,4,128]{2,1,0:T(4,128)S(1)}, f32[96,4,128]{2,1,0:T(4,128)S(1)}, u32[]{:S(2)}, u32[]{:S(2)}) %collective-permute-start.7) | collective-permute-done | bytes 196640 | tf_op jit(solution)/shard_map/ppermute | solution.py:384
  133.1 4.1 %collective-permute-done.8.high_g.high = f32[96,4,128]{2,1,0:T(4,128)S(1)} collective-permute-done((f32[96,4,128]{2,1,0:T(4,128)S(1)}, f32[96,4,128]{2,1,0:T(4,128)S(1)}, u32[]{:S(2)}, u32[]{:S(2)}) %collective-permute-start.8) | collective-permute-done | bytes 196640 | tf_op jit(solution)/shard_map/ppermute | solution.py:384
  137.2 4.1 %shard_map.164 = (f32[64,16,128]{2,1,0:T(8,128)S(1)}, f32[8,1,128]{2,1,0:T(1,128)}) custom-call(f32[64,16,128]{2,1,0:T(8,128)S(1)} %get-tuple-element.55.summed, f32[64,16,128]{2,1,0:T(8,128)S(1)} %get-tuple-element.56.smooth, f32[96,4,128]{2,1,0:T(4,128)S(1)} %collective-permute-done.7.low_g.low, f32[96,4,128]{2,1,0:T(4,128)S(1)} %collective-permute-done.8.high_g.high, ...), custom_call_target="tpu_custom_call" | custom-call | flops 5242880 | bytes 1769472 | tf_op jit(solution)/shard_map/pallas_call | solution.py:30
  142.1 6.1 %all-to-all-start.3 = ((f32[8,1,128]{2,1,0:T(1,128)}), f32[8,1,128]{2,1,0:T(1,128)S(1)}, u32[]{:S(2)}, u32[]{:S(2)}) async-start(f32[8,1,128]{2,1,0:T(1,128)} %get-tuple-element.59), calls=%async_computation.3 | async-start | bytes 8192 | tf_op jit(solution)/shard_map/all_to_all | solution.py:487
  148.2 3.6 %shard_map.165 = (f32[64,16,128]{2,1,0:T(8,128)S(1)}, f32[64,16,128]{2,1,0:T(8,128)S(1)}) custom-call(s32[4]{0:T(128)S(1)} %pad_add_fusion.place, s32[1]{0:T(128)S(6)} %copy.19.src_cell, f32[1,3]{1,0:T(1,128)S(1)} %copy-done.18, f32[64,16,128]{2,1,0:T(8,128)S(1)} %get-tuple-element.54.u_two, f32[64,16,128]{2,1,0:T(8,128)S(1)} %get-tuple-element.43.u_one, ...), custom_call_target="tpu_custom_call" | custom-call | flops 10485760 | bytes 3014688 | tf_op jit(solution)/shard_map/pallas_call | solution.py:30
  152.7 0.8 copy-done.10
  153.5 1.0 copy-done.7
  154.5 1.0 copy-done.9
  155.6 1.0 copy-done.11
  156.6 1.7 %shard_map.166 = (f32[2,16,128]{2,1,0:T(8,128)}, f32[2,16,128]{2,1,0:T(8,128)}, f32[1,64,16,128]{3,2,1,0:T(8,128)}) custom-call(s32[4]{0:T(128)S(1)} %pad_add_fusion.place, f32[8,1,128]{2,1,0:T(1,128)S(1)} %all-to-all-done.3.squares, f32[64,16,128]{2,1,0:T(8,128)S(1)} %copy-done.7, f32[64,16,128]{2,1,0:T(8,128)S(1)} %get-tuple-element.47.model, ...), custom_call_target="tpu_custom_call" | custom-call | flops 2621440 | bytes 2101264 | tf_op jit(solution)/shard_map/pallas_call | solution.py:30
  (51 shorter events, 7.8 us)
Async XLA Ops:
  0.6 0.7 copy-start.14
  1.4 0.7 copy-start.15
  2.1 0.7 copy-start.16
  2.8 0.7 copy-start.17
  3.6 40.9 %copy-start = (f32[1,64,16,128]{3,2,1,0:T(8,128)S(1)}, f32[1,64,16,128]{3,2,1,0:T(8,128)}, u32[]{:S(2)}) copy-start(f32[1,64,16,128]{3,2,1,0:T(8,128)} %u_cur.3) | copy-start | bytes 1572868
  3.6 40.9 %copy-start.1 = (f32[1,64,16,128]{3,2,1,0:T(8,128)S(1)}, f32[1,64,16,128]{3,2,1,0:T(8,128)}, u32[]{:S(2)}) copy-start(f32[1,64,16,128]{3,2,1,0:T(8,128)} %a_cur.3) | copy-start | bytes 1572868
  41.6 30.6 %collective-permute-start = (f32[16,4,2,16,128]{4,3,2,1,0:T(8,128)S(1)}, f32[16,4,2,16,128]{4,3,2,1,0:T(8,128)}, u32[]{:S(2)}, u32[]{:S(2)}) collective-permute-start(f32[16,4,2,16,128]{4,3,2,1,0:T(8,128)S(1)} %all_to_all.20.mine), channel_id=1, source_target_pairs={{0,8},{8,0},{1,9},{9,1},{2,10},{10,2},{3,11},{11,3},{4,12},{12,4},... | collective-permute-start | bytes 3145736 | tf_op jit(solution)/shard_map/ppermute | solution.py:443
  44.6 7.4 %copy-start.21 = (s32[16,2,4]{0,2,1:T(4,128)S(1)}, s32[16,2,4]{0,2,1:T(4,128)}, u32[]{:S(2)}) copy-start(s32[16,2,4]{0,2,1:T(4,128)} %param.22) | copy-start | bytes 1540
  45.4 9.1 %collective-permute-start.1 = (f32[2,64,4,128]{3,2,1,0:T(4,128)}, f32[2,64,4,128]{3,2,1,0:T(4,128)S(1)}, u32[]{:S(2)}, u32[]{:S(2)}) collective-permute-start(f32[2,64,4,128]{3,2,1,0:T(4,128)} %pad_maximum_fusion), channel_id=1, source_target_pairs={{0,1},{1,2},{2,3},{3,4},{4,5},{5,6},{6,7},{8,9},{9,10},{10,11},{11... | collective-permute-start | bytes 786440 | tf_op jit(solution)/shard_map/ppermute | solution.py:384
  48.6 11.6 %copy-start.12 = (f32[1,64,16,128]{3,2,1,0:T(8,128)S(1)}, f32[1,64,16,128]{3,2,1,0:T(8,128)}, u32[]{:S(2)}) copy-start(f32[1,64,16,128]{3,2,1,0:T(8,128)} %u_prev.1) | copy-start | bytes 1572868
  48.6 11.6 %copy-start.13 = (f32[1,64,16,128]{3,2,1,0:T(8,128)S(1)}, f32[1,64,16,128]{3,2,1,0:T(8,128)}, u32[]{:S(2)}) copy-start(f32[1,64,16,128]{3,2,1,0:T(8,128)} %a_prev.1) | copy-start | bytes 1572868
  49.4 9.8 %collective-permute-start.2 = (f32[2,64,4,128]{3,2,1,0:T(4,128)}, f32[2,64,4,128]{3,2,1,0:T(4,128)}, u32[]{:S(2)}, u32[]{:S(2)}) collective-permute-start(f32[2,64,4,128]{3,2,1,0:T(4,128)} %pad_maximum_fusion.1), channel_id=1, source_target_pairs={{1,0},{2,1},{3,2},{4,3},{5,4},{6,5},{7,6},{9,8},{10,9},{11,10},{12... | collective-permute-start | bytes 786440 | tf_op jit(solution)/shard_map/ppermute | solution.py:384
  59.1 1.0 copy-start.20
  60.1 0.7 copy-start.18
  60.1 0.7 copy-start.19
  74.1 13.0 %copy-start.2 = (f32[64,16,128]{2,1,0:T(8,128)}, f32[64,16,128]{2,1,0:T(8,128)S(1)}, u32[]{:S(2)}) copy-start(f32[64,16,128]{2,1,0:T(8,128)S(1)} %get-tuple-element.48.aniso_h) | copy-start | bytes 1572868
  74.1 13.0 %copy-start.4 = (f32[64,16,128]{2,1,0:T(8,128)}, f32[64,16,128]{2,1,0:T(8,128)S(1)}, u32[]{:S(2)}) copy-start(f32[64,16,128]{2,1,0:T(8,128)S(1)} %get-tuple-element.49.aniso_c) | copy-start | bytes 1572868
  74.1 5.4 %collective-permute-start.3 = (f32[80,4,128]{2,1,0:T(4,128)S(1)}, f32[80,4,128]{2,1,0:T(4,128)S(1)}, u32[]{:S(2)}, u32[]{:S(2)}) collective-permute-start(f32[80,4,128]{2,1,0:T(4,128)S(1)} %get-tuple-element.50), channel_id=1, source_target_pairs={{0,1},{1,2},{2,3},{3,4},{4,5},{5,6},{6,7},{8,9},{9,10},{10,11},{11... | collective-permute-start | bytes 491528 | tf_op jit(solution)/shard_map/ppermute | solution.py:384
  77.3 6.1 %collective-permute-start.4 = (f32[80,4,128]{2,1,0:T(4,128)S(1)}, f32[80,4,128]{2,1,0:T(4,128)S(1)}, u32[]{:S(2)}, u32[]{:S(2)}) collective-permute-start(f32[80,4,128]{2,1,0:T(4,128)S(1)} %get-tuple-element.51), channel_id=1, source_target_pairs={{1,0},{2,1},{3,2},{4,3},{5,4},{6,5},{7,6},{9,8},{10,9},{11,10},{12... | collective-permute-start | bytes 491528 | tf_op jit(solution)/shard_map/ppermute | solution.py:384
  87.1 3.8 %collective-permute-start.5 = (f32[16,2,16,128]{3,2,1,0:T(8,128)S(1)}, f32[16,2,16,128]{3,2,1,0:T(8,128)S(1)}, u32[]{:S(2)}, u32[]{:S(2)}) collective-permute-start(f32[16,2,16,128]{3,2,1,0:T(8,128)S(1)} %get-tuple-element.53), channel_id=1, source_target_pairs={{0,8},{8,0},{1,9},{9,1},{2,10},{10,2},{3,11},{11,3},{4,12},{12,4},... | collective-permute-start | bytes 786440 | tf_op jit(solution)/shard_map/ppermute | solution.py:464
  120.3 4.2 %collective-permute-start.6 = (f32[16,2,16,128]{3,2,1,0:T(8,128)S(1)}, f32[16,2,16,128]{3,2,1,0:T(8,128)S(1)}, u32[]{:S(2)}, u32[]{:S(2)}) collective-permute-start(f32[16,2,16,128]{3,2,1,0:T(8,128)S(1)} %all_to_all.22.mine), channel_id=1, source_target_pairs={{0,8},{8,0},{1,9},{9,1},{2,10},{10,2},{3,11},{11,3},{4,12},{12,4},... | collective-permute-start | bytes 786440 | tf_op jit(solution)/shard_map/ppermute | solution.py:468
  125.2 7.9 %collective-permute-start.7 = (f32[96,4,128]{2,1,0:T(4,128)S(1)}, f32[96,4,128]{2,1,0:T(4,128)S(1)}, u32[]{:S(2)}, u32[]{:S(2)}) collective-permute-start(f32[96,4,128]{2,1,0:T(4,128)S(1)} %get-tuple-element.57), channel_id=1, source_target_pairs={{0,1},{1,2},{2,3},{3,4},{4,5},{5,6},{6,7},{8,9},{9,10},{10,11},{11... | collective-permute-start | bytes 589832 | tf_op jit(solution)/shard_map/ppermute | solution.py:384
  129.2 8.0 %collective-permute-start.8 = (f32[96,4,128]{2,1,0:T(4,128)S(1)}, f32[96,4,128]{2,1,0:T(4,128)S(1)}, u32[]{:S(2)}, u32[]{:S(2)}) collective-permute-start(f32[96,4,128]{2,1,0:T(4,128)S(1)} %get-tuple-element.58), channel_id=1, source_target_pairs={{1,0},{2,1},{3,2},{4,3},{5,4},{6,5},{7,6},{9,8},{10,9},{11,10},{12... | collective-permute-start | bytes 589832 | tf_op jit(solution)/shard_map/ppermute | solution.py:384
  137.2 11.0 %copy-start.3 = (f32[64,16,128]{2,1,0:T(8,128)S(1)}, f32[64,16,128]{2,1,0:T(8,128)}, u32[]{:S(2)}) copy-start(f32[64,16,128]{2,1,0:T(8,128)} %copy-done.2) | copy-start | bytes 1572868
  137.2 11.0 %copy-start.5 = (f32[64,16,128]{2,1,0:T(8,128)S(1)}, f32[64,16,128]{2,1,0:T(8,128)}, u32[]{:S(2)}) copy-start(f32[64,16,128]{2,1,0:T(8,128)} %copy-done.4) | copy-start | bytes 1572868
  141.3 0.8 copy-start.6
  142.1 11.4 %all-to-all-start.3 = ((f32[8,1,128]{2,1,0:T(1,128)}), f32[8,1,128]{2,1,0:T(1,128)S(1)}, u32[]{:S(2)}, u32[]{:S(2)}) async-start(f32[8,1,128]{2,1,0:T(1,128)} %get-tuple-element.59), calls=%async_computation.3 | async-start | bytes 8192 | tf_op jit(solution)/shard_map/all_to_all | solution.py:487
  151.9 0.8 copy-start.8
  152.7 0.8 copy-start.10
  153.5 1.0 copy-start.7
  154.5 1.0 copy-start.9
  155.6 1.0 copy-start.11

commit v3 on v2

--- a/solution.py
+++ b/solution.py
@@ -14,45 +14,58 @@
 PEERS = ("xh", "z")
 SWAP = [(0, 1), (1, 0)]
 REACH = 4
-VMEM_LIMIT = 16 * 2**20
 MID = 8
 CHUNK = 4
 VMEM = pl.BlockSpec(memory_space=pltpu.VMEM)
 SMEM = pl.BlockSpec(memory_space=pltpu.SMEM)
+HBM = pl.BlockSpec(memory_space=pltpu.HBM)
 
 
 def f32(*shape):
     return jax.ShapeDtypeStruct(shape, jnp.float32)
 
 
-def call(kernel, args, smem, outs, scratch=(), flops=0):
+def call(kernel, args, smem, outs, scratch=(), flops=0, hbm_in=(), hbm_out=(), grant=16):
     bytes_accessed = 4 * sum(a.size for a in args)
+    spec = lambda i: SMEM if i < smem else HBM if i in hbm_in else VMEM
+    single = not isinstance(outs, tuple)
+    out_specs = [HBM if i in hbm_out else VMEM for i in range(1 if single else len(outs))]
     return pl.pallas_call(
         kernel,
         out_shape=outs,
-        in_specs=[SMEM if i < smem else VMEM for i in range(len(args))],
-        out_specs=jax.tree.map(lambda _: VMEM, outs),
+        in_specs=[spec(i) for i in range(len(args))],
+        out_specs=out_specs[0] if single else tuple(out_specs),
         scratch_shapes=list(scratch),
         cost_estimate=pl.CostEstimate(
             flops=flops, bytes_accessed=bytes_accessed, transcendentals=0
         ),
-        compiler_params=pltpu.CompilerParams(vmem_limit_bytes=VMEM_LIMIT),
+        compiler_params=pltpu.CompilerParams(vmem_limit_bytes=grant * 2**20),
     )(*args)
 
 
-def fill_padded(pad, read, low, high):
-    cells_x, cells_z = pad.shape[0] - 2 * REACH, pad.shape[1] - 2 * MID
-    zeros = jnp.zeros((REACH, *pad.shape[1:]), jnp.float32)
-    pad[pl.ds(0, REACH)] = zeros
-    pad[pl.ds(REACH + cells_x, REACH)] = zeros
+def fill_rows(rows, read):
+    cells_x = rows.shape[0] - 2 * REACH
+    zeros = jnp.zeros((REACH, *rows.shape[1:]), jnp.float32)
+    rows[pl.ds(0, REACH)] = zeros
+    rows[pl.ds(REACH + cells_x, REACH)] = zeros
 
     @pl.loop(0, cells_x // CHUNK)
     def _(step):
         x = step * CHUNK
-        to = pl.ds(REACH + x, CHUNK)
-        pad[to, pl.ds(MID, cells_z), :] = read(x)
-        pad[to, pl.ds(MID - REACH, REACH), :] = low(x)
-        pad[to, pl.ds(MID + cells_z, REACH), :] = high(x)
+        rows[pl.ds(REACH + x, CHUNK)] = read(pl.ds(x, CHUNK))
+
+
+def fill_depth(pad, place, read, low, high):
+    cells_x, cells_z = pad.shape[0], pad.shape[1] - 2 * MID
+    below = place[0] > 0
+    above = place[0] + cells_z < place[1]
+
+    @pl.loop(0, cells_x // CHUNK)
+    def _(step):
+        at = pl.ds(step * CHUNK, CHUNK)
+        pad[at, pl.ds(MID, cells_z), :] = read(at)
+        pad[at, pl.ds(MID - REACH, REACH), :] = jnp.where(below, low(at), 0.0)
+        pad[at, pl.ds(MID + cells_z, REACH), :] = jnp.where(above, high(at), 0.0)
 
 
 def depth_pass(pad, first_z, second_z):
@@ -64,7 +77,7 @@
     @pl.loop(0, cells_x // CHUNK)
     def _(step):
         x = step * CHUNK
-        at = lambda k: pad[pl.ds(REACH + x, CHUNK), pl.ds(MID + k, cells_z), :]
+        at = lambda k: pad[pl.ds(x, CHUNK), pl.ds(MID + k, cells_z), :]
         two = second_coef[0] * at(0)
         one = None
         for k in range(1, 5):
@@ -83,11 +96,11 @@
     return up, down
 
 
-def lateral(pad, x, masks, cells_z):
+def lateral(rows, x, masks):
     up, down = masks
-    at = lambda k: pad[pl.ds(REACH + x + k, CHUNK), pl.ds(MID, cells_z), :]
+    at = lambda k: rows[pl.ds(REACH + x + k, CHUNK)]
     v = at(0)
-    cells_y = v.shape[2]
+    cells_z, cells_y = v.shape[1:]
     total = (2.0 * second_coef[0]) * v
     for k in range(1, 5):
         total = total + second_coef[k] * (at(k) + at(-k))
@@ -120,51 +133,74 @@
         ref[at] = ref[at] + jnp.where(lane == cell % cells_y, amount, 0.0)
 
 
-def spread_kernel(model, aniso_h, aniso_c, smooth, out):
-    for j, ref in enumerate((model, aniso_h, aniso_c, smooth)):
-        block = ref[...]
-        for peer in range(out.shape[0]):
-            out[peer, j] = block
-
-
-def land_kernel(low, high, low_out, high_out):
-    low_out[...] = low[...]
-    high_out[...] = high[...]
+def spread_kernel(model, aniso_h, aniso_c, smooth, out, own, sem_in, sem_out):
+    arrays = (model, aniso_h, aniso_c, smooth)
+    loads = [pltpu.make_async_copy(ref, own.at[j], sem_in.at[j]) for j, ref in enumerate(arrays)]
+    for load in loads:
+        load.start()
+    for load in loads:
+        load.wait()
+    sends = [pltpu.make_async_copy(own, out.at[p], sem_out.at[p]) for p in range(out.shape[0])]
+    for send in sends:
+        send.start()
+    for send in sends:
+        send.wait()
+
+
+def place_receivers(out, rec_cell, rec_data, z_start, depth_cells):
+    cells_x, cells_z, cells_y = out.shape
+    cell = rec_cell[...]
+    row = cell // cells_y
+    z = row % depth_cells - z_start
+    key = jnp.where((z >= 0) & (z < cells_z), row // depth_cells * cells_z + z, -1)
+    y = cell % cells_y
+    count = cell.shape[1]
+    lanes = jnp.where(
+        lax.broadcasted_iota(jnp.int32, (cells_y, count), 0) == y, 1.0, 0.0
+    ).astype(jnp.bfloat16)
+    rest, terms = rec_data[0, pl.ds(0, 1), :], []
+    for _ in range(3):
+        term = rest.astype(jnp.bfloat16).astype(jnp.float32)
+        terms.append(term)
+        rest = rest - term
+    block = min(16, cells_x)
+
+    @pl.loop(0, cells_x // block)
+    def _(step):
+        first = step * block * cells_z
+        index = first + lax.broadcasted_iota(jnp.int32, (block * cells_z, count), 0)
+        hit = index == key
+        total = None
+        for term in terms:
+            left = jnp.where(hit, term, 0.0).astype(jnp.bfloat16)
+            part = lax.dot_general(
+                left, lanes, (((1,), (1,)), ((), ())), preferred_element_type=jnp.float32
+            )
+            total = part if total is None else total + part
+        at = pl.ds(step * block, block)
+        out[at] = out[at] + total.reshape(block, cells_z, cells_y)
 
 
 def open_kernel(
-    place, src_cell, src_wave, rec_cell, rec_data, onehot, shot_group,
+    place, src_cell, src_wave, onehot, shot_group, rec_cell, rec_data,
     u_prev, u_cur, a_prev, a_cur, low, high,
     base_u, lat_u, dep_u, cross_u, base_a, lat_a, dep_a, cross_a, weight,
-    pad, first_z,
+    old, now, base, lat, dep, cross, scale_row, rows, pad, first_z, sem_in, sem_out,
 ):
     cells_x, cells_z, cells_y = lat_u.shape
     masks = lateral_masks(cells_y)
-    sides = ((u_prev, u_cur, base_u, lat_u, dep_u, cross_u),
-             (a_prev, a_cur, base_a, lat_a, dep_a, cross_a))
-    for j, (old, now, base, lat, dep, cross) in enumerate(sides):
-        fill_padded(
-            pad,
-            lambda x, now=now: now[0, pl.ds(x, CHUNK)],
-            lambda x, j=j: low[j, pl.ds(x, CHUNK)],
-            lambda x, j=j: high[j, pl.ds(x, CHUNK)],
-        )
-        depth_pass(pad, first_z, dep)
-
-        @pl.loop(0, cells_x // CHUNK)
-        def _(step, old=old, now=now, base=base, lat=lat, cross=cross):
-            x = step * CHUNK
-            rows = pl.ds(x, CHUNK)
-            lat[rows] = lateral(pad, x, masks, cells_z)
-            cross[rows] = crossing(first_z, x)
-            base[rows] = 2.0 * now[0, rows] - old[0, rows]
-
-    z_start, depth_cells = place[0], place[1]
-    add_at(base_u, src_cell[0], src_wave[0, 0], z_start, depth_cells)
-
-    @pl.loop(0, rec_cell.shape[1])
-    def _(r):
-        add_at(base_a, rec_cell[0, r], rec_data[0, 0, r], z_start, depth_cells)
+    loads = []
+    for j, (before, current) in enumerate(((u_prev, u_cur), (a_prev, a_cur))):
+        loads.append(pltpu.make_async_copy(current.at[0], now.at[j], sem_in.at[j, 0]))
+        loads.append(pltpu.make_async_copy(before.at[0], old.at[j], sem_in.at[j, 1]))
+    for load in loads:
+        load.start()
+    sends = []
+
+    def send(source, target):
+        copy = pltpu.make_async_copy(source, target, sem_out.at[len(sends)])
+        copy.start()
+        sends.append(copy)
 
     blocks = onehot.shape[1]
     position = lax.broadcasted_iota(jnp.int32, weight.shape, 1)
@@ -175,7 +211,54 @@
             for b in range(onehot.shape[2])
         )
         value = jnp.where(position // (cells_z // blocks) == block, scale, value)
-    weight[...] = value
+    scale_row[...] = value
+    send(scale_row, weight)
+
+    targets = ((base_u, lat_u, dep_u, cross_u), (base_a, lat_a, dep_a, cross_a))
+    for j in range(2):
+        loads[2 * j].wait()
+        loads[2 * j + 1].wait()
+        fill_depth(
+            pad,
+            place,
+            lambda at, j=j: now[j, at],
+            lambda at, j=j: low[j, at],
+            lambda at, j=j: high[j, at],
+        )
+        depth_pass(pad, first_z, dep.at[j])
+        send(dep.at[j], targets[j][2])
+        fill_rows(rows, lambda at, j=j: now[j, at])
+
+        @pl.loop(0, cells_x // CHUNK)
+        def _(step, j=j):
+            x = step * CHUNK
+            at = pl.ds(x, CHUNK)
+            lat[j, at] = lateral(rows, x, masks)
+            cross[j, at] = crossing(first_z, x)
+            base[j, at] = 2.0 * now[j, at] - old[j, at]
+
+        send(lat.at[j], targets[j][1])
+        send(cross.at[j], targets[j][3])
+        if j == 0:
+            add_at(base.at[0], src_cell[0], src_wave[0, 0], place[0], place[1])
+        else:
+            place_receivers(base.at[1], rec_cell, rec_data, place[0], place[1])
+        send(base.at[j], targets[j][0])
+    for copy in sends:
+        copy.wait()
+
+
+def fetch_kernel(*refs):
+    count = (len(refs) - 1) // 2
+    sources, targets, sem = refs[:count], refs[count:-1], refs[-1]
+    copies = [
+        pltpu.make_async_copy(source, target, sem.at[i])
+        for i, (source, target) in enumerate(zip(sources, targets))
+    ]
+    for copy in copies:
+        copy.start()
+    for copy in copies:
+        copy.wait()
 
 
 def first_kernel(
@@ -206,33 +289,36 @@
             high[edge] = s[:, cells_z - 1][None]
 
 
+def side_kernel(now, old, aniso_h, base, side, rows):
+    cells_x, _, cells_y = base.shape
+    masks = lateral_masks(cells_y)
+    fill_rows(rows, lambda at: now[at])
+
+    @pl.loop(0, cells_x // CHUNK)
+    def _(step):
+        x = step * CHUNK
+        at = pl.ds(x, CHUNK)
+        base[at] = 2.0 * now[at] - old[at]
+        side[at] = aniso_h[at] * lateral(rows, x, masks)
+
+
 def second_kernel(
     place, src_cell, src_wave,
-    u_one, u_cur, a_one, grad, weight, model, aniso_h, aniso_c, low, high,
+    u_one, base, side, a_one, grad, weight, model, aniso_c, low, high,
     u_two, keep, send, pad, first_z, dep,
 ):
-    cells_x, cells_z, cells_y = u_two.shape
-    masks = lateral_masks(cells_y)
-    fill_padded(
-        pad,
-        lambda x: u_one[pl.ds(x, CHUNK)],
-        lambda x: low[pl.ds(x, CHUNK)],
-        lambda x: high[pl.ds(x, CHUNK)],
-    )
+    cells_x, _, _ = u_two.shape
+    fill_depth(pad, place, lambda at: u_one[at], lambda at: low[at], lambda at: high[at])
     depth_pass(pad, first_z, dep)
     own = place[2] == 0
 
     @pl.loop(0, cells_x // CHUNK)
     def _(step):
         x = step * CHUNK
-        rows = pl.ds(x, CHUNK)
-        k_u = (
-            aniso_h[rows] * lateral(pad, x, masks, cells_z)
-            + dep[rows]
-            + aniso_c[rows] * crossing(first_z, x)
-        )
-        u_two[rows] = 2.0 * u_one[rows] - u_cur[0, rows] + model[rows] * k_u
-        total = weight[...] * (grad[rows] + a_one[rows] * k_u)
+        at = pl.ds(x, CHUNK)
+        k_u = side[at] + dep[at] + aniso_c[at] * crossing(first_z, x)
+        u_two[at] = base[at] + model[at] * k_u
+        total = weight[...] * (grad[at] + a_one[at] * k_u)
         keep[step] = jnp.where(own, total[:2], total[2:])
         send[step] = jnp.where(own, total[2:], total[:2])
 
@@ -268,9 +354,11 @@
 SM = 16
 
 
-def relax_kernel(summed, smooth, low_g, high_g, low_s, high_s, out, square, wide, once, coef):
+def relax_kernel(place, summed, smooth, low_g, high_g, low_s, high_s, out, square, wide, once, coef):
     cells_x, cells_z, cells_y = summed.shape
     tall = wide.shape[1]
+    below = place[0] > 0
+    above = place[0] + cells_z < place[1]
     zero_row = jnp.zeros((1, tall, cells_y), jnp.float32)
     for ref in (wide, once):
         ref[pl.ds(0, 1)] = zero_row
@@ -286,12 +374,12 @@
             x = q * CHUNK + j
             halo = (pl.ds(cells_x + 2 * q + j // 2, 1), pl.ds(2 * (j % 2), 2), slice(None))
             wide[pl.ds(x + 1, 1), pl.ds(SM, cells_z), :] = summed[pl.ds(x, 1)]
-            wide[pl.ds(x + 1, 1), pl.ds(SM - 2, 2), :] = low_g[halo]
-            wide[pl.ds(x + 1, 1), pl.ds(SM + cells_z, 2), :] = high_g[halo]
+            wide[pl.ds(x + 1, 1), pl.ds(SM - 2, 2), :] = jnp.where(below, low_g[halo], 0.0)
+            wide[pl.ds(x + 1, 1), pl.ds(SM + cells_z, 2), :] = jnp.where(above, high_g[halo], 0.0)
             edge = (pl.ds(cells_x + q, 1), pl.ds(j, 1), slice(None))
             coef[pl.ds(x, 1), pl.ds(SM, cells_z), :] = smooth[pl.ds(x, 1)]
-            coef[pl.ds(x, 1), pl.ds(SM - 1, 1), :] = low_s[edge]
-            coef[pl.ds(x, 1), pl.ds(SM + cells_z, 1), :] = high_s[edge]
+            coef[pl.ds(x, 1), pl.ds(SM - 1, 1), :] = jnp.where(below, low_s[edge], 0.0)
+            coef[pl.ds(x, 1), pl.ds(SM + cells_z, 1), :] = jnp.where(above, high_s[edge], 0.0)
 
     lane = lax.broadcasted_iota(jnp.int32, (1, 8, cells_y), 2)
 
@@ -325,30 +413,19 @@
 
 
 def third_kernel(
-    place, src_cell, src_wave, u_two, u_one, model, aniso_h, aniso_c, low, high,
+    place, src_cell, src_wave, u_two, base_in, side, model, aniso_c, low, high,
     base, change, pad, first_z, dep,
 ):
-    cells_x, cells_z, cells_y = base.shape
-    masks = lateral_masks(cells_y)
-    fill_padded(
-        pad,
-        lambda x: u_two[pl.ds(x, CHUNK)],
-        lambda x: low[pl.ds(x, CHUNK)],
-        lambda x: high[pl.ds(x, CHUNK)],
-    )
+    cells_x = base.shape[0]
+    fill_depth(pad, place, lambda at: u_two[at], lambda at: low[at], lambda at: high[at])
     depth_pass(pad, first_z, dep)
 
     @pl.loop(0, cells_x // CHUNK)
     def _(step):
         x = step * CHUNK
-        rows = pl.ds(x, CHUNK)
-        k_u = (
-            aniso_h[rows] * lateral(pad, x, masks, cells_z)
-            + dep[rows]
-            + aniso_c[rows] * crossing(first_z, x)
-        )
-        base[rows] = 2.0 * u_two[rows] - u_one[rows]
-        change[rows] = model[rows] * k_u
+        at = pl.ds(x, CHUNK)
+        base[at] = base_in[at]
+        change[at] = model[at] * (side[at] + dep[at] + aniso_c[at] * crossing(first_z, x))
 
     add_at(base, src_cell[0], src_wave[0, 2], place[0], place[1])
 
@@ -379,7 +456,7 @@
 
 def shift(low_edge, high_edge):
     count = lax.axis_size(DEPTH)
-    forward = [(i, i + 1) for i in range(count - 1)]
+    forward = [(i, (i + 1) % count) for i in range(count)]
     backward = [(target, source) for source, target in forward]
     return lax.ppermute(high_edge, DEPTH, forward), lax.ppermute(low_edge, DEPTH, backward)
 
@@ -413,9 +490,12 @@
             lax.axis_index(SHOT) * rows,
         ]
     )
-    pad = pltpu.VMEM((cells_x + 2 * REACH, cells_z + 2 * MID, cells_y), jnp.float32)
-    first_z = pltpu.VMEM((cells_x + 2 * REACH, cells_z, cells_y), jnp.float32)
-    dep = pltpu.VMEM((cells_x, cells_z, cells_y), jnp.float32)
+    scratch = lambda *shape: pltpu.VMEM(shape, jnp.float32)
+    pad = scratch(cells_x, cells_z + 2 * MID, cells_y)
+    first_z = scratch(cells_x + 2 * REACH, cells_z, cells_y)
+    padded_rows = first_z
+    dep = scratch(cells_x, cells_z, cells_y)
+    pair = scratch(2, cells_x, cells_z, cells_y)
     work = 80 * cells_x * cells_z * cells_y
 
     spread = call(
@@ -423,6 +503,14 @@
         (model, aniso_h, aniso_c, smooth_coef),
         0,
         f32(peers, 4, rows, cells_z, cells_y),
+        (
+            scratch(4, rows, cells_z, cells_y),
+            pltpu.SemaphoreType.DMA((4,)),
+            pltpu.SemaphoreType.DMA((peers,)),
+        ),
+        hbm_in=range(4),
+        hbm_out=(0,),
+        grant=62,
     )
     mine = lax.all_to_all(spread, PEERS, 0, 0, tiled=True)
 
@@ -430,32 +518,48 @@
         [lax.slice_in_dim(v, start, start + REACH, axis=2) for v in (u_cur, a_cur)]
     )
     low, high = shift(edges(0), edges(cells_z - REACH))
-    low, high = call(land_kernel, (low, high), 0, (f32(*low.shape), f32(*high.shape)))
     *parts, weight = call(
         open_kernel,
-        (place, src_cell, src_wave, rec_cell, rec_data, bin_onehot, shot_group)
+        (place, src_cell, src_wave, bin_onehot, shot_group, rec_cell, rec_data)
         + (u_prev, u_cur, a_prev, a_cur, low, high),
-        7,
+        5,
         (slab,) * 8 + (f32(1, cells_z, cells_y),),
-        (pad, first_z),
+        (pair,) * 6
+        + (scratch(1, cells_z, cells_y), padded_rows, pad, first_z)
+        + (pltpu.SemaphoreType.DMA((2, 2)), pltpu.SemaphoreType.DMA((9,))),
         2 * work,
+        hbm_in=range(7, 11),
+        hbm_out=range(9),
+        grant=61,
     )
     other = lax.ppermute(mine, "core", SWAP)
+    *parts, weight, adjoint = call(
+        fetch_kernel,
+        (*parts, weight, a_cur),
+        0,
+        (slab,) * 8 + (f32(1, cells_z, cells_y), f32(*a_cur.shape)),
+        (pltpu.SemaphoreType.DMA((10,)),),
+        hbm_in=range(10),
+        grant=49,
+    )
     payload = f32(cells_x + peers, REACH, cells_y)
     u_one, a_one, grad, model_slab, h_slab, c_slab, smooth_slab, low_edge, high_edge = call(
         first_kernel,
-        (place, mine, other, a_cur, *parts),
+        (place, mine, other, adjoint, *parts),
         1,
         (slab,) * 7 + (payload, payload),
         (),
         20 * slab.size,
     )
     low_one, high_one = shift(low_edge, high_edge)
+    base, side = call(
+        side_kernel, (u_one, u_cur[0], h_slab), 0, (slab, slab), (padded_rows,), work // 2
+    )
     split = f32(peers, rows, cells_z, cells_y)
     u_two, keep, send = call(
         second_kernel,
         (place, src_cell, src_wave)
-        + (u_one, u_cur, a_one, grad, weight, model_slab, h_slab, c_slab, low_one, high_one),
+        + (u_one, base, side, a_one, grad, weight, model_slab, c_slab, low_one, high_one),
         3,
         (slab, split, split),
         (pad, first_z, dep),
@@ -471,11 +575,14 @@
         join_kernel, (place, mine, other, u_two), 1, (slab, payload, payload)
     )
     low_two, high_two = shift(low_edge, high_edge)
+    base, side = call(
+        side_kernel, (u_two, u_one, h_slab), 0, (slab, slab), (padded_rows,), work // 2
+    )
     tall = cells_z + 2 * SM
     smoothed, square = call(
         relax_kernel,
-        (summed, smooth_slab, low_two, high_two, low_one, high_one),
-        0,
+        (place, summed, smooth_slab, low_two, high_two, low_one, high_one),
+        1,
         (slab, f32(lax.axis_size(DEPTH), 1, cells_y)),
         (
             pltpu.VMEM((cells_x + 2, tall, cells_y), jnp.float32),
@@ -488,7 +595,7 @@
     base, change = call(
         third_kernel,
         (place, src_cell, src_wave)
-        + (u_two, u_one, model_slab, h_slab, c_slab, low_two, high_two),
+        + (u_two, base, side, model_slab, c_slab, low_two, high_two),
         3,
         (slab, slab),
         (pad, first_z, dep),

time: 160 us -> 146 us (0.912)
  waiting for transfers between devices: 20.7 us -> 11.6 us
  starting transfers between devices: 29 us -> 23.4 us
  Pallas kernels: 28.2 us -> 32.2 us
  local copies, waits for them, and re-layouts: 9.27 us -> 6.87 us
    ppermute x3, waiting for transfers between devices: 12.5 us -> 0.01 us  [shift(): lax.ppermute(low_edge, DEPTH, backward)]
    ppermute x3, starting transfers between devices: 10.4 us -> 1.54 us  [shift(): lax.ppermute(high_edge, DEPTH, forward)]
    ppermute x3, starting transfers between devices: 3.86 us -> 9.48 us  [shift(): lax.ppermute(low_edge, DEPTH, backward)]
    pallas_call x10 -> x12, Pallas kernels: 28.2 us -> 32.2 us  [call(): pl.pallas_call(kernel, out_shape=outs, in_specs=[spec(i) for i in range(l...]
    ppermute x3, waiting for transfers between devices: 5.87 us -> 9.19 us  [shift(): lax.ppermute(high_edge, DEPTH, forward)]
    unnamed x45 -> x27, local copies, waits for them, and re-layouts: 9.17 us -> 6.78 us
  transfers between devices with their start and end apart: 10 -> 10, of which waited for: 8 -> 5; matrix products, arithmetic and copies ran while one was open for 1% -> 1% of each run, Pallas kernels for 10% -> 14%
where the time goes in v3:
time: 146 us; the launch traced here: 144 us
  blocking collectives  67.4 us (46%)
  Pallas kernels  32.2 us (22%)
  starting transfers between devices  23.4 us (16%)
  waiting for transfers between devices  11.6 us (8%)
  local copies, waits for them, and re-layouts  6.87 us (5%)
  between operations  2.13 us (1%)
    all_to_all x1, blocking collectives, body(): mine = lax.all_to_all(spread, PEERS, 0, 0, tiled=True)  38.2 us
    pallas_call x12, Pallas kernels, call(): pl.pallas_call(kernel, out_shape=outs, in_specs=[spec(i) for i in range(l...  32.2 us
    all_to_all x1, blocking collectives, body(): mine = lax.all_to_all(total, PEERS, 0, 0, tiled=True)  14.6 us
    all_to_all x1, blocking collectives, body(): shares = lax.all_to_all(chip_sum, PEERS, 0, 0, tiled=True)  14.6 us
    ppermute x3, starting transfers between devices, shift(): lax.ppermute(low_edge, DEPTH, backward)  9.48 us
    ppermute x3, waiting for transfers between devices, shift(): lax.ppermute(high_edge, DEPTH, forward)  9.19 us
    unnamed x27, local copies, waits for them, and re-layouts  6.78 us
    ppermute x2, starting transfers between devices, body(): other = lax.ppermute(mine, 'core', SWAP)  5.9 us
  transfers between devices with their start and end apart: 10, of which 5 were waited for; matrix products, arithmetic and copies ran while one was open for 1% of the time, Pallas kernels for 14%

profile of v3, /device:TPU:1, one launch (start us, length us, event | category | flops | bytes accessed | tf_op | source)
XLA Modules:
  0.0 144.4 jit_solution(17962464843387928275)
XLA Ops:
  0.6 1.9 %shard_map.157 = f32[16,4,2,16,128]{4,3,2,1,0:T(8,128)} custom-call(f32[2,16,128]{2,1,0:T(8,128)} %model.1, f32[2,16,128]{2,1,0:T(8,128)} %aniso_h.1, f32[2,16,128]{2,1,0:T(8,128)} %aniso_c.1, f32[2,16,128]{2,1,0:T(8,128)} %smooth.1), custom_call_target="tpu_custom_call" | custom-call | bytes 65536 | tf_op jit(solution)/shard_map/pallas_call | solution.py:33
  2.6 38.2 %all_to_all.20.mine = f32[16,4,2,16,128]{4,3,2,1,0:T(8,128)S(1)} all-to-all(f32[16,4,2,16,128]{4,3,2,1,0:T(8,128)} %shard_map.157), channel_id=1, replica_groups=mesh['xh'=2,'z'=8,'core'=2,'xl'=2,'y'=4] {'xh','z'}, dimensions={0} | all-to-all | bytes 2097152 | tf_op jit(solution)/shard_map/all_to_all | solution.py:515
  40.8 2.8 %collective-permute-start = (f32[16,4,2,16,128]{4,3,2,1,0:T(8,128)S(1)}, f32[16,4,2,16,128]{4,3,2,1,0:T(8,128)}, u32[]{:S(2)}, u32[]{:S(2)}) collective-permute-start(f32[16,4,2,16,128]{4,3,2,1,0:T(8,128)S(1)} %all_to_all.20.mine), channel_id=1, source_target_pairs={{0,8},{8,0},{1,9},{9,1},{2,10},{10,2},{3,11},{11,3},{4,12},{12,4},... | collective-permute-start | bytes 3145736 | tf_op jit(solution)/shard_map/ppermute | solution.py:535
  43.8 1.4 collective-permute-start.1
  45.3 2.4 %collective-permute-start.2 = (f32[2,64,4,128]{3,2,1,0:T(4,128)S(1)}, f32[2,64,4,128]{3,2,1,0:T(4,128)S(1)}, u32[]{:S(2)}, u32[]{:S(2)}) collective-permute-start(f32[2,64,4,128]{3,2,1,0:T(4,128)S(1)} %pad_maximum_fusion.1), channel_id=1, source_target_pairs={{1,0},{2,1},{3,2},{4,3},{5,4},{6,5},{7,6},{0,7},{9,8},{10,9},{11,1... | collective-permute-start | bytes 786440 | tf_op jit(solution)/shard_map/ppermute | solution.py:461
  50.3 3.6 %collective-permute-done.1.low = f32[2,64,4,128]{3,2,1,0:T(4,128)S(1)} collective-permute-done((f32[2,64,4,128]{3,2,1,0:T(4,128)S(1)}, f32[2,64,4,128]{3,2,1,0:T(4,128)S(1)}, u32[]{:S(2)}, u32[]{:S(2)}) %collective-permute-start.1) | collective-permute-done | bytes 262176 | tf_op jit(solution)/shard_map/ppermute | solution.py:461
  53.9 0.7 copy-done.10
  54.6 0.7 copy-done.11
  55.3 10.7 %shard_map.158 = (f32[64,16,128]{2,1,0:T(8,128)}, f32[64,16,128]{2,1,0:T(8,128)}, f32[64,16,128]{2,1,0:T(8,128)}, f32[64,16,128]{2,1,0:T(8,128)}, f32[64,16,128]...) custom-call(s32[4]{0:T(128)} %pad_add_fusion.place, ...), custom_call_target="tpu_custom_call" | custom-call | flops 20971520 | bytes 2623524 | tf_op jit(solution)/shard_map/pallas_call | solution.py:33
  66.7 2.4 %shard_map.159 = (f32[64,16,128]{2,1,0:T(8,128)S(1)}, f32[64,16,128]{2,1,0:T(8,128)S(1)}, f32[64,16,128]{2,1,0:T(8,128)S(1)}, f32[64,16,128]{2,1,0:T(8,128)S(1)}...) custom-call(f32[64,16,128]{2,1,0:T(8,128)} %get-tuple-element.45.ref, ...), custom_call_target="tpu_custom_call" | custom-call | bytes 4726784 | tf_op jit(solution)/shard_map/pallas_call | solution.py:33
  69.7 1.8 %shard_map.160 = (f32[64,16,128]{2,1,0:T(8,128)S(1)}, f32[64,16,128]{2,1,0:T(8,128)S(1)}, f32[64,16,128]{2,1,0:T(8,128)S(1)}, f32[64,16,128]{2,1,0:T(8,128)S(1)}...) custom-call(s32[4]{0:T(128)S(1)} %copy-done.6, ...), custom_call_target="tpu_custom_call" | custom-call | flops 2621440 | bytes 6815760 | tf_op jit(solution)/shard_map/pallas_call | solution.py:33
  71.7 3.6 %collective-permute-start.4 = (f32[80,4,128]{2,1,0:T(4,128)S(1)}, f32[80,4,128]{2,1,0:T(4,128)S(1)}, u32[]{:S(2)}, u32[]{:S(2)}) collective-permute-start(f32[80,4,128]{2,1,0:T(4,128)S(1)} %get-tuple-element.73), channel_id=1, source_target_pairs={{1,0},{2,1},{3,2},{4,3},{5,4},{6,5},{7,6},{0,7},{9,8},{10,9},{11,1... | collective-permute-start | bytes 491528 | tf_op jit(solution)/shard_map/ppermute | solution.py:461
  75.2 2.4 %shard_map.161 = (f32[64,16,128]{2,1,0:T(8,128)S(1)}, f32[64,16,128]{2,1,0:T(8,128)S(1)}) custom-call(f32[64,16,128]{2,1,0:T(8,128)S(1)} %get-tuple-element.63.now.u_one.old, f32[64,16,128]{2,1,0:T(8,128)S(1)} %bitcast.4, f32[64,16,128]{2,1,0:T(8,128)S(1)} %get-tuple-element.64.aniso_h), custom_call_target="tpu_custom_call" | custom-call | flops 5242880 | bytes 1572864 | tf_op jit(solution)/shard_map/pallas_call | solution.py:33
  77.7 1.0 collective-permute-done.3.low.low_s
  79.3 1.8 %shard_map.162 = (f32[64,16,128]{2,1,0:T(8,128)S(1)}, f32[16,2,16,128]{3,2,1,0:T(8,128)S(1)}, f32[16,2,16,128]{3,2,1,0:T(8,128)S(1)}) custom-call(s32[4]{0:T(128)S(1)} %copy-done.6, s32[1]{0:T(128)S(6)} %copy.19.src_cell, f32[1,3]{1,0:T(1,128)S(1)} %copy-done.8, f32[64,16,128]{2,1,0:T(8,128)S(1)} %get-tuple-element.63.now.u_one.old, ...), custom_call_target="tpu_custom_call" | custom-call | flops 10485760 | bytes 4005920 | tf_op jit(solution)/shard_map/pallas_call | solution.py:33
  81.1 1.8 %collective-permute-start.5 = (f32[16,2,16,128]{3,2,1,0:T(8,128)S(1)}, f32[16,2,16,128]{3,2,1,0:T(8,128)S(1)}, u32[]{:S(2)}, u32[]{:S(2)}) collective-permute-start(f32[16,2,16,128]{3,2,1,0:T(8,128)S(1)} %get-tuple-element.75), channel_id=1, source_target_pairs={{0,8},{8,0},{1,9},{9,1},{2,10},{10,2},{3,11},{11,3},{4,12},{12,4},... | collective-permute-start | bytes 786440 | tf_op jit(solution)/shard_map/ppermute | solution.py:568
  82.9 1.2 collective-permute-done.5
  84.1 14.6 %all_to_all.21.parts = f32[16,2,16,128]{3,2,1,0:T(8,128)S(1)} all-to-all(f32[16,2,16,128]{3,2,1,0:T(8,128)S(1)} %add.15), channel_id=1, replica_groups=mesh['xh'=2,'z'=8,'core'=2,'xl'=2,'y'=4] {'xh','z'}, dimensions={0} | all-to-all | bytes 524288 | tf_op jit(solution)/shard_map/all_to_all | solution.py:569
  98.7 14.6 %all_to_all.22.mine = f32[16,2,16,128]{3,2,1,0:T(8,128)S(1)} all-to-all(f32[16,2,16,128]{3,2,1,0:T(8,128)S(1)} %shard_map.163), channel_id=1, replica_groups=mesh['xh'=2,'z'=8,'core'=2,'xl'=2,'y'=4] {'xh','z'}, dimensions={0} | all-to-all | bytes 524288 | tf_op jit(solution)/shard_map/all_to_all | solution.py:571
  113.3 3.1 %collective-permute-start.6 = (f32[16,2,16,128]{3,2,1,0:T(8,128)S(1)}, f32[16,2,16,128]{3,2,1,0:T(8,128)S(1)}, u32[]{:S(2)}, u32[]{:S(2)}) collective-permute-start(f32[16,2,16,128]{3,2,1,0:T(8,128)S(1)} %all_to_all.22.mine), channel_id=1, source_target_pairs={{0,8},{8,0},{1,9},{9,1},{2,10},{10,2},{3,11},{11,3},{4,12},{12,4},... | collective-permute-start | bytes 786440 | tf_op jit(solution)/shard_map/ppermute | solution.py:572
  116.4 1.2 collective-permute-done.6.other
  117.6 0.7 shard_map.164
  118.4 3.6 %collective-permute-start.8 = (f32[96,4,128]{2,1,0:T(4,128)S(1)}, f32[96,4,128]{2,1,0:T(4,128)S(1)}, u32[]{:S(2)}, u32[]{:S(2)}) collective-permute-start(f32[96,4,128]{2,1,0:T(4,128)S(1)} %get-tuple-element.80), channel_id=1, source_target_pairs={{1,0},{2,1},{3,2},{4,3},{5,4},{6,5},{7,6},{0,7},{9,8},{10,9},{11,1... | collective-permute-start | bytes 589832 | tf_op jit(solution)/shard_map/ppermute | solution.py:461
  121.9 4.6 %collective-permute-done.7.low_g.low = f32[96,4,128]{2,1,0:T(4,128)S(1)} collective-permute-done((f32[96,4,128]{2,1,0:T(4,128)S(1)}, f32[96,4,128]{2,1,0:T(4,128)S(1)}, u32[]{:S(2)}, u32[]{:S(2)}) %collective-permute-start.7) | collective-permute-done | bytes 196640 | tf_op jit(solution)/shard_map/ppermute | solution.py:461
  126.6 4.7 %shard_map.165 = (f32[64,16,128]{2,1,0:T(8,128)S(1)}, f32[8,1,128]{2,1,0:T(1,128)}) custom-call(s32[4]{0:T(128)S(1)} %copy-done.6, f32[64,16,128]{2,1,0:T(8,128)S(1)} %get-tuple-element.77.summed, f32[64,16,128]{2,1,0:T(8,128)S(1)} %get-tuple-element.78.smooth, f32[96,4,128]{2,1,0:T(4,128)S(1)} %collective-permute-done.7.low_g.low, ...), custom_call_target="tpu_custom_call" | custom-call | flops 5242880 | bytes 1769488 | tf_op jit(solution)/shard_map/pallas_call | solution.py:33
  131.2 0.8 copy-done.2
  132.0 4.7 %all-to-all-start.3 = ((f32[8,1,128]{2,1,0:T(1,128)}), f32[8,1,128]{2,1,0:T(1,128)S(1)}, u32[]{:S(2)}, u32[]{:S(2)}) async-start(f32[8,1,128]{2,1,0:T(1,128)} %get-tuple-element.81), calls=%async_computation.3 | async-start | bytes 8192 | tf_op jit(solution)/shard_map/all_to_all | solution.py:594
  136.7 2.4 %shard_map.166 = (f32[64,16,128]{2,1,0:T(8,128)S(1)}, f32[64,16,128]{2,1,0:T(8,128)S(1)}) custom-call(f32[64,16,128]{2,1,0:T(8,128)S(1)} %get-tuple-element.76.u_two.now, f32[64,16,128]{2,1,0:T(8,128)S(1)} %get-tuple-element.63.now.u_one.old, f32[64,16,128]{2,1,0:T(8,128)S(1)} %get-tuple-element.64.aniso_h), custom_call_target="tpu_custom_call" | custom-call | flops 5242880 | bytes 1572864 | tf_op jit(solution)/shard_map/pallas_call | solution.py:33
  139.1 1.7 %shard_map.167 = (f32[64,16,128]{2,1,0:T(8,128)S(1)}, f32[64,16,128]{2,1,0:T(8,128)S(1)}) custom-call(s32[4]{0:T(128)S(1)} %copy-done.6, s32[1]{0:T(128)S(6)} %copy.19.src_cell, f32[1,3]{1,0:T(1,128)S(1)} %copy-done.8, f32[64,16,128]{2,1,0:T(8,128)S(1)} %get-tuple-element.76.u_two.now, f32[64,16,128]{2,1,0:T(8,128)S(1)} %get-tuple-element.83.base_in, ...), custom_call_target="tpu_custom_call" | custom-call | flops 10485760 | bytes 3014688 | tf_op jit(solution)/shard_map/pallas_call | solution.py:33
  140.8 0.8 copy-done.4
  141.6 1.0 copy-done.5
  142.7 1.7 %shard_map.168 = (f32[2,16,128]{2,1,0:T(8,128)}, f32[2,16,128]{2,1,0:T(8,128)}, f32[1,64,16,128]{3,2,1,0:T(8,128)}) custom-call(s32[4]{0:T(128)S(1)} %copy-done.6, f32[8,1,128]{2,1,0:T(1,128)S(1)} %all-to-all-done.3.squares, f32[64,16,128]{2,1,0:T(8,128)S(1)} %copy-done.3, f32[64,16,128]{2,1,0:T(8,128)S(1)} %get-tuple-element.70.model, ...), custom_call_target="tpu_custom_call" | custom-call | flops 2621440 | bytes 2101264 | tf_op jit(solution)/shard_map/pallas_call | solution.py:33
  (35 shorter events, 3.9 us)
Async XLA Ops:
  2.6 41.1 %copy-start = (f32[1,64,16,128]{3,2,1,0:T(8,128)S(1)}, f32[1,64,16,128]{3,2,1,0:T(8,128)}, u32[]{:S(2)}) copy-start(f32[1,64,16,128]{3,2,1,0:T(8,128)} %u_cur.1) | copy-start | bytes 1572868
  2.6 41.1 %copy-start.9 = (f32[1,64,16,128]{3,2,1,0:T(8,128)S(1)}, f32[1,64,16,128]{3,2,1,0:T(8,128)}, u32[]{:S(2)}) copy-start(f32[1,64,16,128]{3,2,1,0:T(8,128)} %refs_9_.1) | copy-start | bytes 1572868
  40.8 28.3 %collective-permute-start = (f32[16,4,2,16,128]{4,3,2,1,0:T(8,128)S(1)}, f32[16,4,2,16,128]{4,3,2,1,0:T(8,128)}, u32[]{:S(2)}, u32[]{:S(2)}) collective-permute-start(f32[16,4,2,16,128]{4,3,2,1,0:T(8,128)S(1)} %all_to_all.20.mine), channel_id=1, source_target_pairs={{0,8},{8,0},{1,9},{9,1},{2,10},{10,2},{3,11},{11,3},{4,12},{12,4},... | collective-permute-start | bytes 3145736 | tf_op jit(solution)/shard_map/ppermute | solution.py:535
  43.8 10.0 %collective-permute-start.1 = (f32[2,64,4,128]{3,2,1,0:T(4,128)S(1)}, f32[2,64,4,128]{3,2,1,0:T(4,128)S(1)}, u32[]{:S(2)}, u32[]{:S(2)}) collective-permute-start(f32[2,64,4,128]{3,2,1,0:T(4,128)S(1)} %pad_maximum_fusion), channel_id=1, source_target_pairs={{0,1},{1,2},{2,3},{3,4},{4,5},{5,6},{6,7},{7,0},{8,9},{9,10},{10,1... | collective-permute-start | bytes 786440 | tf_op jit(solution)/shard_map/ppermute | solution.py:461
  45.3 8.6 %collective-permute-start.2 = (f32[2,64,4,128]{3,2,1,0:T(4,128)S(1)}, f32[2,64,4,128]{3,2,1,0:T(4,128)S(1)}, u32[]{:S(2)}, u32[]{:S(2)}) collective-permute-start(f32[2,64,4,128]{3,2,1,0:T(4,128)S(1)} %pad_maximum_fusion.1), channel_id=1, source_target_pairs={{1,0},{2,1},{3,2},{4,3},{5,4},{6,5},{7,6},{0,7},{9,8},{10,9},{11,1... | collective-permute-start | bytes 786440 | tf_op jit(solution)/shard_map/ppermute | solution.py:461
  47.6 0.7 copy-start.12
  53.9 0.7 copy-start.10
  54.6 0.7 copy-start.11
  66.0 0.7 copy-start.7
  69.1 0.7 copy-start.6
  69.7 5.5 %copy-start.1 = (f32[1,64,16,128]{3,2,1,0:T(8,128)S(1)}, f32[1,64,16,128]{3,2,1,0:T(8,128)}, u32[]{:S(2)}) copy-start(f32[1,64,16,128]{3,2,1,0:T(8,128)} %u_cur.1) | copy-start | bytes 1572868
  71.6 7.1 %collective-permute-start.3 = (f32[80,4,128]{2,1,0:T(4,128)S(1)}, f32[80,4,128]{2,1,0:T(4,128)S(1)}, u32[]{:S(2)}, u32[]{:S(2)}) collective-permute-start(f32[80,4,128]{2,1,0:T(4,128)S(1)} %get-tuple-element.72), channel_id=1, source_target_pairs={{0,1},{1,2},{2,3},{3,4},{4,5},{5,6},{6,7},{7,0},{8,9},{9,10},{10,1... | collective-permute-start | bytes 491528 | tf_op jit(solution)/shard_map/ppermute | solution.py:461
  71.7 7.0 %collective-permute-start.4 = (f32[80,4,128]{2,1,0:T(4,128)S(1)}, f32[80,4,128]{2,1,0:T(4,128)S(1)}, u32[]{:S(2)}, u32[]{:S(2)}) collective-permute-start(f32[80,4,128]{2,1,0:T(4,128)S(1)} %get-tuple-element.73), channel_id=1, source_target_pairs={{1,0},{2,1},{3,2},{4,3},{5,4},{6,5},{7,6},{0,7},{9,8},{10,9},{11,1... | collective-permute-start | bytes 491528 | tf_op jit(solution)/shard_map/ppermute | solution.py:461
  78.7 0.7 copy-start.8
  81.1 3.0 %collective-permute-start.5 = (f32[16,2,16,128]{3,2,1,0:T(8,128)S(1)}, f32[16,2,16,128]{3,2,1,0:T(8,128)S(1)}, u32[]{:S(2)}, u32[]{:S(2)}) collective-permute-start(f32[16,2,16,128]{3,2,1,0:T(8,128)S(1)} %get-tuple-element.75), channel_id=1, source_target_pairs={{0,8},{8,0},{1,9},{9,1},{2,10},{10,2},{3,11},{11,3},{4,12},{12,4},... | collective-permute-start | bytes 786440 | tf_op jit(solution)/shard_map/ppermute | solution.py:568
  113.3 4.2 %collective-permute-start.6 = (f32[16,2,16,128]{3,2,1,0:T(8,128)S(1)}, f32[16,2,16,128]{3,2,1,0:T(8,128)S(1)}, u32[]{:S(2)}, u32[]{:S(2)}) collective-permute-start(f32[16,2,16,128]{3,2,1,0:T(8,128)S(1)} %all_to_all.22.mine), channel_id=1, source_target_pairs={{0,8},{8,0},{1,9},{9,1},{2,10},{10,2},{3,11},{11,3},{4,12},{12,4},... | collective-permute-start | bytes 786440 | tf_op jit(solution)/shard_map/ppermute | solution.py:572
  118.3 8.3 %collective-permute-start.7 = (f32[96,4,128]{2,1,0:T(4,128)S(1)}, f32[96,4,128]{2,1,0:T(4,128)S(1)}, u32[]{:S(2)}, u32[]{:S(2)}) collective-permute-start(f32[96,4,128]{2,1,0:T(4,128)S(1)} %get-tuple-element.79), channel_id=1, source_target_pairs={{0,1},{1,2},{2,3},{3,4},{4,5},{5,6},{6,7},{7,0},{8,9},{9,10},{10,1... | collective-permute-start | bytes 589832 | tf_op jit(solution)/shard_map/ppermute | solution.py:461
  118.4 8.2 %collective-permute-start.8 = (f32[96,4,128]{2,1,0:T(4,128)S(1)}, f32[96,4,128]{2,1,0:T(4,128)S(1)}, u32[]{:S(2)}, u32[]{:S(2)}) collective-permute-start(f32[96,4,128]{2,1,0:T(4,128)S(1)} %get-tuple-element.80), channel_id=1, source_target_pairs={{1,0},{2,1},{3,2},{4,3},{5,4},{6,5},{7,6},{0,7},{9,8},{10,9},{11,1... | collective-permute-start | bytes 589832 | tf_op jit(solution)/shard_map/ppermute | solution.py:461
  131.2 0.8 copy-start.2
  132.0 9.6 %all-to-all-start.3 = ((f32[8,1,128]{2,1,0:T(1,128)}), f32[8,1,128]{2,1,0:T(1,128)S(1)}, u32[]{:S(2)}, u32[]{:S(2)}) async-start(f32[8,1,128]{2,1,0:T(1,128)} %get-tuple-element.81), calls=%async_computation.3 | async-start | bytes 8192 | tf_op jit(solution)/shard_map/all_to_all | solution.py:594
  139.1 2.5 %copy-start.3 = (f32[64,16,128]{2,1,0:T(8,128)S(1)}, f32[64,16,128]{2,1,0:T(8,128)}, u32[]{:S(2)}) copy-start(f32[64,16,128]{2,1,0:T(8,128)} %copy-done.2) | copy-start | bytes 1572868
  140.8 0.8 copy-start.4
  141.6 1.0 copy-start.5

commit v4 on v3

--- a/solution.py
+++ b/solution.py
@@ -1,3 +1,5 @@
+import functools
+
 import jax
 import jax.numpy as jnp
 from jax import lax
@@ -43,6 +45,12 @@
     )(*args)
 
 
+def position():
+    layer = lax.axis_index("xl") * lax.axis_size("y") + lax.axis_index("y")
+    chip = lax.axis_index("xh") * lax.axis_size("z") + lax.axis_index("z")
+    return layer, lax.axis_index("core"), chip
+
+
 def fill_rows(rows, read):
     cells_x = rows.shape[0] - 2 * REACH
     zeros = jnp.zeros((REACH, *rows.shape[1:]), jnp.float32)
@@ -55,10 +63,19 @@
         rows[pl.ds(REACH + x, CHUNK)] = read(pl.ds(x, CHUNK))
 
 
-def fill_depth(pad, place, read, low, high):
+def has_sides():
+    layer, _, _ = position()
+    return layer > 0, layer < lax.axis_size("xl") * lax.axis_size("y") - 1
+
+
+def depth_range(cells_z):
+    layer, _, _ = position()
+    return layer * cells_z, cells_z * lax.axis_size("xl") * lax.axis_size("y")
+
+
+def fill_depth(pad, read, low, high):
     cells_x, cells_z = pad.shape[0], pad.shape[1] - 2 * MID
-    below = place[0] > 0
-    above = place[0] + cells_z < place[1]
+    below, above = has_sides()
 
     @pl.loop(0, cells_x // CHUNK)
     def _(step):
@@ -121,8 +138,9 @@
     return total
 
 
-def add_at(ref, cell, amount, z_start, depth_cells):
+def add_at(ref, cell, amount):
     cells_z, cells_y = ref.shape[1], ref.shape[2]
+    z_start, depth_cells = depth_range(cells_z)
     row = cell // cells_y
     x, z = row // depth_cells, row % depth_cells - z_start
 
@@ -147,8 +165,9 @@
         send.wait()
 
 
-def place_receivers(out, rec_cell, rec_data, z_start, depth_cells):
+def place_receivers(out, rec_cell, rec_data):
     cells_x, cells_z, cells_y = out.shape
+    z_start, depth_cells = depth_range(cells_z)
     cell = rec_cell[...]
     row = cell // cells_y
     z = row % depth_cells - z_start
@@ -182,7 +201,7 @@
 
 
 def open_kernel(
-    place, src_cell, src_wave, onehot, shot_group, rec_cell, rec_data,
+    src_cell, src_wave, onehot, shot_group, rec_cell, rec_data,
     u_prev, u_cur, a_prev, a_cur, low, high,
     base_u, lat_u, dep_u, cross_u, base_a, lat_a, dep_a, cross_a, weight,
     old, now, base, lat, dep, cross, scale_row, rows, pad, first_z, sem_in, sem_out,
@@ -203,14 +222,14 @@
         sends.append(copy)
 
     blocks = onehot.shape[1]
-    position = lax.broadcasted_iota(jnp.int32, weight.shape, 1)
+    depth = lax.broadcasted_iota(jnp.int32, weight.shape, 1)
     value = jnp.zeros(weight.shape, jnp.float32)
     for block in range(blocks):
         scale = sum(
             onehot[shot_group[0], block, b].astype(jnp.float32) * 2.0 ** (-b)
             for b in range(onehot.shape[2])
         )
-        value = jnp.where(position // (cells_z // blocks) == block, scale, value)
+        value = jnp.where(depth // (cells_z // blocks) == block, scale, value)
     scale_row[...] = value
     send(scale_row, weight)
 
@@ -220,7 +239,6 @@
         loads[2 * j + 1].wait()
         fill_depth(
             pad,
-            place,
             lambda at, j=j: now[j, at],
             lambda at, j=j: low[j, at],
             lambda at, j=j: high[j, at],
@@ -240,9 +258,9 @@
         send(lat.at[j], targets[j][1])
         send(cross.at[j], targets[j][3])
         if j == 0:
-            add_at(base.at[0], src_cell[0], src_wave[0, 0], place[0], place[1])
+            add_at(base.at[0], src_cell[0], src_wave[0, 0])
         else:
-            place_receivers(base.at[1], rec_cell, rec_data, place[0], place[1])
+            place_receivers(base.at[1], rec_cell, rec_data)
         send(base.at[j], targets[j][0])
     for copy in sends:
         copy.wait()
@@ -262,12 +280,12 @@
 
 
 def first_kernel(
-    place, mine, other, a_cur,
+    mine, other, a_cur,
     base_u, lat_u, dep_u, cross_u, base_a, lat_a, dep_a, cross_a,
     u_one, a_one, grad, model, aniso_h, aniso_c, smooth, low, high,
 ):
     cells_x, cells_z, _ = u_one.shape
-    own = place[2] == 0
+    own = position()[1] == 0
 
     @pl.loop(0, mine.shape[0])
     def _(q):
@@ -289,7 +307,7 @@
             high[edge] = s[:, cells_z - 1][None]
 
 
-def side_kernel(now, old, aniso_h, base, side, rows):
+def side_kernel(step_index, src_cell, src_wave, now, old, aniso_h, base, side, rows):
     cells_x, _, cells_y = base.shape
     masks = lateral_masks(cells_y)
     fill_rows(rows, lambda at: now[at])
@@ -301,16 +319,17 @@
         base[at] = 2.0 * now[at] - old[at]
         side[at] = aniso_h[at] * lateral(rows, x, masks)
 
+    add_at(base, src_cell[0], src_wave[0, step_index])
+
 
 def second_kernel(
-    place, src_cell, src_wave,
     u_one, base, side, a_one, grad, weight, model, aniso_c, low, high,
     u_two, keep, send, pad, first_z, dep,
 ):
-    cells_x, _, _ = u_two.shape
-    fill_depth(pad, place, lambda at: u_one[at], lambda at: low[at], lambda at: high[at])
+    cells_x = u_two.shape[0]
+    fill_depth(pad, lambda at: u_one[at], lambda at: low[at], lambda at: high[at])
     depth_pass(pad, first_z, dep)
-    own = place[2] == 0
+    own = position()[1] == 0
 
     @pl.loop(0, cells_x // CHUNK)
     def _(step):
@@ -322,8 +341,6 @@
         keep[step] = jnp.where(own, total[:2], total[2:])
         send[step] = jnp.where(own, total[2:], total[:2])
 
-    add_at(u_two, src_cell[0], src_wave[0, 1], place[0], place[1])
-
 
 def sum_kernel(parts, out):
     total = parts[0]
@@ -333,11 +350,12 @@
         out[peer] = total
 
 
-def join_kernel(place, mine, other, u_two, summed, low, high):
+def join_kernel(mine, other, u_two, summed, low, high):
     cells_x, cells_z, _ = summed.shape
-    own = place[2] == 0
-
-    @pl.loop(0, mine.shape[0])
+    count = mine.shape[0]
+    own = position()[1] == 0
+
+    @pl.loop(0, count)
     def _(q):
         for p in range(2):
             rows = pl.ds(q * 4 + p * 2, 2)
@@ -345,96 +363,142 @@
             summed[rows] = g
             low[rows] = u_two[rows, :REACH]
             high[rows] = u_two[rows, cells_z - REACH :]
-            for r in range(2):
-                edge = (pl.ds(cells_x + 2 * q + p, 1), pl.ds(2 * r, 2), slice(None))
-                low[edge] = g[r, :2][None]
-                high[edge] = g[r, cells_z - 2 :][None]
-
-
-SM = 16
-
-
-def relax_kernel(place, summed, smooth, low_g, high_g, low_s, high_s, out, square, wide, once, coef):
+            for k in range(2):
+                edge = (pl.ds(cells_x + k * count + q, 1), pl.ds(2 * p, 2), slice(None))
+                low[edge] = g[:, k][None]
+                high[edge] = g[:, cells_z - 1 - k][None]
+
+
+def shifted_y(flat):
+    cells_y = flat.shape[-1]
+    lane = lax.broadcasted_iota(jnp.int32, (1,) * (flat.ndim - 2) + (8, cells_y), flat.ndim - 1)
+    axis = flat.ndim - 1
+    if flat.ndim == 2:
+        lane = lax.broadcasted_iota(jnp.int32, flat.shape, 1)
+    right = jnp.where(lane < cells_y - 1, pltpu.roll(flat, cells_y - 1, axis), 0.0)
+    left = jnp.where(lane >= 1, pltpu.roll(flat, 1, axis), 0.0)
+    return right + left
+
+
+def relax_kernel(summed, smooth, out, inner, own_g, own_s, own_out, wide, once):
     cells_x, cells_z, cells_y = summed.shape
-    tall = wide.shape[1]
-    below = place[0] > 0
-    above = place[0] + cells_z < place[1]
-    zero_row = jnp.zeros((1, tall, cells_y), jnp.float32)
     for ref in (wide, once):
-        ref[pl.ds(0, 1)] = zero_row
-        ref[pl.ds(cells_x + 1, 1)] = zero_row
+        blank = jnp.zeros((1, *ref.shape[1:]), jnp.float32)
+        ref[pl.ds(0, 1)] = blank
+        ref[pl.ds(cells_x + 1, 1)] = blank
 
     @pl.loop(0, cells_x // CHUNK)
     def _(q):
-        for ref, shift in ((wide, 1), (coef, 0)):
-            zero = jnp.zeros((CHUNK, 8, cells_y), jnp.float32)
-            for tile in (0, 8, SM + cells_z, SM + cells_z + 8):
-                ref[pl.ds(q * CHUNK + shift, CHUNK), pl.ds(tile, 8), :] = zero
-        for j in range(CHUNK):
-            x = q * CHUNK + j
-            halo = (pl.ds(cells_x + 2 * q + j // 2, 1), pl.ds(2 * (j % 2), 2), slice(None))
-            wide[pl.ds(x + 1, 1), pl.ds(SM, cells_z), :] = summed[pl.ds(x, 1)]
-            wide[pl.ds(x + 1, 1), pl.ds(SM - 2, 2), :] = jnp.where(below, low_g[halo], 0.0)
-            wide[pl.ds(x + 1, 1), pl.ds(SM + cells_z, 2), :] = jnp.where(above, high_g[halo], 0.0)
-            edge = (pl.ds(cells_x + q, 1), pl.ds(j, 1), slice(None))
-            coef[pl.ds(x, 1), pl.ds(SM, cells_z), :] = smooth[pl.ds(x, 1)]
-            coef[pl.ds(x, 1), pl.ds(SM - 1, 1), :] = jnp.where(below, low_s[edge], 0.0)
-            coef[pl.ds(x, 1), pl.ds(SM + cells_z, 1), :] = jnp.where(above, high_s[edge], 0.0)
-
-    lane = lax.broadcasted_iota(jnp.int32, (1, 8, cells_y), 2)
-
-    def relaxed(ref, x, start, count, factor):
-        at = lambda dx, dz: ref[pl.ds(x + 1 + dx, CHUNK), pl.ds(start + dz, count), :]
+        at = pl.ds(q * CHUNK + 1, CHUNK)
+        blank = jnp.zeros((CHUNK, 1, cells_y), jnp.float32)
+        for ref in (wide, once):
+            ref[at, pl.ds(MID - 1, 1), :] = blank
+            ref[at, pl.ds(MID + cells_z, 1), :] = blank
+        wide[at, pl.ds(MID, cells_z), :] = summed[pl.ds(q * CHUNK, CHUNK)]
+
+    def relaxed(ref, x, factor):
+        at = lambda dx, dz: ref[pl.ds(x + 1 + dx, CHUNK), pl.ds(MID + dz, cells_z), :]
         v = at(0, 0)
         near = at(1, 0) + at(-1, 0) + at(0, 1) + at(0, -1)
-        flat = v.reshape(CHUNK * count // 8, 8, cells_y)
-        right = jnp.where(lane < cells_y - 1, pltpu.roll(flat, cells_y - 1, 2), 0.0)
-        left = jnp.where(lane >= 1, pltpu.roll(flat, 1, 2), 0.0)
-        near = near + (right + left).reshape(v.shape)
+        flat = v.reshape(CHUNK * cells_z // 8, 8, cells_y)
+        near = near + shifted_y(flat).reshape(v.shape)
         return v + factor * (near - 6.0 * v)
 
     @pl.loop(0, cells_x // CHUNK)
     def _(q):
         x = q * CHUNK
-        once[pl.ds(x + 1, CHUNK), pl.ds(8, cells_z + 16), :] = relaxed(
-            wide, x, 8, cells_z + 16, coef[pl.ds(x, CHUNK), pl.ds(8, cells_z + 16), :]
-        )
+        factor = smooth[pl.ds(x, CHUNK)]
+        once[pl.ds(x + 1, CHUNK), pl.ds(MID, cells_z), :] = relaxed(wide, x, factor)
+        g = summed[pl.ds(x, CHUNK)]
+        for i, k in enumerate((0, cells_z - 1)):
+            own_g[i, pl.ds(x, CHUNK)] = g[:, k]
+        for i, k in enumerate((0, 1, cells_z - 2, cells_z - 1)):
+            own_s[i, pl.ds(x, CHUNK)] = factor[:, k]
+
+    depth = lax.broadcasted_iota(jnp.int32, (1, cells_z, cells_y), 1)
+    between = (depth >= 2) & (depth < cells_z - 2)
 
     def sweep(q, total):
         x = q * CHUNK
-        value = relaxed(once, x, SM, cells_z, smooth[pl.ds(x, CHUNK)])
+        value = relaxed(once, x, smooth[pl.ds(x, CHUNK)])
         out[pl.ds(x, CHUNK)] = value
-        squares = (value * value).reshape(CHUNK * cells_z // 8, 8, cells_y)
-        return total + jnp.sum(squares, axis=0)
-
-    total = lax.fori_loop(0, cells_x // CHUNK, sweep, jnp.zeros((8, cells_y), jnp.float32))
+        for i, k in enumerate((0, 1, cells_z - 2, cells_z - 1)):
+            own_out[i, pl.ds(x, CHUNK)] = value[:, k]
+        squares = jnp.where(between, value * value, 0.0)
+        return total + jnp.sum(squares.reshape(CHUNK * cells_z // 8, 8, cells_y), axis=0)
+
+    inner[...] = lax.fori_loop(
+        0, cells_x // CHUNK, sweep, jnp.zeros((8, cells_y), jnp.float32)
+    )
+
+
+def edge_kernel(
+    smoothed_in, inner, own_g, own_s, own_out, low_two, high_two, low_one, high_one,
+    smoothed, square, planes,
+):
+    cells_x, cells_z, cells_y = smoothed.shape
+    smoothed[...] = smoothed_in[...]
+    count = cells_x // 4
+    blank = jnp.zeros((8, cells_y), jnp.float32)
+    total = inner[...]
+    for side, (sums, smooth, present) in enumerate(
+        ((low_two, low_one, has_sides()[0]), (high_two, high_one, has_sides()[1]))
+    ):
+        for k in range(4):
+            planes[k, pl.ds(0, 8)] = blank
+            planes[k, pl.ds(8 + cells_x, 8)] = blank
+
+        @pl.loop(0, count)
+        def _(q, sums=sums, smooth=smooth, present=present):
+            at = pl.ds(8 + 4 * q, 4)
+            for k in range(2):
+                planes[k, at] = jnp.where(present, sums[cells_x + k * count + q], 0.0)
+            planes[2, at] = jnp.where(present, smooth[cells_x + q], 0.0)
+
+        def near(k):
+            at = lambda dx: planes[k, pl.ds(8 + dx, cells_x)]
+            return at(1) + at(-1) + shifted_y(at(0))
+
+        whole = pl.ds(8, cells_x)
+        first, second, factor = planes[0, whole], planes[1, whole], planes[2, whole]
+        outside = first + factor * (near(0) + second + own_g[side] - 6.0 * first)
+        edge, inside = (0, 1) if side == 0 else (3, 2)
+        change = own_s[edge] * first
+        planes[3, whole] = change
+        value = own_out[edge] + change + own_s[edge] * (near(3) - 6.0 * change + outside)
+        beside = own_out[inside] + own_s[inside] * change
+        squares = value * value + beside * beside
+        total = total + jnp.sum(squares.reshape(cells_x // 8, 8, cells_y), axis=0)
+        planes[0, whole] = value
+        planes[1, whole] = beside
+        rows = (0, 1) if side == 0 else (cells_z - 1, cells_z - 2)
+
+        @pl.loop(0, count)
+        def _(q, rows=rows):
+            for k, z in enumerate(rows):
+                smoothed[pl.ds(4 * q, 4), pl.ds(z, 1), :] = planes[k, pl.ds(8 + 4 * q, 4)][:, None]
+
     row = jnp.sum(total, axis=0, keepdims=True)
     square[...] = jnp.broadcast_to(row[None], square.shape)
 
 
-def third_kernel(
-    place, src_cell, src_wave, u_two, base_in, side, model, aniso_c, low, high,
-    base, change, pad, first_z, dep,
-):
-    cells_x = base.shape[0]
-    fill_depth(pad, place, lambda at: u_two[at], lambda at: low[at], lambda at: high[at])
+def third_kernel(u_two, side, model, aniso_c, low, high, change, pad, first_z, dep):
+    cells_x = change.shape[0]
+    fill_depth(pad, lambda at: u_two[at], lambda at: low[at], lambda at: high[at])
     depth_pass(pad, first_z, dep)
 
     @pl.loop(0, cells_x // CHUNK)
     def _(step):
         x = step * CHUNK
         at = pl.ds(x, CHUNK)
-        base[at] = base_in[at]
         change[at] = model[at] * (side[at] + dep[at] + aniso_c[at] * crossing(first_z, x))
 
-    add_at(base, src_cell[0], src_wave[0, 2], place[0], place[1])
-
-
-def close_kernel(place, squares, smoothed, model, base, change, model_next, grad_dir, wave_next):
+
+def close_kernel(squares, smoothed, model, base, change, model_next, grad_dir, wave_next):
     cells_x, cells_z, cells_y = smoothed.shape
     rows = grad_dir.shape[0]
     total = jnp.sum(jnp.sum(squares[...], axis=0), axis=1, keepdims=True)
-    cells = (cells_x * place[1] * cells_y).astype(jnp.float32)
+    cells = cells_x * depth_range(cells_z)[1] * cells_y
     scale = lax.rsqrt(total / cells + 1e-06)
     scale = jnp.broadcast_to(scale, (8, cells_y))[None]
 
@@ -448,7 +512,8 @@
         shrink = 1.0 - 0.25 * jnp.tanh(factor(smoothed[at]))
         wave_next[0, at] = base[at] + change[at] * shrink
 
-    at = pl.ds(place[3], rows)
+    _, core, chip = position()
+    at = pl.ds((2 * chip + core) * rows, rows)
     direction = factor(smoothed[at])
     grad_dir[...] = direction
     model_next[...] = model[at] * (1.0 - 0.25 * jnp.tanh(direction))
@@ -481,15 +546,6 @@
     rows = model.shape[0]
     peers = lax.axis_size(PEERS)
     slab = f32(cells_x, cells_z, cells_y)
-    depth_cells = cells_z * lax.axis_size(DEPTH)
-    place = jnp.stack(
-        [
-            lax.axis_index(DEPTH) * cells_z,
-            jnp.int32(depth_cells),
-            lax.axis_index("core"),
-            lax.axis_index(SHOT) * rows,
-        ]
-    )
     scratch = lambda *shape: pltpu.VMEM(shape, jnp.float32)
     pad = scratch(cells_x, cells_z + 2 * MID, cells_y)
     first_z = scratch(cells_x + 2 * REACH, cells_z, cells_y)
@@ -520,15 +576,15 @@
     low, high = shift(edges(0), edges(cells_z - REACH))
     *parts, weight = call(
         open_kernel,
-        (place, src_cell, src_wave, bin_onehot, shot_group, rec_cell, rec_data)
+        (src_cell, src_wave, bin_onehot, shot_group, rec_cell, rec_data)
         + (u_prev, u_cur, a_prev, a_cur, low, high),
-        5,
+        4,
         (slab,) * 8 + (f32(1, cells_z, cells_y),),
         (pair,) * 6
         + (scratch(1, cells_z, cells_y), padded_rows, pad, first_z)
         + (pltpu.SemaphoreType.DMA((2, 2)), pltpu.SemaphoreType.DMA((9,))),
         2 * work,
-        hbm_in=range(7, 11),
+        hbm_in=range(6, 10),
         hbm_out=range(9),
         grant=61,
     )
@@ -545,22 +601,26 @@
     payload = f32(cells_x + peers, REACH, cells_y)
     u_one, a_one, grad, model_slab, h_slab, c_slab, smooth_slab, low_edge, high_edge = call(
         first_kernel,
-        (place, mine, other, adjoint, *parts),
-        1,
+        (mine, other, adjoint, *parts),
+        0,
         (slab,) * 7 + (payload, payload),
         (),
         20 * slab.size,
     )
     low_one, high_one = shift(low_edge, high_edge)
     base, side = call(
-        side_kernel, (u_one, u_cur[0], h_slab), 0, (slab, slab), (padded_rows,), work // 2
+        functools.partial(side_kernel, 1),
+        (src_cell, src_wave, u_one, u_cur[0], h_slab),
+        2,
+        (slab, slab),
+        (padded_rows,),
+        work // 2,
     )
     split = f32(peers, rows, cells_z, cells_y)
     u_two, keep, send = call(
         second_kernel,
-        (place, src_cell, src_wave)
-        + (u_one, base, side, a_one, grad, weight, model_slab, c_slab, low_one, high_one),
-        3,
+        (u_one, base, side, a_one, grad, weight, model_slab, c_slab, low_one, high_one),
+        0,
         (slab, split, split),
         (pad, first_z, dep),
         work,
@@ -572,40 +632,48 @@
     other = lax.ppermute(mine, "core", SWAP)
     payload = f32(cells_x + 2 * peers, REACH, cells_y)
     summed, low_edge, high_edge = call(
-        join_kernel, (place, mine, other, u_two), 1, (slab, payload, payload)
+        join_kernel, (mine, other, u_two), 0, (slab, payload, payload)
     )
     low_two, high_two = shift(low_edge, high_edge)
     base, side = call(
-        side_kernel, (u_two, u_one, h_slab), 0, (slab, slab), (padded_rows,), work // 2
-    )
-    tall = cells_z + 2 * SM
-    smoothed, square = call(
+        functools.partial(side_kernel, 2),
+        (src_cell, src_wave, u_two, u_one, h_slab),
+        2,
+        (slab, slab),
+        (padded_rows,),
+        work // 2,
+    )
+    edges = f32(4, cells_x, cells_y)
+    smoothed, inner, own_g, own_s, own_out = call(
         relax_kernel,
-        (place, summed, smooth_slab, low_two, high_two, low_one, high_one),
-        1,
-        (slab, f32(lax.axis_size(DEPTH), 1, cells_y)),
-        (
-            pltpu.VMEM((cells_x + 2, tall, cells_y), jnp.float32),
-            pltpu.VMEM((cells_x + 2, tall, cells_y), jnp.float32),
-            pltpu.VMEM((cells_x, tall, cells_y), jnp.float32),
-        ),
+        (summed, smooth_slab),
+        0,
+        (slab, f32(8, cells_y), f32(2, cells_x, cells_y), edges, edges),
+        (scratch(cells_x + 2, cells_z + 2 * MID, cells_y),) * 2,
         40 * slab.size,
     )
-    squares = lax.all_to_all(square, DEPTH, 0, 0, tiled=True)
-    base, change = call(
+    change = call(
         third_kernel,
-        (place, src_cell, src_wave)
-        + (u_two, base, side, model_slab, c_slab, low_two, high_two),
-        3,
-        (slab, slab),
+        (u_two, side, model_slab, c_slab, low_two, high_two),
+        0,
+        slab,
         (pad, first_z, dep),
         work,
     )
+    smoothed, square = call(
+        edge_kernel,
+        (smoothed, inner, own_g, own_s, own_out, low_two, high_two, low_one, high_one),
+        0,
+        (slab, f32(lax.axis_size(DEPTH), 1, cells_y)),
+        (scratch(4, cells_x + 16, cells_y),),
+        4 * slab.size,
+    )
+    squares = lax.all_to_all(square, DEPTH, 0, 0, tiled=True)
     share = f32(rows, cells_z, cells_y)
     return call(
         close_kernel,
-        (place, squares, smoothed, model_slab, base, change),
-        1,
+        (squares, smoothed, model_slab, base, change),
+        0,
         (share, share, f32(1, cells_x, cells_z, cells_y)),
         (),
         20 * slab.size,

time: 146 us -> 140 us (0.959)
  waiting for transfers between devices: 11.6 us -> 8.19 us
  Pallas kernels: 32.2 us -> 30.6 us
    ppermute x3, waiting for transfers between devices: 9.19 us -> 5.75 us  [shift(): lax.ppermute(high_edge, DEPTH, forward)]
    pallas_call x12 -> x13, Pallas kernels: 32.2 us -> 30.6 us  [call(): pl.pallas_call(kernel, out_shape=outs, in_specs=[spec(i) for i in range(l...]
    unnamed x27 -> x25, local copies, waits for them, and re-layouts: 6.78 us -> 6.14 us
  transfers between devices with their start and end apart: 10 -> 10, of which waited for: 5 -> 5; matrix products, arithmetic and copies ran while one was open for 1% -> 1% of each run, Pallas kernels for 14% -> 17%
where the time goes in v4:
time: 140 us; the launch traced here: 138 us
  blocking collectives  67.4 us (48%)
  Pallas kernels  30.6 us (22%)
  starting transfers between devices  23.1 us (16%)
  waiting for transfers between devices  8.19 us (6%)
  local copies, waits for them, and re-layouts  6.23 us (4%)
  between operations  2.13 us (2%)
    all_to_all x1, blocking collectives, body(): mine = lax.all_to_all(spread, PEERS, 0, 0, tiled=True)  38.2 us
    pallas_call x13, Pallas kernels, call(): pl.pallas_call(kernel, out_shape=outs, in_specs=[spec(i) for i in range(l...  30.6 us
    all_to_all x1, blocking collectives, body(): mine = lax.all_to_all(total, PEERS, 0, 0, tiled=True)  14.6 us
    all_to_all x1, blocking collectives, body(): shares = lax.all_to_all(chip_sum, PEERS, 0, 0, tiled=True)  14.6 us
    ppermute x3, starting transfers between devices, shift(): lax.ppermute(low_edge, DEPTH, backward)  9.48 us
    unnamed x25, local copies, waits for them, and re-layouts  6.14 us
    ppermute x2, starting transfers between devices, body(): other = lax.ppermute(mine, 'core', SWAP)  5.9 us
    ppermute x3, waiting for transfers between devices, shift(): lax.ppermute(high_edge, DEPTH, forward)  5.75 us
  transfers between devices with their start and end apart: 10, of which 5 were waited for; matrix products, arithmetic and copies ran while one was open for 1% of the time, Pallas kernels for 17%

profile of v4, /device:TPU:1, one launch (start us, length us, event | category | flops | bytes accessed | tf_op | source)
XLA Modules:
  0.0 137.9 jit_solution(16696603279257094691)
XLA Ops:
  0.6 1.9 %shard_map.157 = f32[16,4,2,16,128]{4,3,2,1,0:T(8,128)} custom-call(f32[2,16,128]{2,1,0:T(8,128)} %model.1, f32[2,16,128]{2,1,0:T(8,128)} %aniso_h.1, f32[2,16,128]{2,1,0:T(8,128)} %aniso_c.1, f32[2,16,128]{2,1,0:T(8,128)} %smooth.1), custom_call_target="tpu_custom_call" | custom-call | bytes 65536 | tf_op jit(solution)/shard_map/pallas_call | solution.py:35
  2.6 38.2 %all_to_all.20.mine = f32[16,4,2,16,128]{4,3,2,1,0:T(8,128)S(1)} all-to-all(f32[16,4,2,16,128]{4,3,2,1,0:T(8,128)} %shard_map.157), channel_id=1, replica_groups=mesh['xh'=2,'z'=8,'core'=2,'xl'=2,'y'=4] {'xh','z'}, dimensions={0} | all-to-all | bytes 2097152 | tf_op jit(solution)/shard_map/all_to_all | solution.py:571
  40.8 2.8 %collective-permute-start = (f32[16,4,2,16,128]{4,3,2,1,0:T(8,128)S(1)}, f32[16,4,2,16,128]{4,3,2,1,0:T(8,128)}, u32[]{:S(2)}, u32[]{:S(2)}) collective-permute-start(f32[16,4,2,16,128]{4,3,2,1,0:T(8,128)S(1)} %all_to_all.20.mine), channel_id=1, source_target_pairs={{0,8},{8,0},{1,9},{9,1},{2,10},{10,2},{3,11},{11,3},{4,12},{12,4},... | collective-permute-start | bytes 3145736 | tf_op jit(solution)/shard_map/ppermute | solution.py:591
  43.8 1.4 collective-permute-start.1
  45.3 2.4 %collective-permute-start.2 = (f32[2,64,4,128]{3,2,1,0:T(4,128)S(1)}, f32[2,64,4,128]{3,2,1,0:T(4,128)S(1)}, u32[]{:S(2)}, u32[]{:S(2)}) collective-permute-start(f32[2,64,4,128]{3,2,1,0:T(4,128)S(1)} %pad_maximum_fusion.1), channel_id=1, source_target_pairs={{1,0},{2,1},{3,2},{4,3},{5,4},{6,5},{7,6},{0,7},{9,8},{10,9},{11,1... | collective-permute-start | bytes 786440 | tf_op jit(solution)/shard_map/ppermute | solution.py:526
  48.3 0.7 copy.17.onehot
  49.6 4.2 %collective-permute-done.1.low = f32[2,64,4,128]{3,2,1,0:T(4,128)S(1)} collective-permute-done((f32[2,64,4,128]{3,2,1,0:T(4,128)S(1)}, f32[2,64,4,128]{3,2,1,0:T(4,128)S(1)}, u32[]{:S(2)}, u32[]{:S(2)}) %collective-permute-start.1) | collective-permute-done | bytes 262176 | tf_op jit(solution)/shard_map/ppermute | solution.py:526
  53.9 0.7 copy-done.9
  54.6 0.7 copy-done.10
  55.3 10.5 %shard_map.158 = (f32[64,16,128]{2,1,0:T(8,128)}, f32[64,16,128]{2,1,0:T(8,128)}, f32[64,16,128]{2,1,0:T(8,128)}, f32[64,16,128]{2,1,0:T(8,128)}, f32[64,16,128]...) custom-call(s32[1]{0:T(128)S(6)} %copy.19.src_cell, ...), custom_call_target="tpu_custom_call" | custom-call | flops 20971520 | bytes 2623508 | tf_op jit(solution)/shard_map/pallas_call | solution.py:35
  66.6 2.4 %shard_map.159 = (f32[64,16,128]{2,1,0:T(8,128)S(1)}, f32[64,16,128]{2,1,0:T(8,128)S(1)}, f32[64,16,128]{2,1,0:T(8,128)S(1)}, f32[64,16,128]{2,1,0:T(8,128)S(1)}...) custom-call(f32[64,16,128]{2,1,0:T(8,128)} %get-tuple-element.48.ref, ...), custom_call_target="tpu_custom_call" | custom-call | bytes 4726784 | tf_op jit(solution)/shard_map/pallas_call | solution.py:35
  69.0 1.8 %shard_map.160 = (f32[64,16,128]{2,1,0:T(8,128)S(1)}, f32[64,16,128]{2,1,0:T(8,128)S(1)}, f32[64,16,128]{2,1,0:T(8,128)S(1)}, f32[64,16,128]{2,1,0:T(8,128)S(1)}...) custom-call(f32[16,4,2,16,128]{4,3,2,1,0:T(8,128)S(1)} %all_to_all.2, ...), custom_call_target="tpu_custom_call" | custom-call | flops 2621440 | bytes 6815744 | tf_op jit(solution)/shard_map/pallas_call | solution.py:35
  70.9 3.6 %collective-permute-start.4 = (f32[80,4,128]{2,1,0:T(4,128)S(1)}, f32[80,4,128]{2,1,0:T(4,128)S(1)}, u32[]{:S(2)}, u32[]{:S(2)}) collective-permute-start(f32[80,4,128]{2,1,0:T(4,128)S(1)} %get-tuple-element.76), channel_id=1, source_target_pairs={{1,0},{2,1},{3,2},{4,3},{5,4},{6,5},{7,6},{0,7},{9,8},{10,9},{11,1... | collective-permute-start | bytes 491528 | tf_op jit(solution)/shard_map/ppermute | solution.py:526
  75.1 3.0 %shard_map.161 = (f32[64,16,128]{2,1,0:T(8,128)S(1)}, f32[64,16,128]{2,1,0:T(8,128)S(1)}) custom-call(s32[1]{0:T(128)S(6)} %copy.19.src_cell, f32[1,3]{1,0:T(1,128)S(1)} %copy-done.7, f32[64,16,128]{2,1,0:T(8,128)S(1)} %get-tuple-element.66.now.u_one.old, f32[64,16,128]{2,1,0:T(8,128)S(1)} %bitcast.1, f32[64,16,128]{2,1,0:T(8,128)S(1)} %get-tuple-element.67.aniso_h), custom_call_target="tpu_custom_call" | custom-call | flops 5242880 | bytes 1572880 | tf_op jit(solution)/shard_map/pallas_call | solution.py:35
  78.1 1.2 shard_map.162
  79.3 1.6 %collective-permute-start.5 = (f32[16,2,16,128]{3,2,1,0:T(8,128)S(1)}, f32[16,2,16,128]{3,2,1,0:T(8,128)S(1)}, u32[]{:S(2)}, u32[]{:S(2)}) collective-permute-start(f32[16,2,16,128]{3,2,1,0:T(8,128)S(1)} %get-tuple-element.78), channel_id=1, source_target_pairs={{0,8},{8,0},{1,9},{9,1},{2,10},{10,2},{3,11},{11,3},{4,12},{12,4},... | collective-permute-start | bytes 786440 | tf_op jit(solution)/shard_map/ppermute | solution.py:628
  80.9 1.2 collective-permute-done.5
  82.1 14.6 %all_to_all.21.parts = f32[16,2,16,128]{3,2,1,0:T(8,128)S(1)} all-to-all(f32[16,2,16,128]{3,2,1,0:T(8,128)S(1)} %add.3), channel_id=1, replica_groups=mesh['xh'=2,'z'=8,'core'=2,'xl'=2,'y'=4] {'xh','z'}, dimensions={0} | all-to-all | bytes 524288 | tf_op jit(solution)/shard_map/all_to_all | solution.py:629
  96.7 14.6 %all_to_all.22.mine = f32[16,2,16,128]{3,2,1,0:T(8,128)S(1)} all-to-all(f32[16,2,16,128]{3,2,1,0:T(8,128)S(1)} %shard_map.163), channel_id=1, replica_groups=mesh['xh'=2,'z'=8,'core'=2,'xl'=2,'y'=4] {'xh','z'}, dimensions={0} | all-to-all | bytes 524288 | tf_op jit(solution)/shard_map/all_to_all | solution.py:631
  111.3 3.1 %collective-permute-start.6 = (f32[16,2,16,128]{3,2,1,0:T(8,128)S(1)}, f32[16,2,16,128]{3,2,1,0:T(8,128)S(1)}, u32[]{:S(2)}, u32[]{:S(2)}) collective-permute-start(f32[16,2,16,128]{3,2,1,0:T(8,128)S(1)} %all_to_all.22.mine), channel_id=1, source_target_pairs={{0,8},{8,0},{1,9},{9,1},{2,10},{10,2},{3,11},{11,3},{4,12},{12,4},... | collective-permute-start | bytes 786440 | tf_op jit(solution)/shard_map/ppermute | solution.py:632
  114.4 1.2 collective-permute-done.6.other
  115.8 3.6 %collective-permute-start.8 = (f32[96,4,128]{2,1,0:T(4,128)S(1)}, f32[96,4,128]{2,1,0:T(4,128)S(1)}, u32[]{:S(2)}, u32[]{:S(2)}) collective-permute-start(f32[96,4,128]{2,1,0:T(4,128)S(1)} %get-tuple-element.88), channel_id=1, source_target_pairs={{1,0},{2,1},{3,2},{4,3},{5,4},{6,5},{7,6},{0,7},{9,8},{10,9},{11,1... | collective-permute-start | bytes 589832 | tf_op jit(solution)/shard_map/ppermute | solution.py:526
  119.4 3.1 %shard_map.165 = (f32[64,16,128]{2,1,0:T(8,128)S(1)}, f32[8,128]{1,0:T(8,128)S(1)}, f32[2,64,128]{2,1,0:T(8,128)S(1)}, f32[4,64,128]{2,1,0:T(8,128)S(1)}, f32[4,64,128]{2,1,0:T(8,128)S(1)}) custom-call(f32[64,16,128]{2,1,0:T(8,128)S(1)} %get-tuple-element.80.summed, f32[64,16,128]{2,1,0:T(8,128)S(1)} %get-tuple-element.81.smooth), custom_call_target="tpu_custom_call" | custom-call | flops 5242880 | bytes 1048576 | tf_op jit(solution)/shard_map/pallas_call | solution.py:35
  122.5 1.5 %collective-permute-done.7.low_two.low = f32[96,4,128]{2,1,0:T(4,128)S(1)} collective-permute-done((f32[96,4,128]{2,1,0:T(4,128)S(1)}, f32[96,4,128]{2,1,0:T(4,128)S(1)}, u32[]{:S(2)}, u32[]{:S(2)}) %collective-permute-start.7) | collective-permute-done | bytes 196640 | tf_op jit(solution)/shard_map/ppermute | solution.py:526
  124.0 1.3 shard_map.166
  125.3 0.8 copy-done.2
  126.1 4.7 %all-to-all-start.3 = ((f32[8,1,128]{2,1,0:T(1,128)}), f32[8,1,128]{2,1,0:T(1,128)S(1)}, u32[]{:S(2)}, u32[]{:S(2)}) async-start(f32[8,1,128]{2,1,0:T(1,128)} %get-tuple-element.89), calls=%async_computation.3 | async-start | bytes 8192 | tf_op jit(solution)/shard_map/all_to_all | solution.py:671
  130.8 3.0 %shard_map.167 = (f32[64,16,128]{2,1,0:T(8,128)S(1)}, f32[64,16,128]{2,1,0:T(8,128)S(1)}) custom-call(s32[1]{0:T(128)S(6)} %copy.19.src_cell, f32[1,3]{1,0:T(1,128)S(1)} %copy-done.7, f32[64,16,128]{2,1,0:T(8,128)S(1)} %get-tuple-element.79.u_two.now, f32[64,16,128]{2,1,0:T(8,128)S(1)} %get-tuple-element.66.now.u_one.old, ...), custom_call_target="tpu_custom_call" | custom-call | flops 5242880 | bytes 1572880 | tf_op jit(solution)/shard_map/pallas_call | solution.py:35
  133.7 0.8 copy-done.4
  134.6 1.1 shard_map.168.change
  135.7 1.0 copy-done.5
  136.8 1.2 shard_map.169
  (33 shorter events, 2.1 us)
Async XLA Ops:
  2.6 41.1 %copy-start = (f32[1,64,16,128]{3,2,1,0:T(8,128)S(1)}, f32[1,64,16,128]{3,2,1,0:T(8,128)}, u32[]{:S(2)}) copy-start(f32[1,64,16,128]{3,2,1,0:T(8,128)} %u_cur.1) | copy-start | bytes 1572868
  2.6 41.1 %copy-start.8 = (f32[1,64,16,128]{3,2,1,0:T(8,128)S(1)}, f32[1,64,16,128]{3,2,1,0:T(8,128)}, u32[]{:S(2)}) copy-start(f32[1,64,16,128]{3,2,1,0:T(8,128)} %refs_9_.1) | copy-start | bytes 1572868
  40.8 28.2 %collective-permute-start = (f32[16,4,2,16,128]{4,3,2,1,0:T(8,128)S(1)}, f32[16,4,2,16,128]{4,3,2,1,0:T(8,128)}, u32[]{:S(2)}, u32[]{:S(2)}) collective-permute-start(f32[16,4,2,16,128]{4,3,2,1,0:T(8,128)S(1)} %all_to_all.20.mine), channel_id=1, source_target_pairs={{0,8},{8,0},{1,9},{9,1},{2,10},{10,2},{3,11},{11,3},{4,12},{12,4},... | collective-permute-start | bytes 3145736 | tf_op jit(solution)/shard_map/ppermute | solution.py:591
  43.8 10.0 %collective-permute-start.1 = (f32[2,64,4,128]{3,2,1,0:T(4,128)S(1)}, f32[2,64,4,128]{3,2,1,0:T(4,128)S(1)}, u32[]{:S(2)}, u32[]{:S(2)}) collective-permute-start(f32[2,64,4,128]{3,2,1,0:T(4,128)S(1)} %pad_maximum_fusion), channel_id=1, source_target_pairs={{0,1},{1,2},{2,3},{3,4},{4,5},{5,6},{6,7},{7,0},{8,9},{9,10},{10,1... | collective-permute-start | bytes 786440 | tf_op jit(solution)/shard_map/ppermute | solution.py:526
  45.2 3.1 %copy-start.11 = (s32[16,2,4]{0,2,1:T(4,128)S(1)}, s32[16,2,4]{0,2,1:T(4,128)}, u32[]{:S(2)}) copy-start(s32[16,2,4]{0,2,1:T(4,128)} %param.22) | copy-start | bytes 1540
  45.3 8.6 %collective-permute-start.2 = (f32[2,64,4,128]{3,2,1,0:T(4,128)S(1)}, f32[2,64,4,128]{3,2,1,0:T(4,128)S(1)}, u32[]{:S(2)}, u32[]{:S(2)}) collective-permute-start(f32[2,64,4,128]{3,2,1,0:T(4,128)S(1)} %pad_maximum_fusion.1), channel_id=1, source_target_pairs={{1,0},{2,1},{3,2},{4,3},{5,4},{6,5},{7,6},{0,7},{9,8},{10,9},{11,1... | collective-permute-start | bytes 786440 | tf_op jit(solution)/shard_map/ppermute | solution.py:526
  53.9 0.7 copy-start.9
  54.6 0.7 copy-start.10
  65.9 0.7 copy-start.6
  69.0 5.5 %copy-start.1 = (f32[1,64,16,128]{3,2,1,0:T(8,128)S(1)}, f32[1,64,16,128]{3,2,1,0:T(8,128)}, u32[]{:S(2)}) copy-start(f32[1,64,16,128]{3,2,1,0:T(8,128)} %u_cur.1) | copy-start | bytes 1572868
  70.8 7.3 %collective-permute-start.3 = (f32[80,4,128]{2,1,0:T(4,128)S(1)}, f32[80,4,128]{2,1,0:T(4,128)S(1)}, u32[]{:S(2)}, u32[]{:S(2)}) collective-permute-start(f32[80,4,128]{2,1,0:T(4,128)S(1)} %get-tuple-element.75), channel_id=1, source_target_pairs={{0,1},{1,2},{2,3},{3,4},{4,5},{5,6},{6,7},{7,0},{8,9},{9,10},{10,1... | collective-permute-start | bytes 491528 | tf_op jit(solution)/shard_map/ppermute | solution.py:526
  70.9 7.2 %collective-permute-start.4 = (f32[80,4,128]{2,1,0:T(4,128)S(1)}, f32[80,4,128]{2,1,0:T(4,128)S(1)}, u32[]{:S(2)}, u32[]{:S(2)}) collective-permute-start(f32[80,4,128]{2,1,0:T(4,128)S(1)} %get-tuple-element.76), channel_id=1, source_target_pairs={{1,0},{2,1},{3,2},{4,3},{5,4},{6,5},{7,6},{0,7},{9,8},{10,9},{11,1... | collective-permute-start | bytes 491528 | tf_op jit(solution)/shard_map/ppermute | solution.py:526
  74.4 0.7 copy-start.7
  79.3 2.7 %collective-permute-start.5 = (f32[16,2,16,128]{3,2,1,0:T(8,128)S(1)}, f32[16,2,16,128]{3,2,1,0:T(8,128)S(1)}, u32[]{:S(2)}, u32[]{:S(2)}) collective-permute-start(f32[16,2,16,128]{3,2,1,0:T(8,128)S(1)} %get-tuple-element.78), channel_id=1, source_target_pairs={{0,8},{8,0},{1,9},{9,1},{2,10},{10,2},{3,11},{11,3},{4,12},{12,4},... | collective-permute-start | bytes 786440 | tf_op jit(solution)/shard_map/ppermute | solution.py:628
  111.3 4.2 %collective-permute-start.6 = (f32[16,2,16,128]{3,2,1,0:T(8,128)S(1)}, f32[16,2,16,128]{3,2,1,0:T(8,128)S(1)}, u32[]{:S(2)}, u32[]{:S(2)}) collective-permute-start(f32[16,2,16,128]{3,2,1,0:T(8,128)S(1)} %all_to_all.22.mine), channel_id=1, source_target_pairs={{0,8},{8,0},{1,9},{9,1},{2,10},{10,2},{3,11},{11,3},{4,12},{12,4},... | collective-permute-start | bytes 786440 | tf_op jit(solution)/shard_map/ppermute | solution.py:632
  115.7 8.3 %collective-permute-start.7 = (f32[96,4,128]{2,1,0:T(4,128)S(1)}, f32[96,4,128]{2,1,0:T(4,128)S(1)}, u32[]{:S(2)}, u32[]{:S(2)}) collective-permute-start(f32[96,4,128]{2,1,0:T(4,128)S(1)} %get-tuple-element.87), channel_id=1, source_target_pairs={{0,1},{1,2},{2,3},{3,4},{4,5},{5,6},{6,7},{7,0},{8,9},{9,10},{10,1... | collective-permute-start | bytes 589832 | tf_op jit(solution)/shard_map/ppermute | solution.py:526
  115.8 8.2 %collective-permute-start.8 = (f32[96,4,128]{2,1,0:T(4,128)S(1)}, f32[96,4,128]{2,1,0:T(4,128)S(1)}, u32[]{:S(2)}, u32[]{:S(2)}) collective-permute-start(f32[96,4,128]{2,1,0:T(4,128)S(1)} %get-tuple-element.88), channel_id=1, source_target_pairs={{1,0},{2,1},{3,2},{4,3},{5,4},{6,5},{7,6},{0,7},{9,8},{10,9},{11,1... | collective-permute-start | bytes 589832 | tf_op jit(solution)/shard_map/ppermute | solution.py:526
  125.3 0.8 copy-start.2
  126.1 9.6 %all-to-all-start.3 = ((f32[8,1,128]{2,1,0:T(1,128)}), f32[8,1,128]{2,1,0:T(1,128)S(1)}, u32[]{:S(2)}, u32[]{:S(2)}) async-start(f32[8,1,128]{2,1,0:T(1,128)} %get-tuple-element.89), calls=%async_computation.3 | async-start | bytes 8192 | tf_op jit(solution)/shard_map/all_to_all | solution.py:671
  133.7 0.8 copy-start.4
  134.5 1.2 copy-start.3
  135.7 1.0 copy-start.5

commit v5 on v4

--- a/solution.py
+++ b/solution.py
@@ -18,6 +18,7 @@
 REACH = 4
 MID = 8
 CHUNK = 4
+UNROLL = 4
 VMEM = pl.BlockSpec(memory_space=pltpu.VMEM)
 SMEM = pl.BlockSpec(memory_space=pltpu.SMEM)
 HBM = pl.BlockSpec(memory_space=pltpu.HBM)
@@ -312,7 +313,7 @@
     masks = lateral_masks(cells_y)
     fill_rows(rows, lambda at: now[at])
 
-    @pl.loop(0, cells_x // CHUNK)
+    @pl.loop(0, cells_x // CHUNK, unroll=UNROLL)
     def _(step):
         x = step * CHUNK
         at = pl.ds(x, CHUNK)
@@ -387,7 +388,7 @@
         ref[pl.ds(0, 1)] = blank
         ref[pl.ds(cells_x + 1, 1)] = blank
 
-    @pl.loop(0, cells_x // CHUNK)
+    @pl.loop(0, cells_x // CHUNK, unroll=2)
     def _(q):
         at = pl.ds(q * CHUNK + 1, CHUNK)
         blank = jnp.zeros((CHUNK, 1, cells_y), jnp.float32)
@@ -404,7 +405,7 @@
         near = near + shifted_y(flat).reshape(v.shape)
         return v + factor * (near - 6.0 * v)
 
-    @pl.loop(0, cells_x // CHUNK)
+    @pl.loop(0, cells_x // CHUNK, unroll=2)
     def _(q):
         x = q * CHUNK
         factor = smooth[pl.ds(x, CHUNK)]
@@ -428,7 +429,7 @@
         return total + jnp.sum(squares.reshape(CHUNK * cells_z // 8, 8, cells_y), axis=0)
 
     inner[...] = lax.fori_loop(
-        0, cells_x // CHUNK, sweep, jnp.zeros((8, cells_y), jnp.float32)
+        0, cells_x // CHUNK, sweep, jnp.zeros((8, cells_y), jnp.float32), unroll=2
     )
 
 

time: 140 us -> 140 us (level)
  Pallas kernels: 30.6 us -> 27.6 us
  waiting for transfers between devices: 8.19 us -> 11 us
    pallas_call x13, Pallas kernels: 30.6 us -> 27.6 us  [call(): pl.pallas_call(kernel, out_shape=outs, in_specs=[spec(i) for i in range(l...]
    ppermute x3, waiting for transfers between devices: 5.75 us -> 7.67 us  [shift(): lax.ppermute(high_edge, DEPTH, forward)]
  transfers between devices with their start and end apart: 10 -> 10, of which waited for: 5 -> 6; matrix products, arithmetic and copies ran while one was open for 1% -> 1% of each run, Pallas kernels for 17% -> 15%
where the time goes in v5:
time: 140 us; the launch traced here: 138 us
  blocking collectives  67.4 us (48%)
  Pallas kernels  27.6 us (20%)
  starting transfers between devices  23.4 us (17%)
  waiting for transfers between devices  11 us (8%)
  local copies, waits for them, and re-layouts  6.23 us (4%)
  between operations  2.11 us (2%)
    all_to_all x1, blocking collectives, body(): mine = lax.all_to_all(spread, PEERS, 0, 0, tiled=True)  38.2 us
    pallas_call x13, Pallas kernels, call(): pl.pallas_call(kernel, out_shape=outs, in_specs=[spec(i) for i in range(l...  27.6 us
    all_to_all x1, blocking collectives, body(): mine = lax.all_to_all(total, PEERS, 0, 0, tiled=True)  14.6 us
    all_to_all x1, blocking collectives, body(): shares = lax.all_to_all(chip_sum, PEERS, 0, 0, tiled=True)  14.6 us
    ppermute x3, starting transfers between devices, shift(): lax.ppermute(low_edge, DEPTH, backward)  9.48 us
    ppermute x3, waiting for transfers between devices, shift(): lax.ppermute(high_edge, DEPTH, forward)  7.67 us
    unnamed x25, local copies, waits for them, and re-layouts  6.14 us
    ppermute x2, starting transfers between devices, body(): other = lax.ppermute(mine, 'core', SWAP)  5.9 us
  transfers between devices with their start and end apart: 10, of which 6 were waited for; matrix products, arithmetic and copies ran while one was open for 1% of the time, Pallas kernels for 15%

profile of v5, /device:TPU:1, one launch (start us, length us, event | category | flops | bytes accessed | tf_op | source)
XLA Modules:
  0.0 137.9 jit_solution(16832177876912755569)
XLA Ops:
  0.6 1.9 %shard_map.157 = f32[16,4,2,16,128]{4,3,2,1,0:T(8,128)} custom-call(f32[2,16,128]{2,1,0:T(8,128)} %model.1, f32[2,16,128]{2,1,0:T(8,128)} %aniso_h.1, f32[2,16,128]{2,1,0:T(8,128)} %aniso_c.1, f32[2,16,128]{2,1,0:T(8,128)} %smooth.1), custom_call_target="tpu_custom_call" | custom-call | bytes 65536 | tf_op jit(solution)/shard_map/pallas_call | solution.py:36
  2.6 38.2 %all_to_all.20.mine = f32[16,4,2,16,128]{4,3,2,1,0:T(8,128)S(1)} all-to-all(f32[16,4,2,16,128]{4,3,2,1,0:T(8,128)} %shard_map.157), channel_id=1, replica_groups=mesh['xh'=2,'z'=8,'core'=2,'xl'=2,'y'=4] {'xh','z'}, dimensions={0} | all-to-all | bytes 2097152 | tf_op jit(solution)/shard_map/all_to_all | solution.py:572
  40.8 2.8 %collective-permute-start = (f32[16,4,2,16,128]{4,3,2,1,0:T(8,128)S(1)}, f32[16,4,2,16,128]{4,3,2,1,0:T(8,128)}, u32[]{:S(2)}, u32[]{:S(2)}) collective-permute-start(f32[16,4,2,16,128]{4,3,2,1,0:T(8,128)S(1)} %all_to_all.20.mine), channel_id=1, source_target_pairs={{0,8},{8,0},{1,9},{9,1},{2,10},{10,2},{3,11},{11,3},{4,12},{12,4},... | collective-permute-start | bytes 3145736 | tf_op jit(solution)/shard_map/ppermute | solution.py:592
  43.8 1.4 collective-permute-start.1
  45.3 2.4 %collective-permute-start.2 = (f32[2,64,4,128]{3,2,1,0:T(4,128)S(1)}, f32[2,64,4,128]{3,2,1,0:T(4,128)S(1)}, u32[]{:S(2)}, u32[]{:S(2)}) collective-permute-start(f32[2,64,4,128]{3,2,1,0:T(4,128)S(1)} %pad_maximum_fusion.1), channel_id=1, source_target_pairs={{1,0},{2,1},{3,2},{4,3},{5,4},{6,5},{7,6},{0,7},{9,8},{10,9},{11,1... | collective-permute-start | bytes 786440 | tf_op jit(solution)/shard_map/ppermute | solution.py:527
  49.6 4.2 %collective-permute-done.1.low = f32[2,64,4,128]{3,2,1,0:T(4,128)S(1)} collective-permute-done((f32[2,64,4,128]{3,2,1,0:T(4,128)S(1)}, f32[2,64,4,128]{3,2,1,0:T(4,128)S(1)}, u32[]{:S(2)}, u32[]{:S(2)}) %collective-permute-start.1) | collective-permute-done | bytes 262176 | tf_op jit(solution)/shard_map/ppermute | solution.py:527
  53.9 0.7 copy-done.9
  54.6 0.7 copy-done.10
  55.3 10.5 %shard_map.158 = (f32[64,16,128]{2,1,0:T(8,128)}, f32[64,16,128]{2,1,0:T(8,128)}, f32[64,16,128]{2,1,0:T(8,128)}, f32[64,16,128]{2,1,0:T(8,128)}, f32[64,16,128]...) custom-call(s32[1]{0:T(128)S(6)} %copy.19.src_cell, ...), custom_call_target="tpu_custom_call" | custom-call | flops 20971520 | bytes 2623508 | tf_op jit(solution)/shard_map/pallas_call | solution.py:36
  66.6 2.4 %shard_map.159 = (f32[64,16,128]{2,1,0:T(8,128)S(1)}, f32[64,16,128]{2,1,0:T(8,128)S(1)}, f32[64,16,128]{2,1,0:T(8,128)S(1)}, f32[64,16,128]{2,1,0:T(8,128)S(1)}...) custom-call(f32[64,16,128]{2,1,0:T(8,128)} %get-tuple-element.48.ref, ...), custom_call_target="tpu_custom_call" | custom-call | bytes 4726784 | tf_op jit(solution)/shard_map/pallas_call | solution.py:36
  69.0 1.8 %shard_map.160 = (f32[64,16,128]{2,1,0:T(8,128)S(1)}, f32[64,16,128]{2,1,0:T(8,128)S(1)}, f32[64,16,128]{2,1,0:T(8,128)S(1)}, f32[64,16,128]{2,1,0:T(8,128)S(1)}...) custom-call(f32[16,4,2,16,128]{4,3,2,1,0:T(8,128)S(1)} %all_to_all.2, ...), custom_call_target="tpu_custom_call" | custom-call | flops 2621440 | bytes 6815744 | tf_op jit(solution)/shard_map/pallas_call | solution.py:36
  70.9 3.6 %collective-permute-start.4 = (f32[80,4,128]{2,1,0:T(4,128)S(1)}, f32[80,4,128]{2,1,0:T(4,128)S(1)}, u32[]{:S(2)}, u32[]{:S(2)}) collective-permute-start(f32[80,4,128]{2,1,0:T(4,128)S(1)} %get-tuple-element.76), channel_id=1, source_target_pairs={{1,0},{2,1},{3,2},{4,3},{5,4},{6,5},{7,6},{0,7},{9,8},{10,9},{11,1... | collective-permute-start | bytes 491528 | tf_op jit(solution)/shard_map/ppermute | solution.py:527
  75.1 2.1 %shard_map.161 = (f32[64,16,128]{2,1,0:T(8,128)S(1)}, f32[64,16,128]{2,1,0:T(8,128)S(1)}) custom-call(s32[1]{0:T(128)S(6)} %copy.19.src_cell, f32[1,3]{1,0:T(1,128)S(1)} %copy-done.7, f32[64,16,128]{2,1,0:T(8,128)S(1)} %get-tuple-element.66.now.u_one.old, f32[64,16,128]{2,1,0:T(8,128)S(1)} %bitcast.1, f32[64,16,128]{2,1,0:T(8,128)S(1)} %get-tuple-element.67.aniso_h), custom_call_target="tpu_custom_call" | custom-call | flops 5242880 | bytes 1572880 | tf_op jit(solution)/shard_map/pallas_call | solution.py:36
  77.9 1.2 shard_map.162
  79.0 1.8 %collective-permute-start.5 = (f32[16,2,16,128]{3,2,1,0:T(8,128)S(1)}, f32[16,2,16,128]{3,2,1,0:T(8,128)S(1)}, u32[]{:S(2)}, u32[]{:S(2)}) collective-permute-start(f32[16,2,16,128]{3,2,1,0:T(8,128)S(1)} %get-tuple-element.78), channel_id=1, source_target_pairs={{0,8},{8,0},{1,9},{9,1},{2,10},{10,2},{3,11},{11,3},{4,12},{12,4},... | collective-permute-start | bytes 786440 | tf_op jit(solution)/shard_map/ppermute | solution.py:629
  80.9 1.2 collective-permute-done.5
  82.1 14.6 %all_to_all.21.parts = f32[16,2,16,128]{3,2,1,0:T(8,128)S(1)} all-to-all(f32[16,2,16,128]{3,2,1,0:T(8,128)S(1)} %add.3), channel_id=1, replica_groups=mesh['xh'=2,'z'=8,'core'=2,'xl'=2,'y'=4] {'xh','z'}, dimensions={0} | all-to-all | bytes 524288 | tf_op jit(solution)/shard_map/all_to_all | solution.py:630
  96.7 14.6 %all_to_all.22.mine = f32[16,2,16,128]{3,2,1,0:T(8,128)S(1)} all-to-all(f32[16,2,16,128]{3,2,1,0:T(8,128)S(1)} %shard_map.163), channel_id=1, replica_groups=mesh['xh'=2,'z'=8,'core'=2,'xl'=2,'y'=4] {'xh','z'}, dimensions={0} | all-to-all | bytes 524288 | tf_op jit(solution)/shard_map/all_to_all | solution.py:632
  111.3 3.1 %collective-permute-start.6 = (f32[16,2,16,128]{3,2,1,0:T(8,128)S(1)}, f32[16,2,16,128]{3,2,1,0:T(8,128)S(1)}, u32[]{:S(2)}, u32[]{:S(2)}) collective-permute-start(f32[16,2,16,128]{3,2,1,0:T(8,128)S(1)} %all_to_all.22.mine), channel_id=1, source_target_pairs={{0,8},{8,0},{1,9},{9,1},{2,10},{10,2},{3,11},{11,3},{4,12},{12,4},... | collective-permute-start | bytes 786440 | tf_op jit(solution)/shard_map/ppermute | solution.py:633
  114.4 1.2 collective-permute-done.6.other
  115.8 3.6 %collective-permute-start.8 = (f32[96,4,128]{2,1,0:T(4,128)S(1)}, f32[96,4,128]{2,1,0:T(4,128)S(1)}, u32[]{:S(2)}, u32[]{:S(2)}) collective-permute-start(f32[96,4,128]{2,1,0:T(4,128)S(1)} %get-tuple-element.88), channel_id=1, source_target_pairs={{1,0},{2,1},{3,2},{4,3},{5,4},{6,5},{7,6},{0,7},{9,8},{10,9},{11,1... | collective-permute-start | bytes 589832 | tf_op jit(solution)/shard_map/ppermute | solution.py:527
  119.4 1.9 %shard_map.165 = (f32[64,16,128]{2,1,0:T(8,128)S(1)}, f32[8,128]{1,0:T(8,128)S(1)}, f32[2,64,128]{2,1,0:T(8,128)S(1)}, f32[4,64,128]{2,1,0:T(8,128)S(1)}, f32[4,64,128]{2,1,0:T(8,128)S(1)}) custom-call(f32[64,16,128]{2,1,0:T(8,128)S(1)} %get-tuple-element.80.summed, f32[64,16,128]{2,1,0:T(8,128)S(1)} %get-tuple-element.81.smooth), custom_call_target="tpu_custom_call" | custom-call | flops 5242880 | bytes 1048576 | tf_op jit(solution)/shard_map/pallas_call | solution.py:36
  121.3 2.7 %collective-permute-done.7.low_two.low = f32[96,4,128]{2,1,0:T(4,128)S(1)} collective-permute-done((f32[96,4,128]{2,1,0:T(4,128)S(1)}, f32[96,4,128]{2,1,0:T(4,128)S(1)}, u32[]{:S(2)}, u32[]{:S(2)}) %collective-permute-start.7) | collective-permute-done | bytes 196640 | tf_op jit(solution)/shard_map/ppermute | solution.py:527
  124.0 1.3 shard_map.166
  125.3 0.8 copy-done.2
  126.1 4.7 %all-to-all-start.3 = ((f32[8,1,128]{2,1,0:T(1,128)}), f32[8,1,128]{2,1,0:T(1,128)S(1)}, u32[]{:S(2)}, u32[]{:S(2)}) async-start(f32[8,1,128]{2,1,0:T(1,128)} %get-tuple-element.89), calls=%async_computation.3 | async-start | bytes 8192 | tf_op jit(solution)/shard_map/all_to_all | solution.py:672
  130.8 2.1 %shard_map.167 = (f32[64,16,128]{2,1,0:T(8,128)S(1)}, f32[64,16,128]{2,1,0:T(8,128)S(1)}) custom-call(s32[1]{0:T(128)S(6)} %copy.19.src_cell, f32[1,3]{1,0:T(1,128)S(1)} %copy-done.7, f32[64,16,128]{2,1,0:T(8,128)S(1)} %get-tuple-element.79.u_two.now, f32[64,16,128]{2,1,0:T(8,128)S(1)} %get-tuple-element.66.now.u_one.old, ...), custom_call_target="tpu_custom_call" | custom-call | flops 5242880 | bytes 1572880 | tf_op jit(solution)/shard_map/pallas_call | solution.py:36
  132.8 0.8 copy-done.4
  133.6 1.1 shard_map.168.change
  134.7 1.0 all-to-all-done.3.squares
  135.7 1.0 copy-done.5
  136.8 1.2 shard_map.169
  (33 shorter events, 3.4 us)
Async XLA Ops:
  2.6 41.1 %copy-start = (f32[1,64,16,128]{3,2,1,0:T(8,128)S(1)}, f32[1,64,16,128]{3,2,1,0:T(8,128)}, u32[]{:S(2)}) copy-start(f32[1,64,16,128]{3,2,1,0:T(8,128)} %u_cur.1) | copy-start | bytes 1572868
  2.6 41.1 %copy-start.8 = (f32[1,64,16,128]{3,2,1,0:T(8,128)S(1)}, f32[1,64,16,128]{3,2,1,0:T(8,128)}, u32[]{:S(2)}) copy-start(f32[1,64,16,128]{3,2,1,0:T(8,128)} %refs_9_.1) | copy-start | bytes 1572868
  40.8 28.2 %collective-permute-start = (f32[16,4,2,16,128]{4,3,2,1,0:T(8,128)S(1)}, f32[16,4,2,16,128]{4,3,2,1,0:T(8,128)}, u32[]{:S(2)}, u32[]{:S(2)}) collective-permute-start(f32[16,4,2,16,128]{4,3,2,1,0:T(8,128)S(1)} %all_to_all.20.mine), channel_id=1, source_target_pairs={{0,8},{8,0},{1,9},{9,1},{2,10},{10,2},{3,11},{11,3},{4,12},{12,4},... | collective-permute-start | bytes 3145736 | tf_op jit(solution)/shard_map/ppermute | solution.py:592
  43.8 10.0 %collective-permute-start.1 = (f32[2,64,4,128]{3,2,1,0:T(4,128)S(1)}, f32[2,64,4,128]{3,2,1,0:T(4,128)S(1)}, u32[]{:S(2)}, u32[]{:S(2)}) collective-permute-start(f32[2,64,4,128]{3,2,1,0:T(4,128)S(1)} %pad_maximum_fusion), channel_id=1, source_target_pairs={{0,1},{1,2},{2,3},{3,4},{4,5},{5,6},{6,7},{7,0},{8,9},{9,10},{10,1... | collective-permute-start | bytes 786440 | tf_op jit(solution)/shard_map/ppermute | solution.py:527
  45.2 3.1 %copy-start.11 = (s32[16,2,4]{0,2,1:T(4,128)S(1)}, s32[16,2,4]{0,2,1:T(4,128)}, u32[]{:S(2)}) copy-start(s32[16,2,4]{0,2,1:T(4,128)} %param.22) | copy-start | bytes 1540
  45.3 8.6 %collective-permute-start.2 = (f32[2,64,4,128]{3,2,1,0:T(4,128)S(1)}, f32[2,64,4,128]{3,2,1,0:T(4,128)S(1)}, u32[]{:S(2)}, u32[]{:S(2)}) collective-permute-start(f32[2,64,4,128]{3,2,1,0:T(4,128)S(1)} %pad_maximum_fusion.1), channel_id=1, source_target_pairs={{1,0},{2,1},{3,2},{4,3},{5,4},{6,5},{7,6},{0,7},{9,8},{10,9},{11,1... | collective-permute-start | bytes 786440 | tf_op jit(solution)/shard_map/ppermute | solution.py:527
  53.9 0.7 copy-start.9
  54.6 0.7 copy-start.10
  65.9 0.7 copy-start.6
  69.0 5.5 %copy-start.1 = (f32[1,64,16,128]{3,2,1,0:T(8,128)S(1)}, f32[1,64,16,128]{3,2,1,0:T(8,128)}, u32[]{:S(2)}) copy-start(f32[1,64,16,128]{3,2,1,0:T(8,128)} %u_cur.1) | copy-start | bytes 1572868
  70.8 7.1 %collective-permute-start.3 = (f32[80,4,128]{2,1,0:T(4,128)S(1)}, f32[80,4,128]{2,1,0:T(4,128)S(1)}, u32[]{:S(2)}, u32[]{:S(2)}) collective-permute-start(f32[80,4,128]{2,1,0:T(4,128)S(1)} %get-tuple-element.75), channel_id=1, source_target_pairs={{0,1},{1,2},{2,3},{3,4},{4,5},{5,6},{6,7},{7,0},{8,9},{9,10},{10,1... | collective-permute-start | bytes 491528 | tf_op jit(solution)/shard_map/ppermute | solution.py:527
  70.9 7.0 %collective-permute-start.4 = (f32[80,4,128]{2,1,0:T(4,128)S(1)}, f32[80,4,128]{2,1,0:T(4,128)S(1)}, u32[]{:S(2)}, u32[]{:S(2)}) collective-permute-start(f32[80,4,128]{2,1,0:T(4,128)S(1)} %get-tuple-element.76), channel_id=1, source_target_pairs={{1,0},{2,1},{3,2},{4,3},{5,4},{6,5},{7,6},{0,7},{9,8},{10,9},{11,1... | collective-permute-start | bytes 491528 | tf_op jit(solution)/shard_map/ppermute | solution.py:527
  74.4 0.7 copy-start.7
  79.0 3.0 %collective-permute-start.5 = (f32[16,2,16,128]{3,2,1,0:T(8,128)S(1)}, f32[16,2,16,128]{3,2,1,0:T(8,128)S(1)}, u32[]{:S(2)}, u32[]{:S(2)}) collective-permute-start(f32[16,2,16,128]{3,2,1,0:T(8,128)S(1)} %get-tuple-element.78), channel_id=1, source_target_pairs={{0,8},{8,0},{1,9},{9,1},{2,10},{10,2},{3,11},{11,3},{4,12},{12,4},... | collective-permute-start | bytes 786440 | tf_op jit(solution)/shard_map/ppermute | solution.py:629
  111.3 4.2 %collective-permute-start.6 = (f32[16,2,16,128]{3,2,1,0:T(8,128)S(1)}, f32[16,2,16,128]{3,2,1,0:T(8,128)S(1)}, u32[]{:S(2)}, u32[]{:S(2)}) collective-permute-start(f32[16,2,16,128]{3,2,1,0:T(8,128)S(1)} %all_to_all.22.mine), channel_id=1, source_target_pairs={{0,8},{8,0},{1,9},{9,1},{2,10},{10,2},{3,11},{11,3},{4,12},{12,4},... | collective-permute-start | bytes 786440 | tf_op jit(solution)/shard_map/ppermute | solution.py:633
  115.7 8.3 %collective-permute-start.7 = (f32[96,4,128]{2,1,0:T(4,128)S(1)}, f32[96,4,128]{2,1,0:T(4,128)S(1)}, u32[]{:S(2)}, u32[]{:S(2)}) collective-permute-start(f32[96,4,128]{2,1,0:T(4,128)S(1)} %get-tuple-element.87), channel_id=1, source_target_pairs={{0,1},{1,2},{2,3},{3,4},{4,5},{5,6},{6,7},{7,0},{8,9},{9,10},{10,1... | collective-permute-start | bytes 589832 | tf_op jit(solution)/shard_map/ppermute | solution.py:527
  115.8 8.2 %collective-permute-start.8 = (f32[96,4,128]{2,1,0:T(4,128)S(1)}, f32[96,4,128]{2,1,0:T(4,128)S(1)}, u32[]{:S(2)}, u32[]{:S(2)}) collective-permute-start(f32[96,4,128]{2,1,0:T(4,128)S(1)} %get-tuple-element.88), channel_id=1, source_target_pairs={{1,0},{2,1},{3,2},{4,3},{5,4},{6,5},{7,6},{0,7},{9,8},{10,9},{11,1... | collective-permute-start | bytes 589832 | tf_op jit(solution)/shard_map/ppermute | solution.py:527
  125.3 0.8 copy-start.2
  126.1 9.6 %all-to-all-start.3 = ((f32[8,1,128]{2,1,0:T(1,128)}), f32[8,1,128]{2,1,0:T(1,128)S(1)}, u32[]{:S(2)}, u32[]{:S(2)}) async-start(f32[8,1,128]{2,1,0:T(1,128)} %get-tuple-element.89), calls=%async_computation.3 | async-start | bytes 8192 | tf_op jit(solution)/shard_map/all_to_all | solution.py:672
  132.8 0.8 copy-start.4
  133.6 2.1 %copy-start.3 = (f32[64,16,128]{2,1,0:T(8,128)S(1)}, f32[64,16,128]{2,1,0:T(8,128)}, u32[]{:S(2)}) copy-start(f32[64,16,128]{2,1,0:T(8,128)} %copy-done.2) | copy-start | bytes 1572868
  135.7 1.0 copy-start.5

commit v6 on v5

--- a/solution.py
+++ b/solution.py
@@ -78,7 +78,7 @@
     cells_x, cells_z = pad.shape[0], pad.shape[1] - 2 * MID
     below, above = has_sides()
 
-    @pl.loop(0, cells_x // CHUNK)
+    @pl.loop(0, cells_x // CHUNK, unroll=2)
     def _(step):
         at = pl.ds(step * CHUNK, CHUNK)
         pad[at, pl.ds(MID, cells_z), :] = read(at)
@@ -92,7 +92,7 @@
     first_z[pl.ds(0, REACH)] = zeros
     first_z[pl.ds(REACH + cells_x, REACH)] = zeros
 
-    @pl.loop(0, cells_x // CHUNK)
+    @pl.loop(0, cells_x // CHUNK, unroll=2)
     def _(step):
         x = step * CHUNK
         at = lambda k: pad[pl.ds(x, CHUNK), pl.ds(MID + k, cells_z), :]
@@ -325,19 +325,22 @@
 
 def second_kernel(
     u_one, base, side, a_one, grad, weight, model, aniso_c, low, high,
-    u_two, keep, send, pad, first_z, dep,
+    u_two, keep, send, low_two, high_two, pad, first_z, dep,
 ):
-    cells_x = u_two.shape[0]
+    cells_x, cells_z, _ = u_two.shape
     fill_depth(pad, lambda at: u_one[at], lambda at: low[at], lambda at: high[at])
     depth_pass(pad, first_z, dep)
     own = position()[1] == 0
 
-    @pl.loop(0, cells_x // CHUNK)
+    @pl.loop(0, cells_x // CHUNK, unroll=2)
     def _(step):
         x = step * CHUNK
         at = pl.ds(x, CHUNK)
         k_u = side[at] + dep[at] + aniso_c[at] * crossing(first_z, x)
-        u_two[at] = base[at] + model[at] * k_u
+        new = base[at] + model[at] * k_u
+        u_two[at] = new
+        low_two[at] = new[:, :REACH]
+        high_two[at] = new[:, cells_z - REACH :]
         total = weight[...] * (grad[at] + a_one[at] * k_u)
         keep[step] = jnp.where(own, total[:2], total[2:])
         send[step] = jnp.where(own, total[2:], total[:2])
@@ -351,8 +354,8 @@
         out[peer] = total
 
 
-def join_kernel(mine, other, u_two, summed, low, high):
-    cells_x, cells_z, _ = summed.shape
+def join_kernel(mine, other, summed, low, high):
+    cells_z = summed.shape[1]
     count = mine.shape[0]
     own = position()[1] == 0
 
@@ -362,10 +365,8 @@
             rows = pl.ds(q * 4 + p * 2, 2)
             g = jnp.where(own == (p == 0), mine[q], other[q])
             summed[rows] = g
-            low[rows] = u_two[rows, :REACH]
-            high[rows] = u_two[rows, cells_z - REACH :]
             for k in range(2):
-                edge = (pl.ds(cells_x + k * count + q, 1), pl.ds(2 * p, 2), slice(None))
+                edge = (pl.ds(k * count + q, 1), pl.ds(2 * p, 2), slice(None))
                 low[edge] = g[:, k][None]
                 high[edge] = g[:, cells_z - 1 - k][None]
 
@@ -434,7 +435,7 @@
 
 
 def edge_kernel(
-    smoothed_in, inner, own_g, own_s, own_out, low_two, high_two, low_one, high_one,
+    smoothed_in, inner, own_g, own_s, own_out, low_sum, high_sum, low_one, high_one,
     smoothed, square, planes,
 ):
     cells_x, cells_z, cells_y = smoothed.shape
@@ -443,7 +444,7 @@
     blank = jnp.zeros((8, cells_y), jnp.float32)
     total = inner[...]
     for side, (sums, smooth, present) in enumerate(
-        ((low_two, low_one, has_sides()[0]), (high_two, high_one, has_sides()[1]))
+        ((low_sum, low_one, has_sides()[0]), (high_sum, high_one, has_sides()[1]))
     ):
         for k in range(4):
             planes[k, pl.ds(0, 8)] = blank
@@ -453,7 +454,7 @@
         def _(q, sums=sums, smooth=smooth, present=present):
             at = pl.ds(8 + 4 * q, 4)
             for k in range(2):
-                planes[k, at] = jnp.where(present, sums[cells_x + k * count + q], 0.0)
+                planes[k, at] = jnp.where(present, sums[k * count + q], 0.0)
             planes[2, at] = jnp.where(present, smooth[cells_x + q], 0.0)
 
         def near(k):
@@ -488,7 +489,132 @@
     fill_depth(pad, lambda at: u_two[at], lambda at: low[at], lambda at: high[at])
     depth_pass(pad, first_z, dep)
 
-    @pl.loop(0, cells_x // CHUNK)
+    @pl.loop(0, cells_x // CHUNK, unroll=2)
+    def _(step):
+        x = step * CHUNK
+        at = pl.ds(x, CHUNK)
+        change[at] = model[at] * (side[at] + dep[at] + aniso_c[at] * crossing(first_z, x))
+
+
+def shifted_y(flat):
+    cells_y = flat.shape[-1]
+    lane = lax.broadcasted_iota(jnp.int32, (1,) * (flat.ndim - 2) + (8, cells_y), flat.ndim - 1)
+    axis = flat.ndim - 1
+    if flat.ndim == 2:
+        lane = lax.broadcasted_iota(jnp.int32, flat.shape, 1)
+    right = jnp.where(lane < cells_y - 1, pltpu.roll(flat, cells_y - 1, axis), 0.0)
+    left = jnp.where(lane >= 1, pltpu.roll(flat, 1, axis), 0.0)
+    return right + left
+
+
+def relax_kernel(summed, smooth, out, inner, own_g, own_s, own_out, wide, once):
+    cells_x, cells_z, cells_y = summed.shape
+    for ref in (wide, once):
+        blank = jnp.zeros((1, *ref.shape[1:]), jnp.float32)
+        ref[pl.ds(0, 1)] = blank
+        ref[pl.ds(cells_x + 1, 1)] = blank
+
+    @pl.loop(0, cells_x // CHUNK, unroll=2)
+    def _(q):
+        at = pl.ds(q * CHUNK + 1, CHUNK)
+        blank = jnp.zeros((CHUNK, 1, cells_y), jnp.float32)
+        for ref in (wide, once):
+            ref[at, pl.ds(MID - 1, 1), :] = blank
+            ref[at, pl.ds(MID + cells_z, 1), :] = blank
+        wide[at, pl.ds(MID, cells_z), :] = summed[pl.ds(q * CHUNK, CHUNK)]
+
+    def relaxed(ref, x, factor):
+        at = lambda dx, dz: ref[pl.ds(x + 1 + dx, CHUNK), pl.ds(MID + dz, cells_z), :]
+        v = at(0, 0)
+        near = at(1, 0) + at(-1, 0) + at(0, 1) + at(0, -1)
+        flat = v.reshape(CHUNK * cells_z // 8, 8, cells_y)
+        near = near + shifted_y(flat).reshape(v.shape)
+        return v + factor * (near - 6.0 * v)
+
+    @pl.loop(0, cells_x // CHUNK, unroll=2)
+    def _(q):
+        x = q * CHUNK
+        factor = smooth[pl.ds(x, CHUNK)]
+        once[pl.ds(x + 1, CHUNK), pl.ds(MID, cells_z), :] = relaxed(wide, x, factor)
+        g = summed[pl.ds(x, CHUNK)]
+        for i, k in enumerate((0, cells_z - 1)):
+            own_g[i, pl.ds(x, CHUNK)] = g[:, k]
+        for i, k in enumerate((0, 1, cells_z - 2, cells_z - 1)):
+            own_s[i, pl.ds(x, CHUNK)] = factor[:, k]
+
+    depth = lax.broadcasted_iota(jnp.int32, (1, cells_z, cells_y), 1)
+    between = (depth >= 2) & (depth < cells_z - 2)
+
+    def sweep(q, total):
+        x = q * CHUNK
+        value = relaxed(once, x, smooth[pl.ds(x, CHUNK)])
+        out[pl.ds(x, CHUNK)] = value
+        for i, k in enumerate((0, 1, cells_z - 2, cells_z - 1)):
+            own_out[i, pl.ds(x, CHUNK)] = value[:, k]
+        squares = jnp.where(between, value * value, 0.0)
+        return total + jnp.sum(squares.reshape(CHUNK * cells_z // 8, 8, cells_y), axis=0)
+
+    inner[...] = lax.fori_loop(
+        0, cells_x // CHUNK, sweep, jnp.zeros((8, cells_y), jnp.float32), unroll=2
+    )
+
+
+def edge_kernel(
+    smoothed_in, inner, own_g, own_s, own_out, low_sum, high_sum, low_one, high_one,
+    smoothed, square, planes,
+):
+    cells_x, cells_z, cells_y = smoothed.shape
+    smoothed[...] = smoothed_in[...]
+    count = cells_x // 4
+    blank = jnp.zeros((8, cells_y), jnp.float32)
+    total = inner[...]
+    for side, (sums, smooth, present) in enumerate(
+        ((low_sum, low_one, has_sides()[0]), (high_sum, high_one, has_sides()[1]))
+    ):
+        for k in range(4):
+            planes[k, pl.ds(0, 8)] = blank
+            planes[k, pl.ds(8 + cells_x, 8)] = blank
+
+        @pl.loop(0, count)
+        def _(q, sums=sums, smooth=smooth, present=present):
+            at = pl.ds(8 + 4 * q, 4)
+            for k in range(2):
+                planes[k, at] = jnp.where(present, sums[k * count + q], 0.0)
+            planes[2, at] = jnp.where(present, smooth[cells_x + q], 0.0)
+
+        def near(k):
+            at = lambda dx: planes[k, pl.ds(8 + dx, cells_x)]
+            return at(1) + at(-1) + shifted_y(at(0))
+
+        whole = pl.ds(8, cells_x)
+        first, second, factor = planes[0, whole], planes[1, whole], planes[2, whole]
+        outside = first + factor * (near(0) + second + own_g[side] - 6.0 * first)
+        edge, inside = (0, 1) if side == 0 else (3, 2)
+        change = own_s[edge] * first
+        planes[3, whole] = change
+        value = own_out[edge] + change + own_s[edge] * (near(3) - 6.0 * change + outside)
+        beside = own_out[inside] + own_s[inside] * change
+        squares = value * value + beside * beside
+        total = total + jnp.sum(squares.reshape(cells_x // 8, 8, cells_y), axis=0)
+        planes[0, whole] = value
+        planes[1, whole] = beside
+        rows = (0, 1) if side == 0 else (cells_z - 1, cells_z - 2)
+
+        @pl.loop(0, count)
+        def _(q, rows=rows):
+            for k, z in enumerate(rows):
+                smoothed[pl.ds(4 * q, 4), pl.ds(z, 1), :] = planes[k, pl.ds(8 + 4 * q, 4)][:, None]
+
+    row = jnp.sum(total, axis=0, keepdims=True)
+    square[...] = jnp.broadcast_to(row[None], square.shape)
+
+
+def third_kernel(u_two, side, model, aniso_c, low, high, change, pad, first_z, dep):
+    cells_x = change.shape[0]
+    fill_depth(pad, lambda at: u_two[at], lambda at: low[at], lambda at: high[at])
+    depth_pass(pad, first_z, dep)
+
+    @pl.loop(0, cells_x // CHUNK, unroll=2)
     def _(step):
         x = step * CHUNK
         at = pl.ds(x, CHUNK)
@@ -618,11 +744,12 @@
         work // 2,
     )
     split = f32(peers, rows, cells_z, cells_y)
-    u_two, keep, send = call(
+    edge = f32(cells_x, REACH, cells_y)
+    u_two, keep, send, low_edge, high_edge = call(
         second_kernel,
         (u_one, base, side, a_one, grad, weight, model_slab, c_slab, low_one, high_one),
         0,
-        (slab, split, split),
+        (slab, split, split, edge, edge),
         (pad, first_z, dep),
         work,
     )
@@ -631,11 +758,12 @@
     total = call(sum_kernel, (shares,), 0, split)
     mine = lax.all_to_all(total, PEERS, 0, 0, tiled=True)
     other = lax.ppermute(mine, "core", SWAP)
-    payload = f32(cells_x + 2 * peers, REACH, cells_y)
+    low_two, high_two = shift(low_edge, high_edge)
+    payload = f32(2 * peers, 4, cells_y)
     summed, low_edge, high_edge = call(
-        join_kernel, (mine, other, u_two), 0, (slab, payload, payload)
-    )
-    low_two, high_two = shift(low_edge, high_edge)
+        join_kernel, (mine, other), 0, (slab, payload, payload)
+    )
+    low_sum, high_sum = shift(low_edge, high_edge)
     base, side = call(
         functools.partial(side_kernel, 2),
         (src_cell, src_wave, u_two, u_one, h_slab),
@@ -663,7 +791,7 @@
     )
     smoothed, square = call(
         edge_kernel,
-        (smoothed, inner, own_g, own_s, own_out, low_two, high_two, low_one, high_one),
+        (smoothed, inner, own_g, own_s, own_out, low_sum, high_sum, low_one, high_one),
         0,
         (slab, f32(lax.axis_size(DEPTH), 1, cells_y)),
         (scratch(4, cells_x + 16, cells_y),),

time: 140 us -> 138 us (0.986)
  starting transfers between devices: 23.4 us -> 25.3 us
  local copies, waits for them, and re-layouts: 6.23 us -> 4.38 us
    ppermute x3 -> x4, starting transfers between devices: 9.48 us -> 12.8 us  [shift(): lax.ppermute(low_edge, DEPTH, backward)]
    unnamed x25 -> x21, local copies, waits for them, and re-layouts: 6.14 us -> 4.29 us
    ppermute x3 -> x4, waiting for transfers between devices: 7.67 us -> 7.45 us  [shift(): lax.ppermute(high_edge, DEPTH, forward)]
  transfers between devices with their start and end apart: 10 -> 12, of which waited for: 6 -> 5; matrix products, arithmetic and copies ran while one was open for 1% -> 1% of each run, Pallas kernels for 15% -> 15%
where the time goes in v6:
time: 138 us; the launch traced here: 137 us
  blocking collectives  67.4 us (49%)
  Pallas kernels  27.8 us (20%)
  starting transfers between devices  25.3 us (18%)
  waiting for transfers between devices  9.68 us (7%)
  local copies, waits for them, and re-layouts  4.38 us (3%)
  between operations  2.13 us (2%)
    all_to_all x1, blocking collectives, body(): mine = lax.all_to_all(spread, PEERS, 0, 0, tiled=True)  38.2 us
    pallas_call x13, Pallas kernels, call(): pl.pallas_call(kernel, out_shape=outs, in_specs=[spec(i) for i in range(l...  27.8 us
    all_to_all x1, blocking collectives, body(): mine = lax.all_to_all(total, PEERS, 0, 0, tiled=True)  14.6 us
    all_to_all x1, blocking collectives, body(): shares = lax.all_to_all(chip_sum, PEERS, 0, 0, tiled=True)  14.6 us
    ppermute x4, starting transfers between devices, shift(): lax.ppermute(low_edge, DEPTH, backward)  12.8 us
    ppermute x4, waiting for transfers between devices, shift(): lax.ppermute(high_edge, DEPTH, forward)  7.45 us
    ppermute x2, starting transfers between devices, body(): other = lax.ppermute(mine, 'core', SWAP)  5.9 us
    unnamed x21, local copies, waits for them, and re-layouts  4.29 us
  transfers between devices with their start and end apart: 12, of which 5 were waited for; matrix products, arithmetic and copies ran while one was open for 1% of the time, Pallas kernels for 15%

profile of v6, /device:TPU:1, one launch (start us, length us, event | category | flops | bytes accessed | tf_op | source)
XLA Modules:
  0.0 136.8 jit_solution(17238909476730506615)
XLA Ops:
  0.6 1.9 %shard_map.157 = f32[16,4,2,16,128]{4,3,2,1,0:T(8,128)} custom-call(f32[2,16,128]{2,1,0:T(8,128)} %model.1, f32[2,16,128]{2,1,0:T(8,128)} %aniso_h.1, f32[2,16,128]{2,1,0:T(8,128)} %aniso_c.1, f32[2,16,128]{2,1,0:T(8,128)} %smooth.1), custom_call_target="tpu_custom_call" | custom-call | bytes 65536 | tf_op jit(solution)/shard_map/pallas_call | solution.py:36
  2.6 38.2 %all_to_all.20.mine = f32[16,4,2,16,128]{4,3,2,1,0:T(8,128)S(1)} all-to-all(f32[16,4,2,16,128]{4,3,2,1,0:T(8,128)} %shard_map.157), channel_id=1, replica_groups=mesh['xh'=2,'z'=8,'core'=2,'xl'=2,'y'=4] {'xh','z'}, dimensions={0} | all-to-all | bytes 2097152 | tf_op jit(solution)/shard_map/all_to_all | solution.py:698
  40.8 2.8 %collective-permute-start = (f32[16,4,2,16,128]{4,3,2,1,0:T(8,128)S(1)}, f32[16,4,2,16,128]{4,3,2,1,0:T(8,128)}, u32[]{:S(2)}, u32[]{:S(2)}) collective-permute-start(f32[16,4,2,16,128]{4,3,2,1,0:T(8,128)S(1)} %all_to_all.20.mine), channel_id=1, source_target_pairs={{0,8},{8,0},{1,9},{9,1},{2,10},{10,2},{3,11},{11,3},{4,12},{12,4},... | collective-permute-start | bytes 3145736 | tf_op jit(solution)/shard_map/ppermute | solution.py:718
  43.8 1.4 %collective-permute-start.1 = (f32[2,64,4,128]{3,2,1,0:T(4,128)S(1)}, f32[2,64,4,128]{3,2,1,0:T(4,128)S(1)}, u32[]{:S(2)}, u32[]{:S(2)}) collective-permute-start(f32[2,64,4,128]{3,2,1,0:T(4,128)S(1)} %pad_maximum_fusion), channel_id=1, source_target_pairs={{0,1},{1,2},{2,3},{3,4},{4,5},{5,6},{6,7},{7,0},{8,9},{9,10},{10,1... | collective-permute-start | bytes 786440 | tf_op jit(solution)/shard_map/ppermute | solution.py:653
  45.3 2.4 %collective-permute-start.2 = (f32[2,64,4,128]{3,2,1,0:T(4,128)S(1)}, f32[2,64,4,128]{3,2,1,0:T(4,128)S(1)}, u32[]{:S(2)}, u32[]{:S(2)}) collective-permute-start(f32[2,64,4,128]{3,2,1,0:T(4,128)S(1)} %pad_maximum_fusion.1), channel_id=1, source_target_pairs={{1,0},{2,1},{3,2},{4,3},{5,4},{6,5},{7,6},{0,7},{9,8},{10,9},{11,1... | collective-permute-start | bytes 786440 | tf_op jit(solution)/shard_map/ppermute | solution.py:653
  48.3 0.7 copy.17.onehot
  49.6 4.2 %collective-permute-done.1.low = f32[2,64,4,128]{3,2,1,0:T(4,128)S(1)} collective-permute-done((f32[2,64,4,128]{3,2,1,0:T(4,128)S(1)}, f32[2,64,4,128]{3,2,1,0:T(4,128)S(1)}, u32[]{:S(2)}, u32[]{:S(2)}) %collective-permute-start.1) | collective-permute-done | bytes 262176 | tf_op jit(solution)/shard_map/ppermute | solution.py:653
  53.9 0.7 copy-done.7
  54.6 0.7 copy-done.8
  55.3 10.4 %shard_map.158 = (f32[64,16,128]{2,1,0:T(8,128)}, f32[64,16,128]{2,1,0:T(8,128)}, f32[64,16,128]{2,1,0:T(8,128)}, f32[64,16,128]{2,1,0:T(8,128)}, f32[64,16,128]...) custom-call(s32[1]{0:T(128)S(6)} %copy.19.src_cell, ...), custom_call_target="tpu_custom_call" | custom-call | flops 20971520 | bytes 2623508 | tf_op jit(solution)/shard_map/pallas_call | solution.py:36
  66.4 2.4 %shard_map.159 = (f32[64,16,128]{2,1,0:T(8,128)S(1)}, f32[64,16,128]{2,1,0:T(8,128)S(1)}, f32[64,16,128]{2,1,0:T(8,128)S(1)}, f32[64,16,128]{2,1,0:T(8,128)S(1)}...) custom-call(f32[64,16,128]{2,1,0:T(8,128)} %get-tuple-element.50.ref, ...), custom_call_target="tpu_custom_call" | custom-call | bytes 4726784 | tf_op jit(solution)/shard_map/pallas_call | solution.py:36
  68.9 1.8 %shard_map.160 = (f32[64,16,128]{2,1,0:T(8,128)S(1)}, f32[64,16,128]{2,1,0:T(8,128)S(1)}, f32[64,16,128]{2,1,0:T(8,128)S(1)}, f32[64,16,128]{2,1,0:T(8,128)S(1)}...) custom-call(f32[16,4,2,16,128]{4,3,2,1,0:T(8,128)S(1)} %all_to_all.2, ...), custom_call_target="tpu_custom_call" | custom-call | flops 2621440 | bytes 6815744 | tf_op jit(solution)/shard_map/pallas_call | solution.py:36
  70.7 3.6 %collective-permute-start.4 = (f32[80,4,128]{2,1,0:T(4,128)S(1)}, f32[80,4,128]{2,1,0:T(4,128)S(1)}, u32[]{:S(2)}, u32[]{:S(2)}) collective-permute-start(f32[80,4,128]{2,1,0:T(4,128)S(1)} %get-tuple-element.78), channel_id=1, source_target_pairs={{1,0},{2,1},{3,2},{4,3},{5,4},{6,5},{7,6},{0,7},{9,8},{10,9},{11,1... | collective-permute-start | bytes 491528 | tf_op jit(solution)/shard_map/ppermute | solution.py:653
  75.0 2.1 %shard_map.161 = (f32[64,16,128]{2,1,0:T(8,128)S(1)}, f32[64,16,128]{2,1,0:T(8,128)S(1)}) custom-call(s32[1]{0:T(128)S(6)} %copy.19.src_cell, f32[1,3]{1,0:T(1,128)S(1)} %copy-done.5, f32[64,16,128]{2,1,0:T(8,128)S(1)} %get-tuple-element.68.now.u_one.old, f32[64,16,128]{2,1,0:T(8,128)S(1)} %bitcast.1, f32[64,16,128]{2,1,0:T(8,128)S(1)} %get-tuple-element.69.aniso_h), custom_call_target="tpu_custom_call" | custom-call | flops 5242880 | bytes 1572880 | tf_op jit(solution)/shard_map/pallas_call | solution.py:36
  77.0 0.7 collective-permute-done.3.low.low_one
  77.7 1.7 %shard_map.162 = (f32[64,16,128]{2,1,0:T(8,128)S(1)}, f32[16,2,16,128]{3,2,1,0:T(8,128)S(1)}, f32[16,2,16,128]{3,2,1,0:T(8,128)S(1)}, f32[64,4,128]{2,1,0:T(4,128)}, f32[64,4,128]{2,1,0:T(4,128)S(1)}) custom-call(f32[64,16,128]{2,1,0:T(8,128)S(1)} %get-tuple-element.68.now.u_one.old, f32[64,16,128]{2,1,0:T(8,128)S(1)} %get-tuple-element.70.base, ...), custom_call_target="tpu_custom_call" | custom-call | flops 10485760 | bytes 4005888 | tf_op jit(solution)/shard_map/pallas_call | solution.py:36
  79.4 1.7 %collective-permute-start.5 = (f32[16,2,16,128]{3,2,1,0:T(8,128)S(1)}, f32[16,2,16,128]{3,2,1,0:T(8,128)S(1)}, u32[]{:S(2)}, u32[]{:S(2)}) collective-permute-start(f32[16,2,16,128]{3,2,1,0:T(8,128)S(1)} %get-tuple-element.80), channel_id=1, source_target_pairs={{0,8},{8,0},{1,9},{9,1},{2,10},{10,2},{3,11},{11,3},{4,12},{12,4},... | collective-permute-start | bytes 786440 | tf_op jit(solution)/shard_map/ppermute | solution.py:756
  81.1 1.2 collective-permute-done.5
  82.3 14.6 %all_to_all.21.parts = f32[16,2,16,128]{3,2,1,0:T(8,128)S(1)} all-to-all(f32[16,2,16,128]{3,2,1,0:T(8,128)S(1)} %add.3), channel_id=1, replica_groups=mesh['xh'=2,'z'=8,'core'=2,'xl'=2,'y'=4] {'xh','z'}, dimensions={0} | all-to-all | bytes 524288 | tf_op jit(solution)/shard_map/all_to_all | solution.py:757
  97.0 14.6 %all_to_all.22.mine = f32[16,2,16,128]{3,2,1,0:T(8,128)S(1)} all-to-all(f32[16,2,16,128]{3,2,1,0:T(8,128)S(1)} %shard_map.163), channel_id=1, replica_groups=mesh['xh'=2,'z'=8,'core'=2,'xl'=2,'y'=4] {'xh','z'}, dimensions={0} | all-to-all | bytes 524288 | tf_op jit(solution)/shard_map/all_to_all | solution.py:759
  111.6 3.1 %collective-permute-start.6 = (f32[16,2,16,128]{3,2,1,0:T(8,128)S(1)}, f32[16,2,16,128]{3,2,1,0:T(8,128)S(1)}, u32[]{:S(2)}, u32[]{:S(2)}) collective-permute-start(f32[16,2,16,128]{3,2,1,0:T(8,128)S(1)} %all_to_all.22.mine), channel_id=1, source_target_pairs={{0,8},{8,0},{1,9},{9,1},{2,10},{10,2},{3,11},{11,3},{4,12},{12,4},... | collective-permute-start | bytes 786440 | tf_op jit(solution)/shard_map/ppermute | solution.py:760
  114.7 3.2 %collective-permute-start.10 = (f32[64,4,128]{2,1,0:T(4,128)}, f32[64,4,128]{2,1,0:T(4,128)S(1)}, u32[]{:S(2)}, u32[]{:S(2)}) collective-permute-start(f32[64,4,128]{2,1,0:T(4,128)} %get-tuple-element.96), channel_id=1, source_target_pairs={{1,0},{2,1},{3,2},{4,3},{5,4},{6,5},{7,6},{0,7},{9,8},{10,9},{11,1... | collective-permute-start | bytes 393224 | tf_op jit(solution)/shard_map/ppermute | solution.py:653
  118.1 3.6 %collective-permute-start.8 = (f32[32,4,128]{2,1,0:T(4,128)S(1)}, f32[32,4,128]{2,1,0:T(4,128)S(1)}, u32[]{:S(2)}, u32[]{:S(2)}) collective-permute-start(f32[32,4,128]{2,1,0:T(4,128)S(1)} %get-tuple-element.89), channel_id=1, source_target_pairs={{1,0},{2,1},{3,2},{4,3},{5,4},{6,5},{7,6},{0,7},{9,8},{10,9},{11,1... | collective-permute-start | bytes 196616 | tf_op jit(solution)/shard_map/ppermute | solution.py:653
  121.8 1.9 %shard_map.165 = (f32[64,16,128]{2,1,0:T(8,128)S(1)}, f32[8,128]{1,0:T(8,128)S(1)}, f32[2,64,128]{2,1,0:T(8,128)S(1)}, f32[4,64,128]{2,1,0:T(8,128)S(1)}, f32[4,64,128]{2,1,0:T(8,128)S(1)}) custom-call(f32[64,16,128]{2,1,0:T(8,128)S(1)} %get-tuple-element.81.summed, f32[64,16,128]{2,1,0:T(8,128)S(1)} %get-tuple-element.82.smooth), custom_call_target="tpu_custom_call" | custom-call | flops 5242880 | bytes 1048576 | tf_op jit(solution)/shard_map/pallas_call | solution.py:36
  123.7 2.5 %collective-permute-done.7.low_sum = f32[32,4,128]{2,1,0:T(4,128)S(1)} collective-permute-done((f32[32,4,128]{2,1,0:T(4,128)S(1)}, f32[32,4,128]{2,1,0:T(4,128)S(1)}, u32[]{:S(2)}, u32[]{:S(2)}) %collective-permute-start.7) | collective-permute-done | bytes 65568 | tf_op jit(solution)/shard_map/ppermute | solution.py:653
  126.2 1.3 shard_map.166
  127.4 3.3 %all-to-all-start.3 = ((f32[8,1,128]{2,1,0:T(1,128)}), f32[8,1,128]{2,1,0:T(1,128)S(1)}, u32[]{:S(2)}, u32[]{:S(2)}) async-start(f32[8,1,128]{2,1,0:T(1,128)} %get-tuple-element.90), calls=%async_computation.3 | async-start | bytes 8192 | tf_op jit(solution)/shard_map/all_to_all | solution.py:800
  130.8 2.1 %shard_map.167 = (f32[64,16,128]{2,1,0:T(8,128)S(1)}, f32[64,16,128]{2,1,0:T(8,128)S(1)}) custom-call(s32[1]{0:T(128)S(6)} %copy.19.src_cell, f32[1,3]{1,0:T(1,128)S(1)} %copy-done.5, f32[64,16,128]{2,1,0:T(8,128)S(1)} %get-tuple-element.92.now.u_two, f32[64,16,128]{2,1,0:T(8,128)S(1)} %get-tuple-element.68.now.u_one.old, ...), custom_call_target="tpu_custom_call" | custom-call | flops 5242880 | bytes 1572880 | tf_op jit(solution)/shard_map/pallas_call | solution.py:36
  132.9 0.8 copy-done.2
  133.6 1.0 shard_map.168.change
  134.6 1.0 all-to-all-done.3.squares
  135.7 1.2 shard_map.169
  (33 shorter events, 2.0 us)
Async XLA Ops:
  2.6 41.1 %copy-start = (f32[1,64,16,128]{3,2,1,0:T(8,128)S(1)}, f32[1,64,16,128]{3,2,1,0:T(8,128)}, u32[]{:S(2)}) copy-start(f32[1,64,16,128]{3,2,1,0:T(8,128)} %u_cur.1) | copy-start | bytes 1572868
  2.6 41.1 %copy-start.6 = (f32[1,64,16,128]{3,2,1,0:T(8,128)S(1)}, f32[1,64,16,128]{3,2,1,0:T(8,128)}, u32[]{:S(2)}) copy-start(f32[1,64,16,128]{3,2,1,0:T(8,128)} %refs_9_.1) | copy-start | bytes 1572868
  40.8 28.0 %collective-permute-start = (f32[16,4,2,16,128]{4,3,2,1,0:T(8,128)S(1)}, f32[16,4,2,16,128]{4,3,2,1,0:T(8,128)}, u32[]{:S(2)}, u32[]{:S(2)}) collective-permute-start(f32[16,4,2,16,128]{4,3,2,1,0:T(8,128)S(1)} %all_to_all.20.mine), channel_id=1, source_target_pairs={{0,8},{8,0},{1,9},{9,1},{2,10},{10,2},{3,11},{11,3},{4,12},{12,4},... | collective-permute-start | bytes 3145736 | tf_op jit(solution)/shard_map/ppermute | solution.py:718
  43.8 10.0 %collective-permute-start.1 = (f32[2,64,4,128]{3,2,1,0:T(4,128)S(1)}, f32[2,64,4,128]{3,2,1,0:T(4,128)S(1)}, u32[]{:S(2)}, u32[]{:S(2)}) collective-permute-start(f32[2,64,4,128]{3,2,1,0:T(4,128)S(1)} %pad_maximum_fusion), channel_id=1, source_target_pairs={{0,1},{1,2},{2,3},{3,4},{4,5},{5,6},{6,7},{7,0},{8,9},{9,10},{10,1... | collective-permute-start | bytes 786440 | tf_op jit(solution)/shard_map/ppermute | solution.py:653
  45.2 3.1 %copy-start.9 = (s32[16,2,4]{0,2,1:T(4,128)S(1)}, s32[16,2,4]{0,2,1:T(4,128)}, u32[]{:S(2)}) copy-start(s32[16,2,4]{0,2,1:T(4,128)} %param.22) | copy-start | bytes 1540
  45.3 8.6 %collective-permute-start.2 = (f32[2,64,4,128]{3,2,1,0:T(4,128)S(1)}, f32[2,64,4,128]{3,2,1,0:T(4,128)S(1)}, u32[]{:S(2)}, u32[]{:S(2)}) collective-permute-start(f32[2,64,4,128]{3,2,1,0:T(4,128)S(1)} %pad_maximum_fusion.1), channel_id=1, source_target_pairs={{1,0},{2,1},{3,2},{4,3},{5,4},{6,5},{7,6},{0,7},{9,8},{10,9},{11,1... | collective-permute-start | bytes 786440 | tf_op jit(solution)/shard_map/ppermute | solution.py:653
  53.9 0.7 copy-start.7
  54.6 0.7 copy-start.8
  65.7 0.7 copy-start.4
  68.8 5.5 %copy-start.1 = (f32[1,64,16,128]{3,2,1,0:T(8,128)S(1)}, f32[1,64,16,128]{3,2,1,0:T(8,128)}, u32[]{:S(2)}) copy-start(f32[1,64,16,128]{3,2,1,0:T(8,128)} %u_cur.1) | copy-start | bytes 1572868
  70.7 7.1 %collective-permute-start.3 = (f32[80,4,128]{2,1,0:T(4,128)S(1)}, f32[80,4,128]{2,1,0:T(4,128)S(1)}, u32[]{:S(2)}, u32[]{:S(2)}) collective-permute-start(f32[80,4,128]{2,1,0:T(4,128)S(1)} %get-tuple-element.77), channel_id=1, source_target_pairs={{0,1},{1,2},{2,3},{3,4},{4,5},{5,6},{6,7},{7,0},{8,9},{9,10},{10,1... | collective-permute-start | bytes 491528 | tf_op jit(solution)/shard_map/ppermute | solution.py:653
  70.7 7.0 %collective-permute-start.4 = (f32[80,4,128]{2,1,0:T(4,128)S(1)}, f32[80,4,128]{2,1,0:T(4,128)S(1)}, u32[]{:S(2)}, u32[]{:S(2)}) collective-permute-start(f32[80,4,128]{2,1,0:T(4,128)S(1)} %get-tuple-element.78), channel_id=1, source_target_pairs={{1,0},{2,1},{3,2},{4,3},{5,4},{6,5},{7,6},{0,7},{9,8},{10,9},{11,1... | collective-permute-start | bytes 491528 | tf_op jit(solution)/shard_map/ppermute | solution.py:653
  74.3 0.7 copy-start.5
  79.4 2.9 %collective-permute-start.5 = (f32[16,2,16,128]{3,2,1,0:T(8,128)S(1)}, f32[16,2,16,128]{3,2,1,0:T(8,128)S(1)}, u32[]{:S(2)}, u32[]{:S(2)}) collective-permute-start(f32[16,2,16,128]{3,2,1,0:T(8,128)S(1)} %get-tuple-element.80), channel_id=1, source_target_pairs={{0,8},{8,0},{1,9},{9,1},{2,10},{10,2},{3,11},{11,3},{4,12},{12,4},... | collective-permute-start | bytes 786440 | tf_op jit(solution)/shard_map/ppermute | solution.py:756
  111.6 6.3 %collective-permute-start.6 = (f32[16,2,16,128]{3,2,1,0:T(8,128)S(1)}, f32[16,2,16,128]{3,2,1,0:T(8,128)S(1)}, u32[]{:S(2)}, u32[]{:S(2)}) collective-permute-start(f32[16,2,16,128]{3,2,1,0:T(8,128)S(1)} %all_to_all.22.mine), channel_id=1, source_target_pairs={{0,8},{8,0},{1,9},{9,1},{2,10},{10,2},{3,11},{11,3},{4,12},{12,4},... | collective-permute-start | bytes 786440 | tf_op jit(solution)/shard_map/ppermute | solution.py:760
  114.7 19.0 %collective-permute-start.10 = (f32[64,4,128]{2,1,0:T(4,128)}, f32[64,4,128]{2,1,0:T(4,128)S(1)}, u32[]{:S(2)}, u32[]{:S(2)}) collective-permute-start(f32[64,4,128]{2,1,0:T(4,128)} %get-tuple-element.96), channel_id=1, source_target_pairs={{1,0},{2,1},{3,2},{4,3},{5,4},{6,5},{7,6},{0,7},{9,8},{10,9},{11,1... | collective-permute-start | bytes 393224 | tf_op jit(solution)/shard_map/ppermute | solution.py:653
  117.9 15.8 %collective-permute-start.9 = (f32[64,4,128]{2,1,0:T(4,128)S(1)}, f32[64,4,128]{2,1,0:T(4,128)S(1)}, u32[]{:S(2)}, u32[]{:S(2)}) collective-permute-start(f32[64,4,128]{2,1,0:T(4,128)S(1)} %get-tuple-element.95), channel_id=1, source_target_pairs={{0,1},{1,2},{2,3},{3,4},{4,5},{5,6},{6,7},{7,0},{8,9},{9,10},{10,1... | collective-permute-start | bytes 393224 | tf_op jit(solution)/shard_map/ppermute | solution.py:653
  118.0 8.1 %collective-permute-start.7 = (f32[32,4,128]{2,1,0:T(4,128)S(1)}, f32[32,4,128]{2,1,0:T(4,128)S(1)}, u32[]{:S(2)}, u32[]{:S(2)}) collective-permute-start(f32[32,4,128]{2,1,0:T(4,128)S(1)} %get-tuple-element.88), channel_id=1, source_target_pairs={{0,1},{1,2},{2,3},{3,4},{4,5},{5,6},{6,7},{7,0},{8,9},{9,10},{10,1... | collective-permute-start | bytes 196616 | tf_op jit(solution)/shard_map/ppermute | solution.py:653
  118.1 8.1 %collective-permute-start.8 = (f32[32,4,128]{2,1,0:T(4,128)S(1)}, f32[32,4,128]{2,1,0:T(4,128)S(1)}, u32[]{:S(2)}, u32[]{:S(2)}) collective-permute-start(f32[32,4,128]{2,1,0:T(4,128)S(1)} %get-tuple-element.89), channel_id=1, source_target_pairs={{1,0},{2,1},{3,2},{4,3},{5,4},{6,5},{7,6},{0,7},{9,8},{10,9},{11,1... | collective-permute-start | bytes 196616 | tf_op jit(solution)/shard_map/ppermute | solution.py:653
  127.4 8.2 %all-to-all-start.3 = ((f32[8,1,128]{2,1,0:T(1,128)}), f32[8,1,128]{2,1,0:T(1,128)S(1)}, u32[]{:S(2)}, u32[]{:S(2)}) async-start(f32[8,1,128]{2,1,0:T(1,128)} %get-tuple-element.90), calls=%async_computation.3 | async-start | bytes 8192 | tf_op jit(solution)/shard_map/all_to_all | solution.py:800
  132.8 0.8 copy-start.2
  133.6 2.0 %copy-start.3 = (f32[64,16,128]{2,1,0:T(8,128)S(1)}, f32[64,16,128]{2,1,0:T(8,128)}, u32[]{:S(2)}) copy-start(f32[64,16,128]{2,1,0:T(8,128)} %copy-done.2) | copy-start | bytes 1572868

commit v7 on v6

--- a/solution.py
+++ b/solution.py
@@ -323,11 +323,26 @@
     add_at(base, src_cell[0], src_wave[0, step_index])
 
 
+def side_halo_kernel(
+    step_index, src_cell, src_wave, now, old, aniso_h, low, high,
+    base, side, low_in, high_in, rows, sem,
+):
+    copies = [
+        pltpu.make_async_copy(low, low_in, sem.at[0]),
+        pltpu.make_async_copy(high, high_in, sem.at[1]),
+    ]
+    for copy in copies:
+        copy.start()
+    side_kernel(step_index, src_cell, src_wave, now, old, aniso_h, base, side, rows)
+    for copy in copies:
+        copy.wait()
+
+
 def second_kernel(
     u_one, base, side, a_one, grad, weight, model, aniso_c, low, high,
-    u_two, keep, send, low_two, high_two, pad, first_z, dep,
+    u_two, keep, send, pad, first_z, dep,
 ):
-    cells_x, cells_z, _ = u_two.shape
+    cells_x = u_two.shape[0]
     fill_depth(pad, lambda at: u_one[at], lambda at: low[at], lambda at: high[at])
     depth_pass(pad, first_z, dep)
     own = position()[1] == 0
@@ -337,13 +352,20 @@
         x = step * CHUNK
         at = pl.ds(x, CHUNK)
         k_u = side[at] + dep[at] + aniso_c[at] * crossing(first_z, x)
-        new = base[at] + model[at] * k_u
-        u_two[at] = new
-        low_two[at] = new[:, :REACH]
-        high_two[at] = new[:, cells_z - REACH :]
+        u_two[at] = base[at] + model[at] * k_u
         total = weight[...] * (grad[at] + a_one[at] * k_u)
         keep[step] = jnp.where(own, total[:2], total[2:])
         send[step] = jnp.where(own, total[2:], total[:2])
+
+
+def rim_kernel(field, low, high):
+    cells_x, cells_z, _ = field.shape
+
+    @pl.loop(0, cells_x // CHUNK, unroll=2)
+    def _(step):
+        at = pl.ds(step * CHUNK, CHUNK)
+        low[at] = field[at, :REACH]
+        high[at] = field[at, cells_z - REACH :]
 
 
 def sum_kernel(parts, out):
@@ -745,11 +767,11 @@
     )
     split = f32(peers, rows, cells_z, cells_y)
     edge = f32(cells_x, REACH, cells_y)
-    u_two, keep, send, low_edge, high_edge = call(
+    u_two, keep, send = call(
         second_kernel,
         (u_one, base, side, a_one, grad, weight, model_slab, c_slab, low_one, high_one),
         0,
-        (slab, split, split, edge, edge),
+        (slab, split, split),
         (pad, first_z, dep),
         work,
     )
@@ -758,19 +780,21 @@
     total = call(sum_kernel, (shares,), 0, split)
     mine = lax.all_to_all(total, PEERS, 0, 0, tiled=True)
     other = lax.ppermute(mine, "core", SWAP)
+    low_edge, high_edge = call(rim_kernel, (u_two,), 0, (edge, edge))
     low_two, high_two = shift(low_edge, high_edge)
     payload = f32(2 * peers, 4, cells_y)
     summed, low_edge, high_edge = call(
         join_kernel, (mine, other), 0, (slab, payload, payload)
     )
     low_sum, high_sum = shift(low_edge, high_edge)
-    base, side = call(
-        functools.partial(side_kernel, 2),
-        (src_cell, src_wave, u_two, u_one, h_slab),
+    base, side, low_two, high_two = call(
+        functools.partial(side_halo_kernel, 2),
+        (src_cell, src_wave, u_two, u_one, h_slab, low_two, high_two),
         2,
-        (slab, slab),
-        (padded_rows,),
+        (slab, slab, edge, edge),
+        (padded_rows, pltpu.SemaphoreType.DMA((2,))),
         work // 2,
+        hbm_in=(5, 6),
     )
     edges = f32(4, cells_x, cells_y)
     smoothed, inner, own_g, own_s, own_out = call(

time: 138 us -> 138 us (level)
    pallas_call x13 -> x14, Pallas kernels: 27.8 us -> 28.2 us  [call(): pl.pallas_call(kernel, out_shape=outs, in_specs=[spec(i) for i in range(l...]
    unnamed x21 -> x25, local copies, waits for them, and re-layouts: 4.29 us -> 4.27 us
  transfers between devices with their start and end apart: 12 -> 12, of which waited for: 5 -> 5; matrix products, arithmetic and copies ran while one was open for 1% -> 1% of each run, Pallas kernels for 15% -> 16%
where the time goes in v7:
time: 138 us; the launch traced here: 137 us
  blocking collectives  67.4 us (49%)
  Pallas kernels  28.2 us (20%)
  starting transfers between devices  25.3 us (18%)
  waiting for transfers between devices  9.27 us (7%)
  local copies, waits for them, and re-layouts  4.37 us (3%)
  between operations  2.17 us (2%)
    all_to_all x1, blocking collectives, body(): mine = lax.all_to_all(spread, PEERS, 0, 0, tiled=True)  38.2 us
    pallas_call x14, Pallas kernels, call(): pl.pallas_call(kernel, out_shape=outs, in_specs=[spec(i) for i in range(l...  28.2 us
    all_to_all x1, blocking collectives, body(): mine = lax.all_to_all(total, PEERS, 0, 0, tiled=True)  14.6 us
    all_to_all x1, blocking collectives, body(): shares = lax.all_to_all(chip_sum, PEERS, 0, 0, tiled=True)  14.6 us
    ppermute x4, starting transfers between devices, shift(): lax.ppermute(low_edge, DEPTH, backward)  12.8 us
    ppermute x4, waiting for transfers between devices, shift(): lax.ppermute(high_edge, DEPTH, forward)  7.42 us
    ppermute x2, starting transfers between devices, body(): other = lax.ppermute(mine, 'core', SWAP)  5.9 us
    unnamed x25, local copies, waits for them, and re-layouts  4.27 us
  transfers between devices with their start and end apart: 12, of which 5 were waited for; matrix products, arithmetic and copies ran while one was open for 1% of the time, Pallas kernels for 16%

profile of v7, /device:TPU:1, one launch (start us, length us, event | category | flops | bytes accessed | tf_op | source)
XLA Modules:
  0.0 137.0 jit_solution(1467721237962196126)
XLA Ops:
  0.6 1.9 %shard_map.157 = f32[16,4,2,16,128]{4,3,2,1,0:T(8,128)} custom-call(f32[2,16,128]{2,1,0:T(8,128)} %model.1, f32[2,16,128]{2,1,0:T(8,128)} %aniso_h.1, f32[2,16,128]{2,1,0:T(8,128)} %aniso_c.1, f32[2,16,128]{2,1,0:T(8,128)} %smooth.1), custom_call_target="tpu_custom_call" | custom-call | bytes 65536 | tf_op jit(solution)/shard_map/pallas_call | solution.py:36
  2.6 38.2 %all_to_all.20.mine = f32[16,4,2,16,128]{4,3,2,1,0:T(8,128)S(1)} all-to-all(f32[16,4,2,16,128]{4,3,2,1,0:T(8,128)} %shard_map.157), channel_id=1, replica_groups=mesh['xh'=2,'z'=8,'core'=2,'xl'=2,'y'=4] {'xh','z'}, dimensions={0} | all-to-all | bytes 2097152 | tf_op jit(solution)/shard_map/all_to_all | solution.py:720
  40.8 2.8 %collective-permute-start = (f32[16,4,2,16,128]{4,3,2,1,0:T(8,128)S(1)}, f32[16,4,2,16,128]{4,3,2,1,0:T(8,128)}, u32[]{:S(2)}, u32[]{:S(2)}) collective-permute-start(f32[16,4,2,16,128]{4,3,2,1,0:T(8,128)S(1)} %all_to_all.20.mine), channel_id=1, source_target_pairs={{0,8},{8,0},{1,9},{9,1},{2,10},{10,2},{3,11},{11,3},{4,12},{12,4},... | collective-permute-start | bytes 3145736 | tf_op jit(solution)/shard_map/ppermute | solution.py:740
  43.8 1.4 %collective-permute-start.1 = (f32[2,64,4,128]{3,2,1,0:T(4,128)S(1)}, f32[2,64,4,128]{3,2,1,0:T(4,128)S(1)}, u32[]{:S(2)}, u32[]{:S(2)}) collective-permute-start(f32[2,64,4,128]{3,2,1,0:T(4,128)S(1)} %pad_maximum_fusion), channel_id=1, source_target_pairs={{0,1},{1,2},{2,3},{3,4},{4,5},{5,6},{6,7},{7,0},{8,9},{9,10},{10,1... | collective-permute-start | bytes 786440 | tf_op jit(solution)/shard_map/ppermute | solution.py:675
  45.3 2.4 %collective-permute-start.2 = (f32[2,64,4,128]{3,2,1,0:T(4,128)S(1)}, f32[2,64,4,128]{3,2,1,0:T(4,128)S(1)}, u32[]{:S(2)}, u32[]{:S(2)}) collective-permute-start(f32[2,64,4,128]{3,2,1,0:T(4,128)S(1)} %pad_maximum_fusion.1), channel_id=1, source_target_pairs={{1,0},{2,1},{3,2},{4,3},{5,4},{6,5},{7,6},{0,7},{9,8},{10,9},{11,1... | collective-permute-start | bytes 786440 | tf_op jit(solution)/shard_map/ppermute | solution.py:675
  48.3 0.7 copy.17.onehot
  49.6 4.2 %collective-permute-done.1.low = f32[2,64,4,128]{3,2,1,0:T(4,128)S(1)} collective-permute-done((f32[2,64,4,128]{3,2,1,0:T(4,128)S(1)}, f32[2,64,4,128]{3,2,1,0:T(4,128)S(1)}, u32[]{:S(2)}, u32[]{:S(2)}) %collective-permute-start.1) | collective-permute-done | bytes 262176 | tf_op jit(solution)/shard_map/ppermute | solution.py:675
  53.9 0.7 copy-done.9
  54.6 0.7 copy-done.10
  55.3 10.4 %shard_map.158 = (f32[64,16,128]{2,1,0:T(8,128)}, f32[64,16,128]{2,1,0:T(8,128)}, f32[64,16,128]{2,1,0:T(8,128)}, f32[64,16,128]{2,1,0:T(8,128)}, f32[64,16,128]...) custom-call(s32[1]{0:T(128)S(6)} %copy.19.src_cell, ...), custom_call_target="tpu_custom_call" | custom-call | flops 20971520 | bytes 2623508 | tf_op jit(solution)/shard_map/pallas_call | solution.py:36
  65.7 0.7 copy-done.6
  66.4 2.4 %shard_map.159 = (f32[64,16,128]{2,1,0:T(8,128)S(1)}, f32[64,16,128]{2,1,0:T(8,128)S(1)}, f32[64,16,128]{2,1,0:T(8,128)S(1)}, f32[64,16,128]{2,1,0:T(8,128)S(1)}...) custom-call(f32[64,16,128]{2,1,0:T(8,128)} %get-tuple-element.52.ref, ...), custom_call_target="tpu_custom_call" | custom-call | bytes 4726784 | tf_op jit(solution)/shard_map/pallas_call | solution.py:36
  68.8 1.8 %shard_map.160 = (f32[64,16,128]{2,1,0:T(8,128)S(1)}, f32[64,16,128]{2,1,0:T(8,128)S(1)}, f32[64,16,128]{2,1,0:T(8,128)S(1)}, f32[64,16,128]{2,1,0:T(8,128)S(1)}...) custom-call(f32[16,4,2,16,128]{4,3,2,1,0:T(8,128)S(1)} %all_to_all.2, ...), custom_call_target="tpu_custom_call" | custom-call | flops 2621440 | bytes 6815744 | tf_op jit(solution)/shard_map/pallas_call | solution.py:36
  70.7 3.6 %collective-permute-start.4 = (f32[80,4,128]{2,1,0:T(4,128)S(1)}, f32[80,4,128]{2,1,0:T(4,128)S(1)}, u32[]{:S(2)}, u32[]{:S(2)}) collective-permute-start(f32[80,4,128]{2,1,0:T(4,128)S(1)} %get-tuple-element.80), channel_id=1, source_target_pairs={{1,0},{2,1},{3,2},{4,3},{5,4},{6,5},{7,6},{0,7},{9,8},{10,9},{11,1... | collective-permute-start | bytes 491528 | tf_op jit(solution)/shard_map/ppermute | solution.py:675
  74.9 2.1 %shard_map.161 = (f32[64,16,128]{2,1,0:T(8,128)S(1)}, f32[64,16,128]{2,1,0:T(8,128)S(1)}) custom-call(s32[1]{0:T(128)S(6)} %copy.19.src_cell, f32[1,3]{1,0:T(1,128)S(1)} %copy-done.7, f32[64,16,128]{2,1,0:T(8,128)S(1)} %get-tuple-element.70.now.u_one.old, f32[64,16,128]{2,1,0:T(8,128)S(1)} %bitcast.1, f32[64,16,128]{2,1,0:T(8,128)S(1)} %get-tuple-element.71.aniso_h), custom_call_target="tpu_custom_call" | custom-call | flops 5242880 | bytes 1572880 | tf_op jit(solution)/shard_map/pallas_call | solution.py:36
  77.7 1.0 shard_map.162
  78.8 1.8 %collective-permute-start.5 = (f32[16,2,16,128]{3,2,1,0:T(8,128)S(1)}, f32[16,2,16,128]{3,2,1,0:T(8,128)S(1)}, u32[]{:S(2)}, u32[]{:S(2)}) collective-permute-start(f32[16,2,16,128]{3,2,1,0:T(8,128)S(1)} %get-tuple-element.82), channel_id=1, source_target_pairs={{0,8},{8,0},{1,9},{9,1},{2,10},{10,2},{3,11},{11,3},{4,12},{12,4},... | collective-permute-start | bytes 786440 | tf_op jit(solution)/shard_map/ppermute | solution.py:778
  80.6 1.2 collective-permute-done.5
  81.8 14.6 %all_to_all.21.parts = f32[16,2,16,128]{3,2,1,0:T(8,128)S(1)} all-to-all(f32[16,2,16,128]{3,2,1,0:T(8,128)S(1)} %add.3), channel_id=1, replica_groups=mesh['xh'=2,'z'=8,'core'=2,'xl'=2,'y'=4] {'xh','z'}, dimensions={0} | all-to-all | bytes 524288 | tf_op jit(solution)/shard_map/all_to_all | solution.py:779
  96.4 14.6 %all_to_all.22.mine = f32[16,2,16,128]{3,2,1,0:T(8,128)S(1)} all-to-all(f32[16,2,16,128]{3,2,1,0:T(8,128)S(1)} %shard_map.163), channel_id=1, replica_groups=mesh['xh'=2,'z'=8,'core'=2,'xl'=2,'y'=4] {'xh','z'}, dimensions={0} | all-to-all | bytes 524288 | tf_op jit(solution)/shard_map/all_to_all | solution.py:781
  111.0 3.1 %collective-permute-start.6 = (f32[16,2,16,128]{3,2,1,0:T(8,128)S(1)}, f32[16,2,16,128]{3,2,1,0:T(8,128)S(1)}, u32[]{:S(2)}, u32[]{:S(2)}) collective-permute-start(f32[16,2,16,128]{3,2,1,0:T(8,128)S(1)} %all_to_all.22.mine), channel_id=1, source_target_pairs={{0,8},{8,0},{1,9},{9,1},{2,10},{10,2},{3,11},{11,3},{4,12},{12,4},... | collective-permute-start | bytes 786440 | tf_op jit(solution)/shard_map/ppermute | solution.py:782
  114.1 0.7 shard_map.167
  114.8 3.2 %collective-permute-start.10 = (f32[64,4,128]{2,1,0:T(4,128)}, f32[64,4,128]{2,1,0:T(4,128)S(1)}, u32[]{:S(2)}, u32[]{:S(2)}) collective-permute-start(f32[64,4,128]{2,1,0:T(4,128)} %get-tuple-element.96), channel_id=1, source_target_pairs={{1,0},{2,1},{3,2},{4,3},{5,4},{6,5},{7,6},{0,7},{9,8},{10,9},{11,1... | collective-permute-start | bytes 393224 | tf_op jit(solution)/shard_map/ppermute | solution.py:675
  118.3 3.6 %collective-permute-start.8 = (f32[32,4,128]{2,1,0:T(4,128)S(1)}, f32[32,4,128]{2,1,0:T(4,128)S(1)}, u32[]{:S(2)}, u32[]{:S(2)}) collective-permute-start(f32[32,4,128]{2,1,0:T(4,128)S(1)} %get-tuple-element.91), channel_id=1, source_target_pairs={{1,0},{2,1},{3,2},{4,3},{5,4},{6,5},{7,6},{0,7},{9,8},{10,9},{11,1... | collective-permute-start | bytes 196616 | tf_op jit(solution)/shard_map/ppermute | solution.py:675
  121.9 1.9 %shard_map.165 = (f32[64,16,128]{2,1,0:T(8,128)S(1)}, f32[8,128]{1,0:T(8,128)S(1)}, f32[2,64,128]{2,1,0:T(8,128)S(1)}, f32[4,64,128]{2,1,0:T(8,128)S(1)}, f32[4,64,128]{2,1,0:T(8,128)S(1)}) custom-call(f32[64,16,128]{2,1,0:T(8,128)S(1)} %get-tuple-element.83.summed, f32[64,16,128]{2,1,0:T(8,128)S(1)} %get-tuple-element.84.smooth), custom_call_target="tpu_custom_call" | custom-call | flops 5242880 | bytes 1048576 | tf_op jit(solution)/shard_map/pallas_call | solution.py:36
  123.8 2.5 %collective-permute-done.7.low_sum = f32[32,4,128]{2,1,0:T(4,128)S(1)} collective-permute-done((f32[32,4,128]{2,1,0:T(4,128)S(1)}, f32[32,4,128]{2,1,0:T(4,128)S(1)}, u32[]{:S(2)}, u32[]{:S(2)}) %collective-permute-start.7) | collective-permute-done | bytes 65568 | tf_op jit(solution)/shard_map/ppermute | solution.py:675
  126.3 1.3 shard_map.166
  127.6 3.3 %all-to-all-start.3 = ((f32[8,1,128]{2,1,0:T(1,128)}), f32[8,1,128]{2,1,0:T(1,128)S(1)}, u32[]{:S(2)}, u32[]{:S(2)}) async-start(f32[8,1,128]{2,1,0:T(1,128)} %get-tuple-element.92), calls=%async_computation.3 | async-start | bytes 8192 | tf_op jit(solution)/shard_map/all_to_all | solution.py:824
  130.9 2.4 %shard_map.168 = (f32[64,16,128]{2,1,0:T(8,128)S(1)}, f32[64,16,128]{2,1,0:T(8,128)S(1)}, f32[64,4,128]{2,1,0:T(4,128)S(1)}, f32[64,4,128]{2,1,0:T(4,128)S(1)}) custom-call(s32[1]{0:T(128)S(6)} %copy.19.src_cell, f32[1,3]{1,0:T(1,128)S(1)} %copy-done.7, f32[64,16,128]{2,1,0:T(8,128)S(1)} %get-tuple-element.94.field.now.u_two, ...), custom_call_target="tpu_custom_call" | custom-call | flops 5242880 | bytes 1835024 | tf_op jit(solution)/shard_map/pallas_call | solution.py:36
  133.4 0.8 copy-done.4
  134.2 0.9 shard_map.169.change
  135.8 1.2 shard_map.170
  (38 shorter events, 2.7 us)
Async XLA Ops:
  2.6 41.1 %copy-start = (f32[1,64,16,128]{3,2,1,0:T(8,128)S(1)}, f32[1,64,16,128]{3,2,1,0:T(8,128)}, u32[]{:S(2)}) copy-start(f32[1,64,16,128]{3,2,1,0:T(8,128)} %u_cur.1) | copy-start | bytes 1572868
  2.6 41.1 %copy-start.8 = (f32[1,64,16,128]{3,2,1,0:T(8,128)S(1)}, f32[1,64,16,128]{3,2,1,0:T(8,128)}, u32[]{:S(2)}) copy-start(f32[1,64,16,128]{3,2,1,0:T(8,128)} %refs_9_.1) | copy-start | bytes 1572868
  40.8 28.0 %collective-permute-start = (f32[16,4,2,16,128]{4,3,2,1,0:T(8,128)S(1)}, f32[16,4,2,16,128]{4,3,2,1,0:T(8,128)}, u32[]{:S(2)}, u32[]{:S(2)}) collective-permute-start(f32[16,4,2,16,128]{4,3,2,1,0:T(8,128)S(1)} %all_to_all.20.mine), channel_id=1, source_target_pairs={{0,8},{8,0},{1,9},{9,1},{2,10},{10,2},{3,11},{11,3},{4,12},{12,4},... | collective-permute-start | bytes 3145736 | tf_op jit(solution)/shard_map/ppermute | solution.py:740
  43.8 10.0 %collective-permute-start.1 = (f32[2,64,4,128]{3,2,1,0:T(4,128)S(1)}, f32[2,64,4,128]{3,2,1,0:T(4,128)S(1)}, u32[]{:S(2)}, u32[]{:S(2)}) collective-permute-start(f32[2,64,4,128]{3,2,1,0:T(4,128)S(1)} %pad_maximum_fusion), channel_id=1, source_target_pairs={{0,1},{1,2},{2,3},{3,4},{4,5},{5,6},{6,7},{7,0},{8,9},{9,10},{10,1... | collective-permute-start | bytes 786440 | tf_op jit(solution)/shard_map/ppermute | solution.py:675
  45.2 3.1 %copy-start.11 = (s32[16,2,4]{0,2,1:T(4,128)S(1)}, s32[16,2,4]{0,2,1:T(4,128)}, u32[]{:S(2)}) copy-start(s32[16,2,4]{0,2,1:T(4,128)} %param.22) | copy-start | bytes 1540
  45.3 8.6 %collective-permute-start.2 = (f32[2,64,4,128]{3,2,1,0:T(4,128)S(1)}, f32[2,64,4,128]{3,2,1,0:T(4,128)S(1)}, u32[]{:S(2)}, u32[]{:S(2)}) collective-permute-start(f32[2,64,4,128]{3,2,1,0:T(4,128)S(1)} %pad_maximum_fusion.1), channel_id=1, source_target_pairs={{1,0},{2,1},{3,2},{4,3},{5,4},{6,5},{7,6},{0,7},{9,8},{10,9},{11,1... | collective-permute-start | bytes 786440 | tf_op jit(solution)/shard_map/ppermute | solution.py:675
  53.9 0.7 copy-start.9
  54.6 0.7 copy-start.10
  65.7 0.7 copy-start.6
  68.8 5.5 %copy-start.1 = (f32[1,64,16,128]{3,2,1,0:T(8,128)S(1)}, f32[1,64,16,128]{3,2,1,0:T(8,128)}, u32[]{:S(2)}) copy-start(f32[1,64,16,128]{3,2,1,0:T(8,128)} %u_cur.1) | copy-start | bytes 1572868
  70.6 6.4 %copy-start.2 = (f32[64,16,128]{2,1,0:T(8,128)}, f32[64,16,128]{2,1,0:T(8,128)S(1)}, u32[]{:S(2)}) copy-start(f32[64,16,128]{2,1,0:T(8,128)S(1)} %get-tuple-element.71.aniso_h) | copy-start | bytes 1572868
  70.6 7.1 %collective-permute-start.3 = (f32[80,4,128]{2,1,0:T(4,128)S(1)}, f32[80,4,128]{2,1,0:T(4,128)S(1)}, u32[]{:S(2)}, u32[]{:S(2)}) collective-permute-start(f32[80,4,128]{2,1,0:T(4,128)S(1)} %get-tuple-element.79), channel_id=1, source_target_pairs={{0,1},{1,2},{2,3},{3,4},{4,5},{5,6},{6,7},{7,0},{8,9},{9,10},{10,1... | collective-permute-start | bytes 491528 | tf_op jit(solution)/shard_map/ppermute | solution.py:675
  70.7 7.0 %collective-permute-start.4 = (f32[80,4,128]{2,1,0:T(4,128)S(1)}, f32[80,4,128]{2,1,0:T(4,128)S(1)}, u32[]{:S(2)}, u32[]{:S(2)}) collective-permute-start(f32[80,4,128]{2,1,0:T(4,128)S(1)} %get-tuple-element.80), channel_id=1, source_target_pairs={{1,0},{2,1},{3,2},{4,3},{5,4},{6,5},{7,6},{0,7},{9,8},{10,9},{11,1... | collective-permute-start | bytes 491528 | tf_op jit(solution)/shard_map/ppermute | solution.py:675
  74.3 0.7 copy-start.7
  78.8 3.0 %collective-permute-start.5 = (f32[16,2,16,128]{3,2,1,0:T(8,128)S(1)}, f32[16,2,16,128]{3,2,1,0:T(8,128)S(1)}, u32[]{:S(2)}, u32[]{:S(2)}) collective-permute-start(f32[16,2,16,128]{3,2,1,0:T(8,128)S(1)} %get-tuple-element.82), channel_id=1, source_target_pairs={{0,8},{8,0},{1,9},{9,1},{2,10},{10,2},{3,11},{11,3},{4,12},{12,4},... | collective-permute-start | bytes 786440 | tf_op jit(solution)/shard_map/ppermute | solution.py:778
  111.0 7.0 %collective-permute-start.6 = (f32[16,2,16,128]{3,2,1,0:T(8,128)S(1)}, f32[16,2,16,128]{3,2,1,0:T(8,128)S(1)}, u32[]{:S(2)}, u32[]{:S(2)}) collective-permute-start(f32[16,2,16,128]{3,2,1,0:T(8,128)S(1)} %all_to_all.22.mine), channel_id=1, source_target_pairs={{0,8},{8,0},{1,9},{9,1},{2,10},{10,2},{3,11},{11,3},{4,12},{12,4},... | collective-permute-start | bytes 786440 | tf_op jit(solution)/shard_map/ppermute | solution.py:782
  114.8 16.1 %collective-permute-start.10 = (f32[64,4,128]{2,1,0:T(4,128)}, f32[64,4,128]{2,1,0:T(4,128)S(1)}, u32[]{:S(2)}, u32[]{:S(2)}) collective-permute-start(f32[64,4,128]{2,1,0:T(4,128)} %get-tuple-element.96), channel_id=1, source_target_pairs={{1,0},{2,1},{3,2},{4,3},{5,4},{6,5},{7,6},{0,7},{9,8},{10,9},{11,1... | collective-permute-start | bytes 393224 | tf_op jit(solution)/shard_map/ppermute | solution.py:675
  118.0 12.9 %collective-permute-start.9 = (f32[64,4,128]{2,1,0:T(4,128)S(1)}, f32[64,4,128]{2,1,0:T(4,128)S(1)}, u32[]{:S(2)}, u32[]{:S(2)}) collective-permute-start(f32[64,4,128]{2,1,0:T(4,128)S(1)} %get-tuple-element.95), channel_id=1, source_target_pairs={{0,1},{1,2},{2,3},{3,4},{4,5},{5,6},{6,7},{7,0},{8,9},{9,10},{10,1... | collective-permute-start | bytes 393224 | tf_op jit(solution)/shard_map/ppermute | solution.py:675
  118.2 8.1 %collective-permute-start.7 = (f32[32,4,128]{2,1,0:T(4,128)S(1)}, f32[32,4,128]{2,1,0:T(4,128)S(1)}, u32[]{:S(2)}, u32[]{:S(2)}) collective-permute-start(f32[32,4,128]{2,1,0:T(4,128)S(1)} %get-tuple-element.90), channel_id=1, source_target_pairs={{0,1},{1,2},{2,3},{3,4},{4,5},{5,6},{6,7},{7,0},{8,9},{9,10},{10,1... | collective-permute-start | bytes 196616 | tf_op jit(solution)/shard_map/ppermute | solution.py:675
  118.3 8.0 %collective-permute-start.8 = (f32[32,4,128]{2,1,0:T(4,128)S(1)}, f32[32,4,128]{2,1,0:T(4,128)S(1)}, u32[]{:S(2)}, u32[]{:S(2)}) collective-permute-start(f32[32,4,128]{2,1,0:T(4,128)S(1)} %get-tuple-element.91), channel_id=1, source_target_pairs={{1,0},{2,1},{3,2},{4,3},{5,4},{6,5},{7,6},{0,7},{9,8},{10,9},{11,1... | collective-permute-start | bytes 196616 | tf_op jit(solution)/shard_map/ppermute | solution.py:675
  126.3 4.6 %copy-start.3 = (f32[64,16,128]{2,1,0:T(8,128)S(1)}, f32[64,16,128]{2,1,0:T(8,128)}, u32[]{:S(2)}) copy-start(f32[64,16,128]{2,1,0:T(8,128)} %copy-done.2) | copy-start | bytes 1572868
  127.6 8.2 %all-to-all-start.3 = ((f32[8,1,128]{2,1,0:T(1,128)}), f32[8,1,128]{2,1,0:T(1,128)S(1)}, u32[]{:S(2)}, u32[]{:S(2)}) async-start(f32[8,1,128]{2,1,0:T(1,128)} %get-tuple-element.92), calls=%async_computation.3 | async-start | bytes 8192 | tf_op jit(solution)/shard_map/all_to_all | solution.py:824
  133.4 0.8 copy-start.4
  134.2 1.6 %copy-start.5 = (f32[64,16,128]{2,1,0:T(8,128)S(1)}, f32[64,16,128]{2,1,0:T(8,128)}, u32[]{:S(2)}) copy-start(f32[64,16,128]{2,1,0:T(8,128)} %copy-done.4) | copy-start | bytes 1572868

commit v8 on v7

--- a/solution.py
+++ b/solution.py
@@ -1,5 +1,3 @@
-import functools
-
 import jax
 import jax.numpy as jnp
 from jax import lax
@@ -18,7 +16,7 @@
 REACH = 4
 MID = 8
 CHUNK = 4
-UNROLL = 4
+BLOCK = 16
 VMEM = pl.BlockSpec(memory_space=pltpu.VMEM)
 SMEM = pl.BlockSpec(memory_space=pltpu.SMEM)
 HBM = pl.BlockSpec(memory_space=pltpu.HBM)
@@ -308,32 +306,58 @@
             high[edge] = s[:, cells_z - 1][None]
 
 
-def side_kernel(step_index, src_cell, src_wave, now, old, aniso_h, base, side, rows):
-    cells_x, _, cells_y = base.shape
-    masks = lateral_masks(cells_y)
+def band(cells_y):
+    apart = lax.broadcasted_iota(jnp.int32, (cells_y, cells_y), 0)
+    apart = apart - lax.broadcasted_iota(jnp.int32, (cells_y, cells_y), 1)
+    value = jnp.zeros((cells_y, cells_y), jnp.float32)
+    for k in range(1, 5):
+        value = jnp.where(jnp.abs(apart) == k, second_coef[k], value)
+    return value
+
+
+def side_part(now, aniso_h, side, rows, also=None):
+    cells_x, cells_z, cells_y = now.shape
+    matrix = band(cells_y)
     fill_rows(rows, lambda at: now[at])
-
-    @pl.loop(0, cells_x // CHUNK, unroll=UNROLL)
-    def _(step):
-        x = step * CHUNK
-        at = pl.ds(x, CHUNK)
-        base[at] = 2.0 * now[at] - old[at]
-        side[at] = aniso_h[at] * lateral(rows, x, masks)
-
-    add_at(base, src_cell[0], src_wave[0, step_index])
-
-
-def side_halo_kernel(
-    step_index, src_cell, src_wave, now, old, aniso_h, low, high,
-    base, side, low_in, high_in, rows, sem,
-):
+    block = min(BLOCK, cells_x)
+
+    @pl.loop(0, cells_x // block)
+    def _(step):
+        x = step * block
+        at = pl.ds(x, block)
+        v = now[at]
+        flat = v.reshape(block * cells_z, cells_y)
+        along_y = jnp.dot(
+            flat, matrix, precision=lax.Precision.HIGHEST, preferred_element_type=jnp.float32
+        )
+        total = (2.0 * second_coef[0]) * v + along_y.reshape(v.shape)
+        for k in range(1, 5):
+            total = total + second_coef[k] * (
+                rows[pl.ds(REACH + x + k, block)] + rows[pl.ds(REACH + x - k, block)]
+            )
+        side[at] = aniso_h[at] * total
+        if also is not None:
+            also(at, v)
+
+
+def side_one_kernel(src_cell, src_wave, now, old, aniso_h, base, side, carry, rows):
+    def also(at, v):
+        base[at] = 2.0 * v - old[at]
+        carry[at] = -v
+
+    side_part(now, aniso_h, side, rows, also)
+    add_at(base, src_cell[0], src_wave[0, 1])
+    add_at(carry, src_cell[0], src_wave[0, 2])
+
+
+def side_two_kernel(now, aniso_h, low, high, side, low_in, high_in, rows, sem):
     copies = [
         pltpu.make_async_copy(low, low_in, sem.at[0]),
         pltpu.make_async_copy(high, high_in, sem.at[1]),
     ]
     for copy in copies:
         copy.start()
-    side_kernel(step_index, src_cell, src_wave, now, old, aniso_h, base, side, rows)
+    side_part(now, aniso_h, side, rows)
     for copy in copies:
         copy.wait()
 
@@ -643,7 +667,7 @@
         change[at] = model[at] * (side[at] + dep[at] + aniso_c[at] * crossing(first_z, x))
 
 
-def close_kernel(squares, smoothed, model, base, change, model_next, grad_dir, wave_next):
+def close_kernel(squares, smoothed, model, u_two, carry, change, model_next, grad_dir, wave_next):
     cells_x, cells_z, cells_y = smoothed.shape
     rows = grad_dir.shape[0]
     total = jnp.sum(jnp.sum(squares[...], axis=0), axis=1, keepdims=True)
@@ -659,7 +683,7 @@
     def _(step):
         at = pl.ds(step * CHUNK, CHUNK)
         shrink = 1.0 - 0.25 * jnp.tanh(factor(smoothed[at]))
-        wave_next[0, at] = base[at] + change[at] * shrink
+        wave_next[0, at] = 2.0 * u_two[at] + carry[at] + change[at] * shrink
 
     _, core, chip = position()
     at = pl.ds((2 * chip + core) * rows, rows)
@@ -757,11 +781,11 @@
         20 * slab.size,
     )
     low_one, high_one = shift(low_edge, high_edge)
-    base, side = call(
-        functools.partial(side_kernel, 1),
+    base, side, carry = call(
+        side_one_kernel,
         (src_cell, src_wave, u_one, u_cur[0], h_slab),
         2,
-        (slab, slab),
+        (slab, slab, slab),
         (padded_rows,),
         work // 2,
     )
@@ -787,14 +811,14 @@
         join_kernel, (mine, other), 0, (slab, payload, payload)
     )
     low_sum, high_sum = shift(low_edge, high_edge)
-    base, side, low_two, high_two = call(
-        functools.partial(side_halo_kernel, 2),
-        (src_cell, src_wave, u_two, u_one, h_slab, low_two, high_two),
-        2,
-        (slab, slab, edge, edge),
+    side, low_two, high_two = call(
+        side_two_kernel,
+        (u_two, h_slab, low_two, high_two),
+        0,
+        (slab, edge, edge),
         (padded_rows, pltpu.SemaphoreType.DMA((2,))),
         work // 2,
-        hbm_in=(5, 6),
+        hbm_in=(2, 3),
     )
     edges = f32(4, cells_x, cells_y)
     smoothed, inner, own_g, own_s, own_out = call(
@@ -825,7 +849,7 @@
     share = f32(rows, cells_z, cells_y)
     return call(
         close_kernel,
-        (squares, smoothed, model_slab, base, change),
+        (squares, smoothed, model_slab, u_two, carry, change),
         0,
         (share, share, f32(1, cells_x, cells_z, cells_y)),
         (),

time: 138 us -> 138 us (level)
  waiting for transfers between devices: 9.27 us -> 11.1 us
  Pallas kernels: 28.2 us -> 26.6 us
    pallas_call x14, Pallas kernels: 28.2 us -> 26.6 us  [call(): pl.pallas_call(kernel, out_shape=outs, in_specs=[spec(i) for i in range(l...]
    all_to_all x1, waiting for transfers between devices: 0.67 us -> 2.26 us  [body(): squares = lax.all_to_all(square, DEPTH, 0, 0, tiled=True)]
    unnamed x25 -> x21, local copies, waits for them, and re-layouts: 4.27 us -> 4.29 us
  transfers between devices with their start and end apart: 12 -> 12, of which waited for: 5 -> 5; matrix products, arithmetic and copies ran while one was open for 1% -> 1% of each run, Pallas kernels for 16% -> 15%
where the time goes in v8:
time: 138 us; the launch traced here: 137 us
  blocking collectives  67.4 us (49%)
  Pallas kernels  26.6 us (19%)
  starting transfers between devices  25.4 us (18%)
  waiting for transfers between devices  11.1 us (8%)
  local copies, waits for them, and re-layouts  4.38 us (3%)
  between operations  2.15 us (2%)
    all_to_all x1, blocking collectives, body(): mine = lax.all_to_all(spread, PEERS, 0, 0, tiled=True)  38.2 us
    pallas_call x14, Pallas kernels, call(): pl.pallas_call(kernel, out_shape=outs, in_specs=[spec(i) for i in range(l...  26.6 us
    all_to_all x1, blocking collectives, body(): mine = lax.all_to_all(total, PEERS, 0, 0, tiled=True)  14.6 us
    all_to_all x1, blocking collectives, body(): shares = lax.all_to_all(chip_sum, PEERS, 0, 0, tiled=True)  14.6 us
    ppermute x4, starting transfers between devices, shift(): lax.ppermute(low_edge, DEPTH, backward)  12.9 us
    ppermute x4, waiting for transfers between devices, shift(): lax.ppermute(high_edge, DEPTH, forward)  7.67 us
    ppermute x2, starting transfers between devices, body(): other = lax.ppermute(mine, 'core', SWAP)  5.9 us
    unnamed x21, local copies, waits for them, and re-layouts  4.29 us
  transfers between devices with their start and end apart: 12, of which 5 were waited for; matrix products, arithmetic and copies ran while one was open for 1% of the time, Pallas kernels for 15%

profile of v8, /device:TPU:1, one launch (start us, length us, event | category | flops | bytes accessed | tf_op | source)
XLA Modules:
  0.0 137.2 jit_solution(13334202876852631070)
XLA Ops:
  0.6 1.9 %shard_map.157 = f32[16,4,2,16,128]{4,3,2,1,0:T(8,128)} custom-call(f32[2,16,128]{2,1,0:T(8,128)} %model.1, f32[2,16,128]{2,1,0:T(8,128)} %aniso_h.1, f32[2,16,128]{2,1,0:T(8,128)} %aniso_c.1, f32[2,16,128]{2,1,0:T(8,128)} %smooth.1), custom_call_target="tpu_custom_call" | custom-call | bytes 65536 | tf_op jit(solution)/shard_map/pallas_call | solution.py:34
  2.6 38.2 %all_to_all.20.mine = f32[16,4,2,16,128]{4,3,2,1,0:T(8,128)S(1)} all-to-all(f32[16,4,2,16,128]{4,3,2,1,0:T(8,128)} %shard_map.157), channel_id=1, replica_groups=mesh['xh'=2,'z'=8,'core'=2,'xl'=2,'y'=4] {'xh','z'}, dimensions={0} | all-to-all | bytes 2097152 | tf_op jit(solution)/shard_map/all_to_all | solution.py:744
  40.8 2.8 %collective-permute-start = (f32[16,4,2,16,128]{4,3,2,1,0:T(8,128)S(1)}, f32[16,4,2,16,128]{4,3,2,1,0:T(8,128)}, u32[]{:S(2)}, u32[]{:S(2)}) collective-permute-start(f32[16,4,2,16,128]{4,3,2,1,0:T(8,128)S(1)} %all_to_all.20.mine), channel_id=1, source_target_pairs={{0,8},{8,0},{1,9},{9,1},{2,10},{10,2},{3,11},{11,3},{4,12},{12,4},... | collective-permute-start | bytes 3145736 | tf_op jit(solution)/shard_map/ppermute | solution.py:764
  43.8 1.4 %collective-permute-start.1 = (f32[2,64,4,128]{3,2,1,0:T(4,128)S(1)}, f32[2,64,4,128]{3,2,1,0:T(4,128)S(1)}, u32[]{:S(2)}, u32[]{:S(2)}) collective-permute-start(f32[2,64,4,128]{3,2,1,0:T(4,128)S(1)} %pad_maximum_fusion), channel_id=1, source_target_pairs={{0,1},{1,2},{2,3},{3,4},{4,5},{5,6},{6,7},{7,0},{8,9},{9,10},{10,1... | collective-permute-start | bytes 786440 | tf_op jit(solution)/shard_map/ppermute | solution.py:699
  45.3 2.4 %collective-permute-start.2 = (f32[2,64,4,128]{3,2,1,0:T(4,128)S(1)}, f32[2,64,4,128]{3,2,1,0:T(4,128)S(1)}, u32[]{:S(2)}, u32[]{:S(2)}) collective-permute-start(f32[2,64,4,128]{3,2,1,0:T(4,128)S(1)} %pad_maximum_fusion.1), channel_id=1, source_target_pairs={{1,0},{2,1},{3,2},{4,3},{5,4},{6,5},{7,6},{0,7},{9,8},{10,9},{11,1... | collective-permute-start | bytes 786440 | tf_op jit(solution)/shard_map/ppermute | solution.py:699
  48.3 0.7 copy.17.onehot
  49.6 4.2 %collective-permute-done.1.low = f32[2,64,4,128]{3,2,1,0:T(4,128)S(1)} collective-permute-done((f32[2,64,4,128]{3,2,1,0:T(4,128)S(1)}, f32[2,64,4,128]{3,2,1,0:T(4,128)S(1)}, u32[]{:S(2)}, u32[]{:S(2)}) %collective-permute-start.1) | collective-permute-done | bytes 262176 | tf_op jit(solution)/shard_map/ppermute | solution.py:699
  53.9 0.7 copy-done.7
  54.6 0.7 copy-done.8
  55.3 10.4 %shard_map.158 = (f32[64,16,128]{2,1,0:T(8,128)}, f32[64,16,128]{2,1,0:T(8,128)}, f32[64,16,128]{2,1,0:T(8,128)}, f32[64,16,128]{2,1,0:T(8,128)}, f32[64,16,128]...) custom-call(s32[1]{0:T(128)S(6)} %copy.19.src_cell, ...), custom_call_target="tpu_custom_call" | custom-call | flops 20971520 | bytes 2623508 | tf_op jit(solution)/shard_map/pallas_call | solution.py:34
  66.4 2.4 %shard_map.159 = (f32[64,16,128]{2,1,0:T(8,128)S(1)}, f32[64,16,128]{2,1,0:T(8,128)S(1)}, f32[64,16,128]{2,1,0:T(8,128)S(1)}, f32[64,16,128]{2,1,0:T(8,128)S(1)}...) custom-call(f32[64,16,128]{2,1,0:T(8,128)} %get-tuple-element.52.ref, ...), custom_call_target="tpu_custom_call" | custom-call | bytes 4726784 | tf_op jit(solution)/shard_map/pallas_call | solution.py:34
  68.8 1.8 %shard_map.160 = (f32[64,16,128]{2,1,0:T(8,128)S(1)}, f32[64,16,128]{2,1,0:T(8,128)S(1)}, f32[64,16,128]{2,1,0:T(8,128)S(1)}, f32[64,16,128]{2,1,0:T(8,128)S(1)}...) custom-call(f32[16,4,2,16,128]{4,3,2,1,0:T(8,128)S(1)} %all_to_all.2, ...), custom_call_target="tpu_custom_call" | custom-call | flops 2621440 | bytes 6815744 | tf_op jit(solution)/shard_map/pallas_call | solution.py:34
  70.7 3.6 %collective-permute-start.4 = (f32[80,4,128]{2,1,0:T(4,128)S(1)}, f32[80,4,128]{2,1,0:T(4,128)S(1)}, u32[]{:S(2)}, u32[]{:S(2)}) collective-permute-start(f32[80,4,128]{2,1,0:T(4,128)S(1)} %get-tuple-element.80), channel_id=1, source_target_pairs={{1,0},{2,1},{3,2},{4,3},{5,4},{6,5},{7,6},{0,7},{9,8},{10,9},{11,1... | collective-permute-start | bytes 491528 | tf_op jit(solution)/shard_map/ppermute | solution.py:699
  74.9 1.8 %shard_map.161 = (f32[64,16,128]{2,1,0:T(8,128)S(1)}, f32[64,16,128]{2,1,0:T(8,128)S(1)}, f32[64,16,128]{2,1,0:T(8,128)S(1)}) custom-call(s32[1]{0:T(128)S(6)} %copy.19.src_cell, f32[1,3]{1,0:T(1,128)S(1)} %copy-done.5, f32[64,16,128]{2,1,0:T(8,128)S(1)} %get-tuple-element.70.now.u_one, f32[64,16,128]{2,1,0:T(8,128)S(1)} %bitcast.1, ...), custom_call_target="tpu_custom_call" | custom-call | flops 5242880 | bytes 1572880 | tf_op jit(solution)/shard_map/pallas_call | solution.py:34
  76.8 0.9 collective-permute-done.3.low.low_one
  77.7 1.0 shard_map.162
  78.8 1.8 %collective-permute-start.5 = (f32[16,2,16,128]{3,2,1,0:T(8,128)S(1)}, f32[16,2,16,128]{3,2,1,0:T(8,128)S(1)}, u32[]{:S(2)}, u32[]{:S(2)}) collective-permute-start(f32[16,2,16,128]{3,2,1,0:T(8,128)S(1)} %get-tuple-element.82), channel_id=1, source_target_pairs={{0,8},{8,0},{1,9},{9,1},{2,10},{10,2},{3,11},{11,3},{4,12},{12,4},... | collective-permute-start | bytes 786440 | tf_op jit(solution)/shard_map/ppermute | solution.py:802
  80.6 1.2 collective-permute-done.5
  81.8 14.6 %all_to_all.21.parts = f32[16,2,16,128]{3,2,1,0:T(8,128)S(1)} all-to-all(f32[16,2,16,128]{3,2,1,0:T(8,128)S(1)} %add.3), channel_id=1, replica_groups=mesh['xh'=2,'z'=8,'core'=2,'xl'=2,'y'=4] {'xh','z'}, dimensions={0} | all-to-all | bytes 524288 | tf_op jit(solution)/shard_map/all_to_all | solution.py:803
  96.4 14.6 %all_to_all.22.mine = f32[16,2,16,128]{3,2,1,0:T(8,128)S(1)} all-to-all(f32[16,2,16,128]{3,2,1,0:T(8,128)S(1)} %shard_map.163), channel_id=1, replica_groups=mesh['xh'=2,'z'=8,'core'=2,'xl'=2,'y'=4] {'xh','z'}, dimensions={0} | all-to-all | bytes 524288 | tf_op jit(solution)/shard_map/all_to_all | solution.py:805
  111.0 3.1 %collective-permute-start.6 = (f32[16,2,16,128]{3,2,1,0:T(8,128)S(1)}, f32[16,2,16,128]{3,2,1,0:T(8,128)S(1)}, u32[]{:S(2)}, u32[]{:S(2)}) collective-permute-start(f32[16,2,16,128]{3,2,1,0:T(8,128)S(1)} %all_to_all.22.mine), channel_id=1, source_target_pairs={{0,8},{8,0},{1,9},{9,1},{2,10},{10,2},{3,11},{11,3},{4,12},{12,4},... | collective-permute-start | bytes 786440 | tf_op jit(solution)/shard_map/ppermute | solution.py:806
  114.2 3.3 %collective-permute-start.10 = (f32[64,4,128]{2,1,0:T(4,128)S(1)}, f32[64,4,128]{2,1,0:T(4,128)S(1)}, u32[]{:S(2)}, u32[]{:S(2)}) collective-permute-start(f32[64,4,128]{2,1,0:T(4,128)S(1)} %get-tuple-element.97), channel_id=1, source_target_pairs={{1,0},{2,1},{3,2},{4,3},{5,4},{6,5},{7,6},{0,7},{9,8},{10,9},{11,1... | collective-permute-start | bytes 393224 | tf_op jit(solution)/shard_map/ppermute | solution.py:699
  117.7 3.6 %collective-permute-start.8 = (f32[32,4,128]{2,1,0:T(4,128)S(1)}, f32[32,4,128]{2,1,0:T(4,128)S(1)}, u32[]{:S(2)}, u32[]{:S(2)}) collective-permute-start(f32[32,4,128]{2,1,0:T(4,128)S(1)} %get-tuple-element.91), channel_id=1, source_target_pairs={{1,0},{2,1},{3,2},{4,3},{5,4},{6,5},{7,6},{0,7},{9,8},{10,9},{11,1... | collective-permute-start | bytes 196616 | tf_op jit(solution)/shard_map/ppermute | solution.py:699
  121.3 1.9 %shard_map.165 = (f32[64,16,128]{2,1,0:T(8,128)S(1)}, f32[8,128]{1,0:T(8,128)S(1)}, f32[2,64,128]{2,1,0:T(8,128)S(1)}, f32[4,64,128]{2,1,0:T(8,128)S(1)}, f32[4,64,128]{2,1,0:T(8,128)S(1)}) custom-call(f32[64,16,128]{2,1,0:T(8,128)S(1)} %get-tuple-element.83.summed, f32[64,16,128]{2,1,0:T(8,128)S(1)} %get-tuple-element.84.smooth), custom_call_target="tpu_custom_call" | custom-call | flops 5242880 | bytes 1048576 | tf_op jit(solution)/shard_map/pallas_call | solution.py:34
  123.2 2.5 %collective-permute-done.7.low_sum = f32[32,4,128]{2,1,0:T(4,128)S(1)} collective-permute-done((f32[32,4,128]{2,1,0:T(4,128)S(1)}, f32[32,4,128]{2,1,0:T(4,128)S(1)}, u32[]{:S(2)}, u32[]{:S(2)}) %collective-permute-start.7) | collective-permute-done | bytes 65568 | tf_op jit(solution)/shard_map/ppermute | solution.py:699
  125.7 1.3 shard_map.166
  127.0 0.8 copy-done.2
  127.8 3.3 %all-to-all-start.3 = ((f32[8,1,128]{2,1,0:T(1,128)}), f32[8,1,128]{2,1,0:T(1,128)S(1)}, u32[]{:S(2)}, u32[]{:S(2)}) async-start(f32[8,1,128]{2,1,0:T(1,128)} %get-tuple-element.92), calls=%async_computation.3 | async-start | bytes 8192 | tf_op jit(solution)/shard_map/all_to_all | solution.py:848
  131.2 1.6 %shard_map.168 = (f32[64,16,128]{2,1,0:T(8,128)S(1)}, f32[64,4,128]{2,1,0:T(4,128)S(1)}, f32[64,4,128]{2,1,0:T(4,128)S(1)}) custom-call(f32[64,16,128]{2,1,0:T(8,128)S(1)} %get-tuple-element.94.field.now.u_two, f32[64,16,128]{2,1,0:T(8,128)S(1)} %get-tuple-element.71.aniso_h, f32[64,4,128]{2,1,0:T(4,128)S(1)} %collective-permute-done.9.low, ...), custom_call_target="tpu_custom_call" | custom-call | flops 5242880 | bytes 1310720 | tf_op jit(solution)/shard_map/pallas_call | solution.py:34
  132.8 1.0 shard_map.169.change
  133.8 2.3 %all-to-all-done.3.squares = f32[8,1,128]{2,1,0:T(1,128)S(1)} async-done(((f32[8,1,128]{2,1,0:T(1,128)}), f32[8,1,128]{2,1,0:T(1,128)S(1)}, u32[]{:S(2)}, u32[]{:S(2)}) %all-to-all-start.3) | async-done | bytes 4128 | tf_op jit(solution)/shard_map/all_to_all | solution.py:848
  136.0 1.2 shard_map.170
  (34 shorter events, 2.1 us)
Async XLA Ops:
  2.6 41.1 %copy-start = (f32[1,64,16,128]{3,2,1,0:T(8,128)S(1)}, f32[1,64,16,128]{3,2,1,0:T(8,128)}, u32[]{:S(2)}) copy-start(f32[1,64,16,128]{3,2,1,0:T(8,128)} %u_cur.1) | copy-start | bytes 1572868
  2.6 41.1 %copy-start.6 = (f32[1,64,16,128]{3,2,1,0:T(8,128)S(1)}, f32[1,64,16,128]{3,2,1,0:T(8,128)}, u32[]{:S(2)}) copy-start(f32[1,64,16,128]{3,2,1,0:T(8,128)} %refs_9_.1) | copy-start | bytes 1572868
  40.8 28.0 %collective-permute-start = (f32[16,4,2,16,128]{4,3,2,1,0:T(8,128)S(1)}, f32[16,4,2,16,128]{4,3,2,1,0:T(8,128)}, u32[]{:S(2)}, u32[]{:S(2)}) collective-permute-start(f32[16,4,2,16,128]{4,3,2,1,0:T(8,128)S(1)} %all_to_all.20.mine), channel_id=1, source_target_pairs={{0,8},{8,0},{1,9},{9,1},{2,10},{10,2},{3,11},{11,3},{4,12},{12,4},... | collective-permute-start | bytes 3145736 | tf_op jit(solution)/shard_map/ppermute | solution.py:764
  43.8 10.0 %collective-permute-start.1 = (f32[2,64,4,128]{3,2,1,0:T(4,128)S(1)}, f32[2,64,4,128]{3,2,1,0:T(4,128)S(1)}, u32[]{:S(2)}, u32[]{:S(2)}) collective-permute-start(f32[2,64,4,128]{3,2,1,0:T(4,128)S(1)} %pad_maximum_fusion), channel_id=1, source_target_pairs={{0,1},{1,2},{2,3},{3,4},{4,5},{5,6},{6,7},{7,0},{8,9},{9,10},{10,1... | collective-permute-start | bytes 786440 | tf_op jit(solution)/shard_map/ppermute | solution.py:699
  45.2 3.1 %copy-start.9 = (s32[16,2,4]{0,2,1:T(4,128)S(1)}, s32[16,2,4]{0,2,1:T(4,128)}, u32[]{:S(2)}) copy-start(s32[16,2,4]{0,2,1:T(4,128)} %param.22) | copy-start | bytes 1540
  45.3 8.6 %collective-permute-start.2 = (f32[2,64,4,128]{3,2,1,0:T(4,128)S(1)}, f32[2,64,4,128]{3,2,1,0:T(4,128)S(1)}, u32[]{:S(2)}, u32[]{:S(2)}) collective-permute-start(f32[2,64,4,128]{3,2,1,0:T(4,128)S(1)} %pad_maximum_fusion.1), channel_id=1, source_target_pairs={{1,0},{2,1},{3,2},{4,3},{5,4},{6,5},{7,6},{0,7},{9,8},{10,9},{11,1... | collective-permute-start | bytes 786440 | tf_op jit(solution)/shard_map/ppermute | solution.py:699
  53.9 0.7 copy-start.7
  54.6 0.7 copy-start.8
  65.7 0.7 copy-start.4
  68.8 5.5 %copy-start.1 = (f32[1,64,16,128]{3,2,1,0:T(8,128)S(1)}, f32[1,64,16,128]{3,2,1,0:T(8,128)}, u32[]{:S(2)}) copy-start(f32[1,64,16,128]{3,2,1,0:T(8,128)} %u_cur.1) | copy-start | bytes 1572868
  70.6 7.1 %collective-permute-start.3 = (f32[80,4,128]{2,1,0:T(4,128)S(1)}, f32[80,4,128]{2,1,0:T(4,128)S(1)}, u32[]{:S(2)}, u32[]{:S(2)}) collective-permute-start(f32[80,4,128]{2,1,0:T(4,128)S(1)} %get-tuple-element.79), channel_id=1, source_target_pairs={{0,1},{1,2},{2,3},{3,4},{4,5},{5,6},{6,7},{7,0},{8,9},{9,10},{10,1... | collective-permute-start | bytes 491528 | tf_op jit(solution)/shard_map/ppermute | solution.py:699
  70.7 7.0 %collective-permute-start.4 = (f32[80,4,128]{2,1,0:T(4,128)S(1)}, f32[80,4,128]{2,1,0:T(4,128)S(1)}, u32[]{:S(2)}, u32[]{:S(2)}) collective-permute-start(f32[80,4,128]{2,1,0:T(4,128)S(1)} %get-tuple-element.80), channel_id=1, source_target_pairs={{1,0},{2,1},{3,2},{4,3},{5,4},{6,5},{7,6},{0,7},{9,8},{10,9},{11,1... | collective-permute-start | bytes 491528 | tf_op jit(solution)/shard_map/ppermute | solution.py:699
  74.3 0.7 copy-start.5
  78.8 3.0 %collective-permute-start.5 = (f32[16,2,16,128]{3,2,1,0:T(8,128)S(1)}, f32[16,2,16,128]{3,2,1,0:T(8,128)S(1)}, u32[]{:S(2)}, u32[]{:S(2)}) collective-permute-start(f32[16,2,16,128]{3,2,1,0:T(8,128)S(1)} %get-tuple-element.82), channel_id=1, source_target_pairs={{0,8},{8,0},{1,9},{9,1},{2,10},{10,2},{3,11},{11,3},{4,12},{12,4},... | collective-permute-start | bytes 786440 | tf_op jit(solution)/shard_map/ppermute | solution.py:802
  111.0 6.4 %collective-permute-start.6 = (f32[16,2,16,128]{3,2,1,0:T(8,128)S(1)}, f32[16,2,16,128]{3,2,1,0:T(8,128)S(1)}, u32[]{:S(2)}, u32[]{:S(2)}) collective-permute-start(f32[16,2,16,128]{3,2,1,0:T(8,128)S(1)} %all_to_all.22.mine), channel_id=1, source_target_pairs={{0,8},{8,0},{1,9},{9,1},{2,10},{10,2},{3,11},{11,3},{4,12},{12,4},... | collective-permute-start | bytes 786440 | tf_op jit(solution)/shard_map/ppermute | solution.py:806
  114.2 17.0 %collective-permute-start.10 = (f32[64,4,128]{2,1,0:T(4,128)S(1)}, f32[64,4,128]{2,1,0:T(4,128)S(1)}, u32[]{:S(2)}, u32[]{:S(2)}) collective-permute-start(f32[64,4,128]{2,1,0:T(4,128)S(1)} %get-tuple-element.97), channel_id=1, source_target_pairs={{1,0},{2,1},{3,2},{4,3},{5,4},{6,5},{7,6},{0,7},{9,8},{10,9},{11,1... | collective-permute-start | bytes 393224 | tf_op jit(solution)/shard_map/ppermute | solution.py:699
  117.5 13.7 %collective-permute-start.9 = (f32[64,4,128]{2,1,0:T(4,128)S(1)}, f32[64,4,128]{2,1,0:T(4,128)S(1)}, u32[]{:S(2)}, u32[]{:S(2)}) collective-permute-start(f32[64,4,128]{2,1,0:T(4,128)S(1)} %get-tuple-element.96), channel_id=1, source_target_pairs={{0,1},{1,2},{2,3},{3,4},{4,5},{5,6},{6,7},{7,0},{8,9},{9,10},{10,1... | collective-permute-start | bytes 393224 | tf_op jit(solution)/shard_map/ppermute | solution.py:699
  117.6 8.1 %collective-permute-start.7 = (f32[32,4,128]{2,1,0:T(4,128)S(1)}, f32[32,4,128]{2,1,0:T(4,128)S(1)}, u32[]{:S(2)}, u32[]{:S(2)}) collective-permute-start(f32[32,4,128]{2,1,0:T(4,128)S(1)} %get-tuple-element.90), channel_id=1, source_target_pairs={{0,1},{1,2},{2,3},{3,4},{4,5},{5,6},{6,7},{7,0},{8,9},{9,10},{10,1... | collective-permute-start | bytes 196616 | tf_op jit(solution)/shard_map/ppermute | solution.py:699
  117.7 8.0 %collective-permute-start.8 = (f32[32,4,128]{2,1,0:T(4,128)S(1)}, f32[32,4,128]{2,1,0:T(4,128)S(1)}, u32[]{:S(2)}, u32[]{:S(2)}) collective-permute-start(f32[32,4,128]{2,1,0:T(4,128)S(1)} %get-tuple-element.91), channel_id=1, source_target_pairs={{1,0},{2,1},{3,2},{4,3},{5,4},{6,5},{7,6},{0,7},{9,8},{10,9},{11,1... | collective-permute-start | bytes 196616 | tf_op jit(solution)/shard_map/ppermute | solution.py:699
  127.0 0.8 copy-start.2
  127.8 8.2 %all-to-all-start.3 = ((f32[8,1,128]{2,1,0:T(1,128)}), f32[8,1,128]{2,1,0:T(1,128)S(1)}, u32[]{:S(2)}, u32[]{:S(2)}) async-start(f32[8,1,128]{2,1,0:T(1,128)} %get-tuple-element.92), calls=%async_computation.3 | async-start | bytes 8192 | tf_op jit(solution)/shard_map/all_to_all | solution.py:848
  132.8 3.2 %copy-start.3 = (f32[64,16,128]{2,1,0:T(8,128)S(1)}, f32[64,16,128]{2,1,0:T(8,128)}, u32[]{:S(2)}) copy-start(f32[64,16,128]{2,1,0:T(8,128)} %copy-done.2) | copy-start | bytes 1572868

commit v9 on v8

--- a/solution.py
+++ b/solution.py
@@ -90,7 +90,7 @@
     first_z[pl.ds(0, REACH)] = zeros
     first_z[pl.ds(REACH + cells_x, REACH)] = zeros
 
-    @pl.loop(0, cells_x // CHUNK, unroll=2)
+    @pl.loop(0, cells_x // CHUNK, unroll=4)
     def _(step):
         x = step * CHUNK
         at = lambda k: pad[pl.ds(x, CHUNK), pl.ds(MID + k, cells_z), :]
@@ -286,7 +286,7 @@
     cells_x, cells_z, _ = u_one.shape
     own = position()[1] == 0
 
-    @pl.loop(0, mine.shape[0])
+    @pl.loop(0, mine.shape[0], unroll=2)
     def _(q):
         for p in range(2):
             rows = pl.ds(q * 4 + p * 2, 2)
@@ -371,7 +371,7 @@
     depth_pass(pad, first_z, dep)
     own = position()[1] == 0
 
-    @pl.loop(0, cells_x // CHUNK, unroll=2)
+    @pl.loop(0, cells_x // CHUNK, unroll=4)
     def _(step):
         x = step * CHUNK
         at = pl.ds(x, CHUNK)
@@ -405,7 +405,7 @@
     count = mine.shape[0]
     own = position()[1] == 0
 
-    @pl.loop(0, count)
+    @pl.loop(0, count, unroll=2)
     def _(q):
         for p in range(2):
             rows = pl.ds(q * 4 + p * 2, 2)
@@ -496,7 +496,7 @@
             planes[k, pl.ds(0, 8)] = blank
             planes[k, pl.ds(8 + cells_x, 8)] = blank
 
-        @pl.loop(0, count)
+        @pl.loop(0, count, unroll=2)
         def _(q, sums=sums, smooth=smooth, present=present):
             at = pl.ds(8 + 4 * q, 4)
             for k in range(2):
@@ -521,7 +521,7 @@
         planes[1, whole] = beside
         rows = (0, 1) if side == 0 else (cells_z - 1, cells_z - 2)
 
-        @pl.loop(0, count)
+        @pl.loop(0, count, unroll=2)
         def _(q, rows=rows):
             for k, z in enumerate(rows):
                 smoothed[pl.ds(4 * q, 4), pl.ds(z, 1), :] = planes[k, pl.ds(8 + 4 * q, 4)][:, None]

time: 138 us -> 139 us (level)
  no operation moved by 1% of the time
where the time goes in v9:
time: 139 us; the launch traced here: 137 us
  blocking collectives  67.4 us (48%)
  Pallas kernels  26.5 us (19%)
  starting transfers between devices  25.4 us (18%)
  waiting for transfers between devices  11.2 us (8%)
  local copies, waits for them, and re-layouts  4.38 us (3%)
  between operations  2.15 us (2%)
    all_to_all x1, blocking collectives, body(): mine = lax.all_to_all(spread, PEERS, 0, 0, tiled=True)  38.2 us
    pallas_call x14, Pallas kernels, call(): pl.pallas_call(kernel, out_shape=outs, in_specs=[spec(i) for i in range(l...  26.5 us
    all_to_all x1, blocking collectives, body(): mine = lax.all_to_all(total, PEERS, 0, 0, tiled=True)  14.6 us
    all_to_all x1, blocking collectives, body(): shares = lax.all_to_all(chip_sum, PEERS, 0, 0, tiled=True)  14.6 us
    ppermute x4, starting transfers between devices, shift(): lax.ppermute(low_edge, DEPTH, backward)  12.9 us
    ppermute x4, waiting for transfers between devices, shift(): lax.ppermute(high_edge, DEPTH, forward)  7.69 us
    ppermute x2, starting transfers between devices, body(): other = lax.ppermute(mine, 'core', SWAP)  5.9 us
    unnamed x21, local copies, waits for them, and re-layouts  4.29 us
  transfers between devices with their start and end apart: 12, of which 5 were waited for; matrix products, arithmetic and copies ran while one was open for 1% of the time, Pallas kernels for 15%

profile of v9, /device:TPU:1, one launch (start us, length us, event | category | flops | bytes accessed | tf_op | source)
XLA Modules:
  0.0 137.2 jit_solution(18284043383940914489)
XLA Ops:
  0.6 1.9 %shard_map.157 = f32[16,4,2,16,128]{4,3,2,1,0:T(8,128)} custom-call(f32[2,16,128]{2,1,0:T(8,128)} %model.1, f32[2,16,128]{2,1,0:T(8,128)} %aniso_h.1, f32[2,16,128]{2,1,0:T(8,128)} %aniso_c.1, f32[2,16,128]{2,1,0:T(8,128)} %smooth.1), custom_call_target="tpu_custom_call" | custom-call | bytes 65536 | tf_op jit(solution)/shard_map/pallas_call | solution.py:34
  2.6 38.2 %all_to_all.20.mine = f32[16,4,2,16,128]{4,3,2,1,0:T(8,128)S(1)} all-to-all(f32[16,4,2,16,128]{4,3,2,1,0:T(8,128)} %shard_map.157), channel_id=1, replica_groups=mesh['xh'=2,'z'=8,'core'=2,'xl'=2,'y'=4] {'xh','z'}, dimensions={0} | all-to-all | bytes 2097152 | tf_op jit(solution)/shard_map/all_to_all | solution.py:744
  40.8 2.8 %collective-permute-start = (f32[16,4,2,16,128]{4,3,2,1,0:T(8,128)S(1)}, f32[16,4,2,16,128]{4,3,2,1,0:T(8,128)}, u32[]{:S(2)}, u32[]{:S(2)}) collective-permute-start(f32[16,4,2,16,128]{4,3,2,1,0:T(8,128)S(1)} %all_to_all.20.mine), channel_id=1, source_target_pairs={{0,8},{8,0},{1,9},{9,1},{2,10},{10,2},{3,11},{11,3},{4,12},{12,4},... | collective-permute-start | bytes 3145736 | tf_op jit(solution)/shard_map/ppermute | solution.py:764
  43.8 1.4 %collective-permute-start.1 = (f32[2,64,4,128]{3,2,1,0:T(4,128)S(1)}, f32[2,64,4,128]{3,2,1,0:T(4,128)S(1)}, u32[]{:S(2)}, u32[]{:S(2)}) collective-permute-start(f32[2,64,4,128]{3,2,1,0:T(4,128)S(1)} %pad_maximum_fusion), channel_id=1, source_target_pairs={{0,1},{1,2},{2,3},{3,4},{4,5},{5,6},{6,7},{7,0},{8,9},{9,10},{10,1... | collective-permute-start | bytes 786440 | tf_op jit(solution)/shard_map/ppermute | solution.py:699
  45.3 2.4 %collective-permute-start.2 = (f32[2,64,4,128]{3,2,1,0:T(4,128)S(1)}, f32[2,64,4,128]{3,2,1,0:T(4,128)S(1)}, u32[]{:S(2)}, u32[]{:S(2)}) collective-permute-start(f32[2,64,4,128]{3,2,1,0:T(4,128)S(1)} %pad_maximum_fusion.1), channel_id=1, source_target_pairs={{1,0},{2,1},{3,2},{4,3},{5,4},{6,5},{7,6},{0,7},{9,8},{10,9},{11,1... | collective-permute-start | bytes 786440 | tf_op jit(solution)/shard_map/ppermute | solution.py:699
  48.3 0.7 copy.17.onehot
  49.6 4.2 %collective-permute-done.1.low = f32[2,64,4,128]{3,2,1,0:T(4,128)S(1)} collective-permute-done((f32[2,64,4,128]{3,2,1,0:T(4,128)S(1)}, f32[2,64,4,128]{3,2,1,0:T(4,128)S(1)}, u32[]{:S(2)}, u32[]{:S(2)}) %collective-permute-start.1) | collective-permute-done | bytes 262176 | tf_op jit(solution)/shard_map/ppermute | solution.py:699
  53.9 0.7 copy-done.7
  54.6 0.7 copy-done.8
  55.3 10.4 %shard_map.158 = (f32[64,16,128]{2,1,0:T(8,128)}, f32[64,16,128]{2,1,0:T(8,128)}, f32[64,16,128]{2,1,0:T(8,128)}, f32[64,16,128]{2,1,0:T(8,128)}, f32[64,16,128]...) custom-call(s32[1]{0:T(128)S(6)} %copy.19.src_cell, ...), custom_call_target="tpu_custom_call" | custom-call | flops 20971520 | bytes 2623508 | tf_op jit(solution)/shard_map/pallas_call | solution.py:34
  66.4 2.4 %shard_map.159 = (f32[64,16,128]{2,1,0:T(8,128)S(1)}, f32[64,16,128]{2,1,0:T(8,128)S(1)}, f32[64,16,128]{2,1,0:T(8,128)S(1)}, f32[64,16,128]{2,1,0:T(8,128)S(1)}...) custom-call(f32[64,16,128]{2,1,0:T(8,128)} %get-tuple-element.52.ref, ...), custom_call_target="tpu_custom_call" | custom-call | bytes 4726784 | tf_op jit(solution)/shard_map/pallas_call | solution.py:34
  68.8 1.9 %shard_map.160 = (f32[64,16,128]{2,1,0:T(8,128)S(1)}, f32[64,16,128]{2,1,0:T(8,128)S(1)}, f32[64,16,128]{2,1,0:T(8,128)S(1)}, f32[64,16,128]{2,1,0:T(8,128)S(1)}...) custom-call(f32[16,4,2,16,128]{4,3,2,1,0:T(8,128)S(1)} %all_to_all.2, ...), custom_call_target="tpu_custom_call" | custom-call | flops 2621440 | bytes 6815744 | tf_op jit(solution)/shard_map/pallas_call | solution.py:34
  70.8 3.6 %collective-permute-start.4 = (f32[80,4,128]{2,1,0:T(4,128)S(1)}, f32[80,4,128]{2,1,0:T(4,128)S(1)}, u32[]{:S(2)}, u32[]{:S(2)}) collective-permute-start(f32[80,4,128]{2,1,0:T(4,128)S(1)} %get-tuple-element.80), channel_id=1, source_target_pairs={{1,0},{2,1},{3,2},{4,3},{5,4},{6,5},{7,6},{0,7},{9,8},{10,9},{11,1... | collective-permute-start | bytes 491528 | tf_op jit(solution)/shard_map/ppermute | solution.py:699
  75.0 1.8 %shard_map.161 = (f32[64,16,128]{2,1,0:T(8,128)S(1)}, f32[64,16,128]{2,1,0:T(8,128)S(1)}, f32[64,16,128]{2,1,0:T(8,128)S(1)}) custom-call(s32[1]{0:T(128)S(6)} %copy.19.src_cell, f32[1,3]{1,0:T(1,128)S(1)} %copy-done.5, f32[64,16,128]{2,1,0:T(8,128)S(1)} %get-tuple-element.70.now.u_one, f32[64,16,128]{2,1,0:T(8,128)S(1)} %bitcast.1, ...), custom_call_target="tpu_custom_call" | custom-call | flops 5242880 | bytes 1572880 | tf_op jit(solution)/shard_map/pallas_call | solution.py:34
  76.8 0.9 collective-permute-done.3.low.low_one
  77.8 1.0 shard_map.162
  78.8 1.8 %collective-permute-start.5 = (f32[16,2,16,128]{3,2,1,0:T(8,128)S(1)}, f32[16,2,16,128]{3,2,1,0:T(8,128)S(1)}, u32[]{:S(2)}, u32[]{:S(2)}) collective-permute-start(f32[16,2,16,128]{3,2,1,0:T(8,128)S(1)} %get-tuple-element.82), channel_id=1, source_target_pairs={{0,8},{8,0},{1,9},{9,1},{2,10},{10,2},{3,11},{11,3},{4,12},{12,4},... | collective-permute-start | bytes 786440 | tf_op jit(solution)/shard_map/ppermute | solution.py:802
  80.6 1.2 collective-permute-done.5
  81.8 14.6 %all_to_all.21.parts = f32[16,2,16,128]{3,2,1,0:T(8,128)S(1)} all-to-all(f32[16,2,16,128]{3,2,1,0:T(8,128)S(1)} %add.3), channel_id=1, replica_groups=mesh['xh'=2,'z'=8,'core'=2,'xl'=2,'y'=4] {'xh','z'}, dimensions={0} | all-to-all | bytes 524288 | tf_op jit(solution)/shard_map/all_to_all | solution.py:803
  96.4 14.6 %all_to_all.22.mine = f32[16,2,16,128]{3,2,1,0:T(8,128)S(1)} all-to-all(f32[16,2,16,128]{3,2,1,0:T(8,128)S(1)} %shard_map.163), channel_id=1, replica_groups=mesh['xh'=2,'z'=8,'core'=2,'xl'=2,'y'=4] {'xh','z'}, dimensions={0} | all-to-all | bytes 524288 | tf_op jit(solution)/shard_map/all_to_all | solution.py:805
  111.0 3.1 %collective-permute-start.6 = (f32[16,2,16,128]{3,2,1,0:T(8,128)S(1)}, f32[16,2,16,128]{3,2,1,0:T(8,128)S(1)}, u32[]{:S(2)}, u32[]{:S(2)}) collective-permute-start(f32[16,2,16,128]{3,2,1,0:T(8,128)S(1)} %all_to_all.22.mine), channel_id=1, source_target_pairs={{0,8},{8,0},{1,9},{9,1},{2,10},{10,2},{3,11},{11,3},{4,12},{12,4},... | collective-permute-start | bytes 786440 | tf_op jit(solution)/shard_map/ppermute | solution.py:806
  114.2 3.3 %collective-permute-start.10 = (f32[64,4,128]{2,1,0:T(4,128)S(1)}, f32[64,4,128]{2,1,0:T(4,128)S(1)}, u32[]{:S(2)}, u32[]{:S(2)}) collective-permute-start(f32[64,4,128]{2,1,0:T(4,128)S(1)} %get-tuple-element.97), channel_id=1, source_target_pairs={{1,0},{2,1},{3,2},{4,3},{5,4},{6,5},{7,6},{0,7},{9,8},{10,9},{11,1... | collective-permute-start | bytes 393224 | tf_op jit(solution)/shard_map/ppermute | solution.py:699
  117.7 3.6 %collective-permute-start.8 = (f32[32,4,128]{2,1,0:T(4,128)S(1)}, f32[32,4,128]{2,1,0:T(4,128)S(1)}, u32[]{:S(2)}, u32[]{:S(2)}) collective-permute-start(f32[32,4,128]{2,1,0:T(4,128)S(1)} %get-tuple-element.91), channel_id=1, source_target_pairs={{1,0},{2,1},{3,2},{4,3},{5,4},{6,5},{7,6},{0,7},{9,8},{10,9},{11,1... | collective-permute-start | bytes 196616 | tf_op jit(solution)/shard_map/ppermute | solution.py:699
  121.3 1.9 %shard_map.165 = (f32[64,16,128]{2,1,0:T(8,128)S(1)}, f32[8,128]{1,0:T(8,128)S(1)}, f32[2,64,128]{2,1,0:T(8,128)S(1)}, f32[4,64,128]{2,1,0:T(8,128)S(1)}, f32[4,64,128]{2,1,0:T(8,128)S(1)}) custom-call(f32[64,16,128]{2,1,0:T(8,128)S(1)} %get-tuple-element.83.summed, f32[64,16,128]{2,1,0:T(8,128)S(1)} %get-tuple-element.84.smooth), custom_call_target="tpu_custom_call" | custom-call | flops 5242880 | bytes 1048576 | tf_op jit(solution)/shard_map/pallas_call | solution.py:34
  123.2 2.5 %collective-permute-done.7.low_sum = f32[32,4,128]{2,1,0:T(4,128)S(1)} collective-permute-done((f32[32,4,128]{2,1,0:T(4,128)S(1)}, f32[32,4,128]{2,1,0:T(4,128)S(1)}, u32[]{:S(2)}, u32[]{:S(2)}) %collective-permute-start.7) | collective-permute-done | bytes 65568 | tf_op jit(solution)/shard_map/ppermute | solution.py:699
  125.8 1.3 shard_map.166
  127.0 0.8 copy-done.2
  127.8 3.3 %all-to-all-start.3 = ((f32[8,1,128]{2,1,0:T(1,128)}), f32[8,1,128]{2,1,0:T(1,128)S(1)}, u32[]{:S(2)}, u32[]{:S(2)}) async-start(f32[8,1,128]{2,1,0:T(1,128)} %get-tuple-element.92), calls=%async_computation.3 | async-start | bytes 8192 | tf_op jit(solution)/shard_map/all_to_all | solution.py:848
  131.2 1.6 %shard_map.168 = (f32[64,16,128]{2,1,0:T(8,128)S(1)}, f32[64,4,128]{2,1,0:T(4,128)S(1)}, f32[64,4,128]{2,1,0:T(4,128)S(1)}) custom-call(f32[64,16,128]{2,1,0:T(8,128)S(1)} %get-tuple-element.94.field.now.u_two, f32[64,16,128]{2,1,0:T(8,128)S(1)} %get-tuple-element.71.aniso_h, f32[64,4,128]{2,1,0:T(4,128)S(1)} %collective-permute-done.9.low, ...), custom_call_target="tpu_custom_call" | custom-call | flops 5242880 | bytes 1310720 | tf_op jit(solution)/shard_map/pallas_call | solution.py:34
  132.8 0.9 shard_map.169.change
  133.7 2.3 %all-to-all-done.3.squares = f32[8,1,128]{2,1,0:T(1,128)S(1)} async-done(((f32[8,1,128]{2,1,0:T(1,128)}), f32[8,1,128]{2,1,0:T(1,128)S(1)}, u32[]{:S(2)}, u32[]{:S(2)}) %all-to-all-start.3) | async-done | bytes 4128 | tf_op jit(solution)/shard_map/all_to_all | solution.py:848
  136.0 1.2 shard_map.170
  (34 shorter events, 2.0 us)
Async XLA Ops:
  2.6 41.1 %copy-start = (f32[1,64,16,128]{3,2,1,0:T(8,128)S(1)}, f32[1,64,16,128]{3,2,1,0:T(8,128)}, u32[]{:S(2)}) copy-start(f32[1,64,16,128]{3,2,1,0:T(8,128)} %u_cur.1) | copy-start | bytes 1572868
  2.6 41.1 %copy-start.6 = (f32[1,64,16,128]{3,2,1,0:T(8,128)S(1)}, f32[1,64,16,128]{3,2,1,0:T(8,128)}, u32[]{:S(2)}) copy-start(f32[1,64,16,128]{3,2,1,0:T(8,128)} %refs_9_.1) | copy-start | bytes 1572868
  40.8 28.0 %collective-permute-start = (f32[16,4,2,16,128]{4,3,2,1,0:T(8,128)S(1)}, f32[16,4,2,16,128]{4,3,2,1,0:T(8,128)}, u32[]{:S(2)}, u32[]{:S(2)}) collective-permute-start(f32[16,4,2,16,128]{4,3,2,1,0:T(8,128)S(1)} %all_to_all.20.mine), channel_id=1, source_target_pairs={{0,8},{8,0},{1,9},{9,1},{2,10},{10,2},{3,11},{11,3},{4,12},{12,4},... | collective-permute-start | bytes 3145736 | tf_op jit(solution)/shard_map/ppermute | solution.py:764
  43.8 10.0 %collective-permute-start.1 = (f32[2,64,4,128]{3,2,1,0:T(4,128)S(1)}, f32[2,64,4,128]{3,2,1,0:T(4,128)S(1)}, u32[]{:S(2)}, u32[]{:S(2)}) collective-permute-start(f32[2,64,4,128]{3,2,1,0:T(4,128)S(1)} %pad_maximum_fusion), channel_id=1, source_target_pairs={{0,1},{1,2},{2,3},{3,4},{4,5},{5,6},{6,7},{7,0},{8,9},{9,10},{10,1... | collective-permute-start | bytes 786440 | tf_op jit(solution)/shard_map/ppermute | solution.py:699
  45.2 3.1 %copy-start.9 = (s32[16,2,4]{0,2,1:T(4,128)S(1)}, s32[16,2,4]{0,2,1:T(4,128)}, u32[]{:S(2)}) copy-start(s32[16,2,4]{0,2,1:T(4,128)} %param.22) | copy-start | bytes 1540
  45.3 8.6 %collective-permute-start.2 = (f32[2,64,4,128]{3,2,1,0:T(4,128)S(1)}, f32[2,64,4,128]{3,2,1,0:T(4,128)S(1)}, u32[]{:S(2)}, u32[]{:S(2)}) collective-permute-start(f32[2,64,4,128]{3,2,1,0:T(4,128)S(1)} %pad_maximum_fusion.1), channel_id=1, source_target_pairs={{1,0},{2,1},{3,2},{4,3},{5,4},{6,5},{7,6},{0,7},{9,8},{10,9},{11,1... | collective-permute-start | bytes 786440 | tf_op jit(solution)/shard_map/ppermute | solution.py:699
  53.9 0.7 copy-start.7
  54.6 0.7 copy-start.8
  65.7 0.7 copy-start.4
  68.8 5.5 %copy-start.1 = (f32[1,64,16,128]{3,2,1,0:T(8,128)S(1)}, f32[1,64,16,128]{3,2,1,0:T(8,128)}, u32[]{:S(2)}) copy-start(f32[1,64,16,128]{3,2,1,0:T(8,128)} %u_cur.1) | copy-start | bytes 1572868
  70.7 7.1 %collective-permute-start.3 = (f32[80,4,128]{2,1,0:T(4,128)S(1)}, f32[80,4,128]{2,1,0:T(4,128)S(1)}, u32[]{:S(2)}, u32[]{:S(2)}) collective-permute-start(f32[80,4,128]{2,1,0:T(4,128)S(1)} %get-tuple-element.79), channel_id=1, source_target_pairs={{0,1},{1,2},{2,3},{3,4},{4,5},{5,6},{6,7},{7,0},{8,9},{9,10},{10,1... | collective-permute-start | bytes 491528 | tf_op jit(solution)/shard_map/ppermute | solution.py:699
  70.8 7.0 %collective-permute-start.4 = (f32[80,4,128]{2,1,0:T(4,128)S(1)}, f32[80,4,128]{2,1,0:T(4,128)S(1)}, u32[]{:S(2)}, u32[]{:S(2)}) collective-permute-start(f32[80,4,128]{2,1,0:T(4,128)S(1)} %get-tuple-element.80), channel_id=1, source_target_pairs={{1,0},{2,1},{3,2},{4,3},{5,4},{6,5},{7,6},{0,7},{9,8},{10,9},{11,1... | collective-permute-start | bytes 491528 | tf_op jit(solution)/shard_map/ppermute | solution.py:699
  74.3 0.7 copy-start.5
  78.8 3.0 %collective-permute-start.5 = (f32[16,2,16,128]{3,2,1,0:T(8,128)S(1)}, f32[16,2,16,128]{3,2,1,0:T(8,128)S(1)}, u32[]{:S(2)}, u32[]{:S(2)}) collective-permute-start(f32[16,2,16,128]{3,2,1,0:T(8,128)S(1)} %get-tuple-element.82), channel_id=1, source_target_pairs={{0,8},{8,0},{1,9},{9,1},{2,10},{10,2},{3,11},{11,3},{4,12},{12,4},... | collective-permute-start | bytes 786440 | tf_op jit(solution)/shard_map/ppermute | solution.py:802
  111.0 6.4 %collective-permute-start.6 = (f32[16,2,16,128]{3,2,1,0:T(8,128)S(1)}, f32[16,2,16,128]{3,2,1,0:T(8,128)S(1)}, u32[]{:S(2)}, u32[]{:S(2)}) collective-permute-start(f32[16,2,16,128]{3,2,1,0:T(8,128)S(1)} %all_to_all.22.mine), channel_id=1, source_target_pairs={{0,8},{8,0},{1,9},{9,1},{2,10},{10,2},{3,11},{11,3},{4,12},{12,4},... | collective-permute-start | bytes 786440 | tf_op jit(solution)/shard_map/ppermute | solution.py:806
  114.2 17.0 %collective-permute-start.10 = (f32[64,4,128]{2,1,0:T(4,128)S(1)}, f32[64,4,128]{2,1,0:T(4,128)S(1)}, u32[]{:S(2)}, u32[]{:S(2)}) collective-permute-start(f32[64,4,128]{2,1,0:T(4,128)S(1)} %get-tuple-element.97), channel_id=1, source_target_pairs={{1,0},{2,1},{3,2},{4,3},{5,4},{6,5},{7,6},{0,7},{9,8},{10,9},{11,1... | collective-permute-start | bytes 393224 | tf_op jit(solution)/shard_map/ppermute | solution.py:699
  117.5 13.7 %collective-permute-start.9 = (f32[64,4,128]{2,1,0:T(4,128)S(1)}, f32[64,4,128]{2,1,0:T(4,128)S(1)}, u32[]{:S(2)}, u32[]{:S(2)}) collective-permute-start(f32[64,4,128]{2,1,0:T(4,128)S(1)} %get-tuple-element.96), channel_id=1, source_target_pairs={{0,1},{1,2},{2,3},{3,4},{4,5},{5,6},{6,7},{7,0},{8,9},{9,10},{10,1... | collective-permute-start | bytes 393224 | tf_op jit(solution)/shard_map/ppermute | solution.py:699
  117.6 8.2 %collective-permute-start.7 = (f32[32,4,128]{2,1,0:T(4,128)S(1)}, f32[32,4,128]{2,1,0:T(4,128)S(1)}, u32[]{:S(2)}, u32[]{:S(2)}) collective-permute-start(f32[32,4,128]{2,1,0:T(4,128)S(1)} %get-tuple-element.90), channel_id=1, source_target_pairs={{0,1},{1,2},{2,3},{3,4},{4,5},{5,6},{6,7},{7,0},{8,9},{9,10},{10,1... | collective-permute-start | bytes 196616 | tf_op jit(solution)/shard_map/ppermute | solution.py:699
  117.7 8.1 %collective-permute-start.8 = (f32[32,4,128]{2,1,0:T(4,128)S(1)}, f32[32,4,128]{2,1,0:T(4,128)S(1)}, u32[]{:S(2)}, u32[]{:S(2)}) collective-permute-start(f32[32,4,128]{2,1,0:T(4,128)S(1)} %get-tuple-element.91), channel_id=1, source_target_pairs={{1,0},{2,1},{3,2},{4,3},{5,4},{6,5},{7,6},{0,7},{9,8},{10,9},{11,1... | collective-permute-start | bytes 196616 | tf_op jit(solution)/shard_map/ppermute | solution.py:699
  127.0 0.8 copy-start.2
  127.8 8.2 %all-to-all-start.3 = ((f32[8,1,128]{2,1,0:T(1,128)}), f32[8,1,128]{2,1,0:T(1,128)S(1)}, u32[]{:S(2)}, u32[]{:S(2)}) async-start(f32[8,1,128]{2,1,0:T(1,128)} %get-tuple-element.92), calls=%async_computation.3 | async-start | bytes 8192 | tf_op jit(solution)/shard_map/all_to_all | solution.py:848
  132.8 3.2 %copy-start.3 = (f32[64,16,128]{2,1,0:T(8,128)S(1)}, f32[64,16,128]{2,1,0:T(8,128)}, u32[]{:S(2)}) copy-start(f32[64,16,128]{2,1,0:T(8,128)} %copy-done.2) | copy-start | bytes 1572868
